TPU v7x, 256 devices: a whole 4x4x8 slice. The times are simulated.
256 devices in a mesh: seq: 32 (over z, x), head: 8 (over y, core).
Axes of the slice: x: 4, y: 4, z: 8, core: 2. Of those that a mesh axis runs over, the one named last changes fastest.
Arguments:
- query: bfloat16 [8, 16384, 128], P('head', 'seq'), may hold values from -8 to 8
- key: bfloat16 [8, 16384, 128], P('head', 'seq'), may hold values from -8 to 8
- value: bfloat16 [8, 16384, 128], P('head', 'seq'), may hold values from -16 to 16
- lin_query: bfloat16 [8, 16384, 128], P('head', 'seq'), may hold values from -52 to 52
- lin_key: bfloat16 [8, 16384, 128], P('head', 'seq'), may hold values from -5 to 5
- gain: float32 [8, 128], P('head'), may hold values from 0.25 to 1.75
- cotangent: bfloat16 [8, 16384, 128], P('head', 'seq'), may hold values from -16 to 16
- key_block: int32 [128, 20], replicated, may hold values from -1 to 127, as said below
Outputs:
- mixed: bfloat16 [8, 16384, 128], P('head', 'seq')
- grad_query: bfloat16 [8, 16384, 128], P('head', 'seq')
- grad_key: bfloat16 [8, 16384, 128], P('head', 'seq')
- grad_value: bfloat16 [8, 16384, 128], P('head', 'seq')
- grad_lin_query: bfloat16 [8, 16384, 128], P('head', 'seq')
- grad_lin_key: bfloat16 [8, 16384, 128], P('head', 'seq')
- grad_gain: float32 [8, 128], P('head')
Inputs may be any that keep to these rules, and one draw needn't show every extreme that they name: `key_block`: row b lists the key blocks that query block b reads: slot 0 is b, slot 1 is b - 1 (-1 when b is 0); each later slot names a block that lies on an earlier index of seq than b and before b - 1, or is -1, and all -1 slots follow the named ones. A row names no block twice. Over all rows' slots from 2 on, at most one block of the blocks on one index of seq is named.
All inputs are finite; a program needn't handle non-finite values.
Results may differ from a plain program's by a relative error of at most 0.039.
Values may be sent and summed in bfloat16 or wider, within the bound.
No kernel may reach another device: no remote copies, remote signals or barrier semaphores. Data moves between devices by JAX's collectives and lax.ppermute only.
A program may use at most 64 MiB of HBM per device.

v0:
```python
import functools

import jax
import jax.numpy as jnp
from jax import lax
from jax.experimental import pallas as pl
from jax.experimental.pallas import tpu as pltpu
from jax.sharding import Mesh, PartitionSpec as P


BLK = 128
NZ, NX, NY, NC = 8, 4, 4, 2
masked_value = -1e30
eps_norm = 1e-05
f32 = jnp.float32
bf16 = jnp.bfloat16
NT = (((1,), (1,)), ((), ()))
TN = (((0,), (0,)), ((), ()))
VM = pl.BlockSpec(memory_space=pltpu.VMEM)
SM = pl.BlockSpec(memory_space=pltpu.SMEM)
AN = pl.BlockSpec(memory_space=pl.ANY)
HB = pl.BlockSpec(memory_space=pltpu.HBM)
FAR = NZ * NX
OWN = FAR
PREV = FAR + 4
HALF = 64
TOP = 192
SENT = 144
POOL = FAR + 5


def mm(a, b, dims=None):
    if dims is None:
        return jnp.dot(a, b, preferred_element_type=f32)
    return lax.dot_general(a, b, dims, preferred_element_type=f32)


def call(body, outs, ins, specs, scratch=(), out_specs=None):
    return pl.pallas_call(
        body,
        out_shape=[jax.ShapeDtypeStruct(s, d) for s, d in outs],
        in_specs=list(specs),
        out_specs=out_specs or [VM] * len(outs),
        scratch_shapes=list(scratch),
        compiler_params=pltpu.CompilerParams(vmem_limit_bytes=40 << 20),
    )(*ins)


def rows(b):
    return pl.ds(b * BLK, BLK)


def as_row(col):
    return jnp.broadcast_to(col, (BLK, BLK)).T[0:1]


def as_cols(row):
    return jnp.broadcast_to(row, (BLK, BLK)).T


def lower_mask():
    return lax.broadcasted_iota(jnp.int32, (BLK, BLK), 0) >= lax.broadcasted_iota(
        jnp.int32, (BLK, BLK), 1
    )


def chosen_block(pos, names):
    base = pos[0] * 16 + pos[1] * 4
    far = names[...]
    col = lax.broadcasted_iota(jnp.int32, far.shape, 1)
    hit = (col >= 2) & (far >= base) & (far < base + 4)
    return jnp.max(jnp.where(hit, far - base, 0).astype(f32)).astype(jnp.int32)


def pick_kernel(pos, names, k, v, top, low, last, sems):
    mine = chosen_block(pos, names)
    pairs = [
        (v.at[mine, pl.ds(HALF, HALF)], low),
        (k.at[3], last.at[pl.ds(0, BLK)]),
        (v.at[3], last.at[pl.ds(BLK, BLK)]),
    ]
    for i in range(NZ):
        pairs.append((k.at[mine], top.at[i, pl.ds(0, BLK)]))
        pairs.append((v.at[mine, pl.ds(0, HALF)], top.at[i, pl.ds(BLK, HALF)]))
    copies = [pltpu.make_async_copy(a, b, sems.at[i]) for i, (a, b) in enumerate(pairs)]
    for c in copies:
        c.start()
    for c in copies:
        c.wait()


def place_of(pos, names, b, j):
    name = names[b, j]
    base = pos[0] * 16 + pos[1] * 4
    live = name >= 0
    if j == 0:
        return OWN + b, live
    if j == 1:
        place = jnp.where(name >= base, OWN + name - base, PREV)
        return jnp.where(live, place, OWN), live
    back_x = jnp.bitwise_and(pos[1] - jnp.bitwise_and(jnp.right_shift(name, 2), 3), NX - 1)
    return jnp.where(live, back_x * NZ + jnp.right_shift(name, 4), OWN), live


def pool_copies(far, low, k, v, prev, pool, sems):
    pairs = [(f, pool.at[pl.ds(NZ * j, NZ), pl.ds(0, TOP)]) for j, f in enumerate(far)]
    pairs += [
        (low.at[:, j], pool.at[pl.ds(NZ * j, NZ), pl.ds(TOP, HALF)]) for j in range(NX)
    ]
    pairs += [
        (k, pool.at[pl.ds(OWN, 4), pl.ds(0, BLK)]),
        (v, pool.at[pl.ds(OWN, 4), pl.ds(BLK, BLK)]),
        (prev, pool.at[PREV]),
    ]
    copies = [pltpu.make_async_copy(a, b, sems.at[i]) for i, (a, b) in enumerate(pairs)]
    for c in copies:
        c.start()
    for c in copies:
        c.wait()


GROUP = 4


def attend_kernel(pos, names, q, lk, f0, f1, f2, f3, low, k, v, prev, att, lse, state, pool, s_scr, sems):
    pool_copies((f0, f1, f2, f3), low, k, v, prev, pool, sems)
    nsel = names.shape[1]
    scale = BLK ** (-0.5)

    def block(b, carry):
        qb = q[rows(b), :]
        top = None
        for g in range(0, nsel, GROUP):
            spots = [place_of(pos, names, b, j) for j in range(g, g + GROUP)]
            keys = jnp.concatenate([pool[p, 0:BLK, :] for p, _ in spots], axis=0)
            s = mm(qb, keys, NT)
            for i, (_, live) in enumerate(spots):
                j = g + i
                piece = s[:, i * BLK : (i + 1) * BLK] * scale + jnp.where(live, 0.0, masked_value)
                if j == 0:
                    piece = jnp.where(lower_mask(), piece, masked_value)
                s_scr[:, j * BLK : (j + 1) * BLK] = piece
                top = piece if top is None else jnp.maximum(top, piece)
        row_max = jnp.max(top, axis=1, keepdims=True)
        part = jnp.zeros((BLK, BLK), f32)
        acc = jnp.zeros((BLK, BLK), f32)
        for g in range(0, nsel, GROUP):
            w = jnp.exp(s_scr[:, g * BLK : (g + GROUP) * BLK] - row_max)
            for i in range(GROUP):
                part = part + w[:, i * BLK : (i + 1) * BLK]
            vals = jnp.concatenate(
                [pool[place_of(pos, names, b, j)[0], BLK:, :] for j in range(g, g + GROUP)], axis=0
            )
            acc = acc + mm(w.astype(bf16), vals)
        total = jnp.sum(part, axis=1, keepdims=True)
        att[rows(b), :] = (acc / total).astype(bf16)
        lse[pl.ds(b, 1), :] = as_row(row_max + jnp.log(total))
        return carry

    lax.fori_loop(0, 4, block, 0)
    state[...] = mm(lk[...], att[...], TN).astype(bf16)


def row_kernel(x0, x1, x2, x3, out):
    total = x0[...].astype(f32)
    for r in (x1, x2, x3):
        total = total + r[...].astype(f32)
    total = total.astype(bf16)
    for i in range(NZ):
        out[i] = total


def linear_kernel(pos, lq, lk, att, gain, cot, x0, x1, x2, x3, zs, lin, prior, sums):
    lower = lower_mask()
    run = jnp.zeros((BLK, BLK), f32)
    for j, r in enumerate((x1, x2, x3)):
        run = run + jnp.where(pos[1] > j, r[...].astype(f32), 0.0)
    for i in range(NZ - 1):
        run = run + jnp.where(pos[0] > i, zs[i].astype(f32), 0.0)
    sums[...] = jnp.zeros((8, BLK), f32)
    for b in range(4):
        r = slice(b * BLK, (b + 1) * BLK)
        before = run.astype(bf16)
        prior[b] = before
        mixing = jnp.where(lower, mm(lq[r], lk[r], NT), 0.0).astype(bf16)
        out = mm(mixing, att[r]) + mm(lq[r], before)
        lin[r] = out
        if b < 3:
            run = run + mm(lk[r], att[r], TN)
        scaled = cot[r].astype(f32) * gain[...]
        sums[b : b + 1] = as_row(jnp.sum(out * out, axis=1, keepdims=True))
        sums[4 + b : 5 + b] = as_row(jnp.sum(out * scaled, axis=1, keepdims=True))


def norm_terms(sums, features):
    inv = lax.rsqrt(sums[0:4] / features + eps_norm)
    return inv, inv * inv * inv * sums[4:8] / features


def split_row(row):
    high = row.astype(bf16)
    return high, (row - high.astype(f32)).astype(bf16)


def norm_kernel(features, lq, lin, gain, cot, s0, s1, s2, s3, glin, inv_out, send, local):
    inv, pull = norm_terms(s0[...] + s1[...] + s2[...] + s3[...], features)
    inv_out[0:4] = inv
    inv_out[4:8] = inv
    ggain = jnp.zeros((1, BLK), f32)
    for b in range(4):
        r = slice(b * BLK, (b + 1) * BLK)
        c = cot[r].astype(f32)
        out = lin[r]
        invc = as_cols(inv[b : b + 1])
        ggain = ggain + jnp.sum(c * (out * invc), axis=0, keepdims=True)
        glin[r] = (invc * (c * gain[...]) - out * as_cols(pull[b : b + 1])).astype(bf16)
    run = jnp.zeros((BLK, BLK), f32)
    for b in range(3, -1, -1):
        r = slice(b * BLK, (b + 1) * BLK)
        local[b] = run
        run = run + mm(lq[r], glin[r], TN)
    send[0:BLK] = run.astype(bf16)
    high, rest = split_row(ggain)
    send[BLK : BLK + 8] = jnp.broadcast_to(high, (8, BLK))
    send[BLK + 8 :] = jnp.broadcast_to(rest, (8, BLK))


def sent_kernel(x0, x1, x2, x3, out):
    total = x0[...].astype(f32)
    for r in (x1, x2, x3):
        total = total + r[...].astype(f32)
    high, rest = split_row(total[BLK : BLK + 8] + total[BLK + 8 :])
    state = total[0:BLK].astype(bf16)
    for i in range(NZ):
        out[i, 0:BLK] = state
        out[i, BLK : BLK + 8] = high
        out[i, BLK + 8 :] = rest


def side_kernel(inv, lin, gain, att, glin, lk, lq, prior, mixed, dlq, pairs_t, mix_t):
    lower = lower_mask()
    upper = lax.broadcasted_iota(jnp.int32, (BLK, BLK), 0) <= lax.broadcasted_iota(
        jnp.int32, (BLK, BLK), 1
    )
    for b in range(4):
        r = slice(b * BLK, (b + 1) * BLK)
        normed = lin[r] * as_cols(inv[b : b + 1])
        mixed[r] = (att[r].astype(f32) + gain[...] * normed).astype(bf16)
        pairs = jnp.where(lower, mm(glin[r], att[r], NT), 0.0).astype(bf16)
        dlq[r] = (mm(pairs, lk[r]) + mm(glin[r], prior[b], NT)).astype(bf16)
        pairs_t[b] = jnp.where(upper, mm(att[r], glin[r], NT), 0.0).astype(bf16)
        mix_t[b] = jnp.where(upper, mm(lk[r], lq[r], NT), 0.0).astype(bf16)


def backward_kernel(pos, names, q, lse, att, cot, lq, lk, glin, pairs_t, mix_t, local,
                    x0, x1, x2, x3, zs, f0, f1, f2, f3, low, k, v, prev,
                    dlk, dq, o0, o1, o2, o3, olow, own, back, ggain, pool, acc, gatt, delta, sems):
    pool_copies((f0, f1, f2, f3), low, k, v, prev, pool, sems)
    nsel = names.shape[1]
    scale = BLK ** (-0.5)
    later = jnp.zeros((BLK, BLK), f32)
    for j, r in enumerate((x1, x2, x3)):
        later = later + jnp.where(pos[1] + j + 1 < NX, r[0:BLK].astype(f32), 0.0)
    gg = jnp.zeros((8, BLK), f32)
    for i in range(NZ):
        later = later + jnp.where(pos[0] < i, zs[i, 0:BLK].astype(f32), 0.0)
        gg = gg + zs[i, BLK : BLK + 8].astype(f32) + zs[i, BLK + 8 :].astype(f32)
    ggain[...] = gg
    for b in range(4):
        r = slice(b * BLK, (b + 1) * BLK)
        after = (later + local[b]).astype(bf16)
        dlk[r] = (mm(pairs_t[b], lq[r]) + mm(att[r], after, NT)).astype(bf16)
        g = cot[r].astype(f32) + mm(mix_t[b], glin[r]) + mm(lk[r], after)
        g = g.astype(bf16)
        gatt[r] = g
        delta[b : b + 1] = as_row(
            jnp.sum(g.astype(f32) * att[r].astype(f32), axis=1, keepdims=True)
        )
    acc[...] = jnp.zeros(acc.shape, f32)

    def block(b, carry):
        qb = q[rows(b), :]
        gb = gatt[rows(b), :]
        lse_b = lse[pl.ds(b, 1), :]
        delta_b = delta[pl.ds(b, 1), :]
        dqb = jnp.zeros((BLK, BLK), f32)
        for g in range(0, nsel, GROUP):
            spots = [place_of(pos, names, b, j) for j in range(g, g + GROUP)]
            keys = jnp.concatenate([pool[p, 0:BLK, :] for p, _ in spots], axis=0)
            vals = jnp.concatenate([pool[p, BLK:, :] for p, _ in spots], axis=0)
            s = mm(keys, qb, NT)
            dp = mm(vals, gb, NT)
            pieces = []
            for i, (_, live) in enumerate(spots):
                r = slice(i * BLK, (i + 1) * BLK)
                piece = s[r] * scale + jnp.where(live, 0.0, masked_value)
                if g + i == 0:
                    keep = lax.broadcasted_iota(jnp.int32, (BLK, BLK), 0) <= lax.broadcasted_iota(
                        jnp.int32, (BLK, BLK), 1
                    )
                    piece = jnp.where(keep, piece, masked_value)
                pieces.append(jnp.exp(piece - lse_b))
            p = jnp.concatenate(pieces, axis=0)
            ds = (p * (dp - delta_b)).astype(bf16)
            dv = mm(p.astype(bf16), gb)
            dk = mm(ds, qb)
            dqb = dqb + mm(ds, keys, TN)
            for i, (spot, _) in enumerate(spots):
                r = slice(i * BLK, (i + 1) * BLK)
                acc[spot, 0:BLK, :] += dk[r]
                acc[spot, BLK:, :] += dv[r]
        dq[rows(b), :] = (dqb * scale).astype(bf16)
        return carry

    lax.fori_loop(0, 4, block, 0)
    for j, o in enumerate((o0, o1, o2, o3)):
        o[:, 0:BLK, :] = (acc[NZ * j : NZ * (j + 1), 0:BLK, :] * scale).astype(bf16)
        o[:, BLK:, :] = acc[NZ * j : NZ * (j + 1), BLK:TOP, :].astype(bf16)
        olow[:, j] = acc[NZ * j : NZ * (j + 1), TOP:, :].astype(bf16)
    own[:, 0:BLK, :] = acc[OWN : OWN + 4, 0:BLK, :] * scale
    own[:, BLK:, :] = acc[OWN : OWN + 4, BLK:, :]
    back[0:BLK] = (acc[PREV, 0:BLK, :] * scale).astype(bf16)
    back[BLK:] = acc[PREV, BLK:, :].astype(bf16)


def fold_kernel(a0, a1, a2, a3, low, top, l0, l1, l2, l3):
    total = a0[...].astype(f32) + a1[...].astype(f32) + a2[...].astype(f32) + a3[...].astype(f32)
    top[...] = total.astype(bf16)
    for j, o in enumerate((l0, l1, l2, l3)):
        part = low[0, j].astype(f32)
        for i in range(1, NZ):
            part = part + low[i, j].astype(f32)
        o[...] = part.astype(bf16)


def finish_kernel(pos, names, own, back, top, l0, l1, l2, l3, gk, gv):
    mine = chosen_block(pos, names)
    total = top[0].astype(f32)
    for i in range(1, NZ):
        total = total + top[i].astype(f32)
    part = l0[...].astype(f32) + l1[...].astype(f32) + l2[...].astype(f32) + l3[...].astype(f32)
    gathered = jnp.concatenate([total, part], axis=0)
    for b in range(4):
        whole = own[b] + jnp.where(mine == b, gathered, 0.0)
        if b == 3:
            whole = whole + back[...].astype(f32)
        gk[b * BLK : (b + 1) * BLK] = whole[0:BLK].astype(bf16)
        gv[b * BLK : (b + 1) * BLK] = whole[BLK:].astype(bf16)


def turn(value, axis, size, by):
    return lax.ppermute(value, axis, [(i, (i + by) % size) for i in range(size)])


def swap(value):
    return lax.all_to_all(value, "z", 0, 0, tiled=True)


def turns(values, sign):
    out = []
    for j, value in enumerate(values):
        out.append(turn(value, "x", NX, sign * (j + 1)))
    return out


def per_device(query, key, value, lin_query, lin_key, gain, cotangent, key_block):
    q, k, v, lq, lk, cot = (a[0] for a in (query, key, value, lin_query, lin_key, cotangent))
    width = q.shape[1]
    seq = ("z", "x")
    zi = lax.axis_index("z")
    xi = lax.axis_index("x")
    pos = jnp.stack([zi, xi]).astype(jnp.int32)
    features = float(NY * NC * width)
    names = lax.dynamic_slice_in_dim(key_block, (zi * NX + xi) * 4, 4, 0)
    k4 = k.reshape(4, BLK, width)
    v4 = v.reshape(4, BLK, width)
    tile = (BLK, BLK)

    tops, low, last = call(
        pick_kernel,
        [((NZ, TOP, width), bf16), ((HALF, width), bf16), ((2 * BLK, width), bf16)],
        (pos, key_block, k4, v4),
        [SM, VM, HB, HB],
        [pltpu.SemaphoreType.DMA((2 * NZ + 3,))],
        [HB, VM, VM],
    )
    prev = lax.ppermute(last, seq, [(i, i + 1) for i in range(NZ * NX - 1)])
    lows = jnp.stack([low] + [turn(low, "x", NX, j) for j in range(1, NX)])
    tops = swap(tops)
    lows = jnp.broadcast_to(lows[None], (NZ, NX, HALF, width))
    tops, lows, prev = lax.optimization_barrier((tops, lows, prev))
    far = [tops] + turns([tops] * 3, 1)
    lows = swap(lows)

    pool_scratch = [pltpu.VMEM((POOL, 2 * BLK, width), bf16)]
    sems = [pltpu.SemaphoreType.DMA((2 * NX + 3,))]
    att, lse, state = call(
        attend_kernel,
        [((512, width), bf16), ((8, BLK), f32), (tile, bf16)],
        (pos, names, q, lk, *far, lows, k4, v4, prev),
        [SM, SM, VM, VM] + [AN] * 8,
        pool_scratch + [pltpu.VMEM((BLK, names.shape[1] * BLK), f32)] + sems,
    )

    xs = [state] + [turn(state, "x", NX, j) for j in range(1, NX)]
    (wide,) = call(row_kernel, [((NZ, BLK, width), bf16)], xs, [VM] * 4)
    lin, prior, sums = call(
        linear_kernel,
        [((512, width), f32), ((4, BLK, width), bf16), ((8, BLK), f32)],
        (pos, lq, lk, att, gain, cot, *xs, swap(wide)),
        [SM] + [VM] * 10,
    )
    sums = sums + turn(sums, "c", NC, 1)
    ys = [sums] + [turn(sums, "y", NY, i) for i in range(1, NY)]
    glin, inv, send, local = call(
        functools.partial(norm_kernel, features),
        [((512, width), bf16), ((8, BLK), f32), ((SENT, BLK), bf16), ((4, BLK, BLK), f32)],
        (lq, lin, gain, cot, *ys),
        [VM] * 8,
    )
    ex = [send] + [turn(send, "x", NX, -j) for j in range(1, NX)]
    mixed, dlq, pairs_t, mix_t = call(
        side_kernel,
        [((512, width), bf16), ((512, width), bf16), ((4, BLK, BLK), bf16), ((4, BLK, BLK), bf16)],
        (inv, lin, gain, att, glin, lk, lq, prior),
        [VM] * 8,
    )
    *ex, mixed, dlq, pairs_t, mix_t = lax.optimization_barrier((*ex, mixed, dlq, pairs_t, mix_t))
    (wide,) = call(sent_kernel, [((NZ, SENT, width), bf16)], ex, [VM] * 4)
    outs = call(
        backward_kernel,
        [((512, width), bf16), ((512, width), bf16)]
        + [((NZ, TOP, width), bf16)] * 4
        + [((NZ, NX, HALF, width), bf16), ((4, 2 * BLK, width), f32)]
        + [((2 * BLK, width), bf16), ((8, BLK), f32)],
        (pos, names, q, lse, att, cot, lq, lk, glin, pairs_t, mix_t, local, *ex, swap(wide))
        + (*far, lows, k4, v4, prev),
        [SM, SM] + [VM] * 15 + [AN] * 8,
        pool_scratch
        + [pltpu.VMEM((POOL, 2 * BLK, width), f32), pltpu.VMEM((512, width), bf16), pltpu.VMEM((8, BLK), f32)]
        + sems,
    )
    dlk, dq = outs[0], outs[1]
    far_out, low_out, own, back, gg = outs[2:6], outs[6], outs[7], outs[8], outs[9]
    back = lax.ppermute(back, seq, [(i + 1, i) for i in range(NZ * NX - 1)])
    got = [far_out[0]] + turns(far_out[1:], -1)
    folded = call(
        fold_kernel,
        [((NZ, TOP, width), bf16)] + [((HALF, width), bf16)] * NX,
        (*got, swap(low_out)),
        [VM] * 5,
    )
    ends = [folded[1]] + turns(folded[2:], -1)
    gk, gv = call(
        finish_kernel,
        [((512, width), bf16), ((512, width), bf16)],
        (pos, key_block, own, back, swap(folded[0]), *ends),
        [SM] + [VM] * 8,
    )
    lead = lambda a: a[None]
    return (lead(mixed), lead(dq), lead(gk), lead(gv), lead(dlq), lead(dlk), gg[0:1])


def solution(mesh):
    grid = Mesh(mesh.devices.reshape(NZ, NX, NY, NC), ("z", "x", "y", "c"))
    cut = P(("y", "c"), ("z", "x"), None)
    flat = P(("y", "c"), None)
    return jax.shard_map(
        per_device,
        mesh=grid,
        in_specs=(cut, cut, cut, cut, cut, flat, cut, P()),
        out_specs=(cut, cut, cut, cut, cut, cut, flat),
        check_vma=False,
    )
```

profile of v0, /device:TPU:8, one launch (start us, length us, event | category | flops | bytes accessed | tf_op | source)
XLA Modules:
  0.0 173.3 jit_solution(1835284335889197291)
XLA Ops:
  0.6 0.7 copy-done.16
  1.5 0.9 copy-done.2
  2.4 0.9 copy-done.4
  3.3 1.7 shard_map.135
  5.1 8.5 %all-to-all-start = ((bf16[8,192,128]{2,1,0:T(8,128)(2,1)}), bf16[8,192,128]{2,1,0:T(8,128)(2,1)S(1)}, u32[]{:S(2)}, u32[]{:S(2)}) async-start(bf16[8,192,128]{2,1,0:T(8,128)(2,1)} %get-tuple-element.52), calls=%async_computation | async-start | bytes 786432 | tf_op jit(solution)/shard_map/all_to_all | solution.py:356
  13.5 2.8 %collective-permute-start.2 = (bf16[64,128]{1,0:T(8,128)(2,1)S(1)}, bf16[64,128]{1,0:T(8,128)(2,1)S(1)}, u32[]{:S(2)}, u32[]{:S(2)}) collective-permute-start(bf16[64,128]{1,0:T(8,128)(2,1)S(1)} %get-tuple-element.53), channel_id=1, source_target_pairs={{0,24},{8,0},{16,8},{24,16},{1,25},{9,1},{17,9},{25,17},{2,26},{10... | collective-permute-start | bytes 49160 | tf_op jit(solution)/shard_map/ppermute | solution.py:352
  16.3 0.8 collective-permute-start.1
  17.1 0.9 collective-permute-start
  18.0 3.7 %collective-permute-start.3 = (bf16[256,128]{1,0:T(8,128)(2,1)S(1)}, bf16[256,128]{1,0:T(8,128)(2,1)S(1)}, u32[]{:S(2)}, u32[]{:S(2)}) collective-permute-start(bf16[256,128]{1,0:T(8,128)(2,1)S(1)} %get-tuple-element.54), channel_id=1, source_target_pairs={{0,8},{8,16},{16,24},{24,32},{32,40},{40,48},{48,56},{56,64},{64,7... | collective-permute-start | bytes 196616 | tf_op jit(solution)/shard_map/ppermute | solution.py:387
  21.7 0.3 collective-permute-done
  22.1 1.5 collective-permute-done.3.prev
  23.6 4.6 %all-to-all-done.f0 = bf16[8,192,128]{2,1,0:T(8,128)(2,1)S(1)} async-done(((bf16[8,192,128]{2,1,0:T(8,128)(2,1)}), bf16[8,192,128]{2,1,0:T(8,128)(2,1)S(1)}, u32[]{:S(2)}, u32[]{:S(2)}) %all-to-all-start) | async-done | bytes 393248 | tf_op jit(solution)/shard_map/all_to_all | solution.py:356
  28.2 0.9 broadcast_in_dim.24
  29.2 6.6 %all-to-all-start.1 = ((bf16[8,4,64,128]{3,2,1,0:T(8,128)(2,1)}), bf16[8,4,64,128]{3,2,1,0:T(8,128)(2,1)S(1)}, u32[]{:S(2)}, u32[]{:S(2)}) async-start(bf16[8,4,64,128]{3,2,1,0:T(8,128)(2,1)} %broadcast_in_dim.24), calls=%async_computation.1 | async-start | bytes 1048576 | tf_op jit(solution)/shard_map/all_to_all | solution.py:356
  36.0 0.4 collective-permute-start.5
  36.5 1.3 collective-permute-start.4
  37.8 10.0 %collective-permute-done.6.f3 = bf16[8,192,128]{2,1,0:T(8,128)(2,1)S(1)} collective-permute-done((bf16[8,192,128]{2,1,0:T(8,128)(2,1)S(1)}, bf16[8,192,128]{2,1,0:T(8,128)(2,1)S(1)}, u32[]{:S(2)}, u32[]{:S(2)}) %collective-permute-start.6) | collective-permute-done | bytes 393248 | tf_op jit(solution)/shard_map/ppermute | solution.py:352
  47.7 1.8 %collective-permute-done.5.f2 = bf16[8,192,128]{2,1,0:T(8,128)(2,1)S(1)} collective-permute-done((bf16[8,192,128]{2,1,0:T(8,128)(2,1)S(1)}, bf16[8,192,128]{2,1,0:T(8,128)(2,1)S(1)}, u32[]{:S(2)}, u32[]{:S(2)}) %collective-permute-start.5) | collective-permute-done | bytes 393248 | tf_op jit(solution)/shard_map/ppermute | solution.py:352
  49.5 6.0 %collective-permute-done.4.f1 = bf16[8,192,128]{2,1,0:T(8,128)(2,1)S(1)} collective-permute-done((bf16[8,192,128]{2,1,0:T(8,128)(2,1)S(1)}, bf16[8,192,128]{2,1,0:T(8,128)(2,1)S(1)}, u32[]{:S(2)}, u32[]{:S(2)}) %collective-permute-start.4) | collective-permute-done | bytes 393248 | tf_op jit(solution)/shard_map/ppermute | solution.py:352
  55.5 4.7 %shard_map.136 = (bf16[512,128]{1,0:T(8,128)(2,1)S(1)}, f32[8,128]{1,0:T(8,128)S(1)}, bf16[128,128]{1,0:T(8,128)(2,1)S(1)}) custom-call(s32[2]{0:T(128)S(1)} %pad_add_fusion.pos, s32[4,20]{1,0:T(4,128)S(1)} %constant_dynamic-slice_fusion.names, bf16[512,128]{1,0:T(8,128)(2,1)S(1)} %bitcast.35, bf16[512,128]{1,0:T(8,128)(2,1)S(1)} %bitcast.22, ...), custom_call_target="tpu_custom_call" | custom-call | tf_op jit(solution)/shard_map/pallas_call | solution.py:39
  60.1 1.0 collective-permute-start.9
  61.1 0.5 collective-permute-start.8
  61.6 0.8 collective-permute-start.7
  62.5 1.7 collective-permute-done.9.x3
  64.1 2.5 %collective-permute-done.8.x2 = bf16[128,128]{1,0:T(8,128)(2,1)S(1)} collective-permute-done((bf16[128,128]{1,0:T(8,128)(2,1)S(1)}, bf16[128,128]{1,0:T(8,128)(2,1)S(1)}, u32[]{:S(2)}, u32[]{:S(2)}) %collective-permute-start.8) | collective-permute-done | bytes 32800 | tf_op jit(solution)/shard_map/ppermute | solution.py:352
  67.0 17.4 %all_to_all.30.zs = bf16[8,128,128]{2,1,0:T(8,128)(2,1)S(1)} all-to-all(bf16[8,128,128]{2,1,0:T(8,128)(2,1)S(1)} %shard_map.137), channel_id=1, replica_groups=mesh['z'=8,'x'=4,'y'=4,'c'=2] {'z'}, dimensions={0} | all-to-all | bytes 524288 | tf_op jit(solution)/shard_map/all_to_all | solution.py:356
  84.3 0.6 copy-done.11
  85.0 1.4 shard_map.138
  86.5 1.2 collective-permute-done.10
  87.7 0.4 collective-permute-start.13
  88.1 2.6 %collective-permute-start.12 = (f32[8,128]{1,0:T(8,128)S(1)}, f32[8,128]{1,0:T(8,128)S(1)}, u32[]{:S(2)}, u32[]{:S(2)}) collective-permute-start(f32[8,128]{1,0:T(8,128)S(1)} %add.11.s0), channel_id=1, source_target_pairs={{0,4},{2,6},{4,0},{6,2},{1,5},{3,7},{5,1},{7,3},{8,12},{10,14},{12... | collective-permute-start | bytes 12296 | tf_op jit(solution)/shard_map/ppermute | solution.py:352
  90.7 1.9 %collective-permute-start.11 = (f32[8,128]{1,0:T(8,128)S(1)}, f32[8,128]{1,0:T(8,128)S(1)}, u32[]{:S(2)}, u32[]{:S(2)}) collective-permute-start(f32[8,128]{1,0:T(8,128)S(1)} %add.11.s0), channel_id=1, source_target_pairs={{0,2},{2,4},{4,6},{6,0},{1,3},{3,5},{5,7},{7,1},{8,10},{10,12},{12... | collective-permute-start | bytes 12296 | tf_op jit(solution)/shard_map/ppermute | solution.py:352
  92.6 0.6 collective-permute-done.12.s2
  93.2 1.1 collective-permute-done.11.s1
  94.3 0.4 shard_map.139
  94.7 1.0 collective-permute-start.16
  95.7 2.6 %collective-permute-start.15 = (bf16[144,128]{1,0:T(8,128)(2,1)S(1)}, bf16[144,128]{1,0:T(8,128)(2,1)S(1)}, u32[]{:S(2)}, u32[]{:S(2)}) collective-permute-start(bf16[144,128]{1,0:T(8,128)(2,1)S(1)} %get-tuple-element.75.x0), channel_id=1, source_target_pairs={{0,16},{8,24},{16,0},{24,8},{1,17},{9,25},{17,1},{25,9},{2,18},{10... | collective-permute-start | bytes 110600 | tf_op jit(solution)/shard_map/ppermute | solution.py:352
  98.3 0.9 collective-permute-start.14
  99.2 1.3 shard_map.140
  100.6 0.6 collective-permute-done.15.x2
  101.2 1.1 collective-permute-done.14.x1
  102.3 13.2 %all_to_all.31.zs = bf16[8,144,128]{2,1,0:T(8,128)(2,1)S(1)} all-to-all(bf16[8,144,128]{2,1,0:T(8,128)(2,1)S(1)} %shard_map.141), channel_id=1, replica_groups=mesh['z'=8,'x'=4,'y'=4,'c'=2] {'z'}, dimensions={0} | all-to-all | bytes 589824 | tf_op jit(solution)/shard_map/all_to_all | solution.py:356
  115.5 8.9 %shard_map.142 = (bf16[512,128]{1,0:T(8,128)(2,1)}, bf16[512,128]{1,0:T(8,128)(2,1)}, bf16[8,192,128]{2,1,0:T(8,128)(2,1)S(1)}, bf16[8,192,128]{2,1,0:T(8,128)(2...) custom-call(s32[2]{0:T(128)S(1)} %pad_add_fusion.pos, ...), custom_call_target="tpu_custom_call" | custom-call | tf_op jit(solution)/shard_map/pallas_call | solution.py:39
  124.4 0.8 copy-done.8
  125.2 0.8 copy-done.9
  126.0 0.8 copy-done.12
  126.7 0.7 copy-done.14
  127.5 0.7 copy-done.15
  128.2 3.6 %all-to-all-start.4 = ((bf16[8,4,64,128]{3,2,1,0:T(8,128)(2,1)}), bf16[8,4,64,128]{3,2,1,0:T(8,128)(2,1)S(1)}, u32[]{:S(2)}, u32[]{:S(2)}) async-start(bf16[8,4,64,128]{3,2,1,0:T(8,128)(2,1)} %copy-done.8), calls=%async_computation.4 | async-start | bytes 1048576 | tf_op jit(solution)/shard_map/all_to_all | solution.py:356
  131.9 2.2 %collective-permute-start.18 = (bf16[8,192,128]{2,1,0:T(8,128)(2,1)}, bf16[8,192,128]{2,1,0:T(8,128)(2,1)S(1)}, u32[]{:S(2)}, u32[]{:S(2)}) collective-permute-start(bf16[8,192,128]{2,1,0:T(8,128)(2,1)} %copy-done.15), channel_id=1, source_target_pairs={{0,24},{8,0},{16,8},{24,16},{1,25},{9,1},{17,9},{25,17},{2,26},{10... | collective-permute-start | bytes 1179656 | tf_op jit(solution)/shard_map/ppermute | solution.py:352
  134.1 0.7 collective-permute-start.19
  134.7 0.3 collective-permute-start.20
  135.0 12.3 %collective-permute-done.18.a1 = bf16[8,192,128]{2,1,0:T(8,128)(2,1)S(1)} collective-permute-done((bf16[8,192,128]{2,1,0:T(8,128)(2,1)}, bf16[8,192,128]{2,1,0:T(8,128)(2,1)S(1)}, u32[]{:S(2)}, u32[]{:S(2)}) %collective-permute-start.18) | collective-permute-done | bytes 393248 | tf_op jit(solution)/shard_map/ppermute | solution.py:352
  147.3 3.5 %collective-permute-done.20.a3 = bf16[8,192,128]{2,1,0:T(8,128)(2,1)S(1)} collective-permute-done((bf16[8,192,128]{2,1,0:T(8,128)(2,1)S(1)}, bf16[8,192,128]{2,1,0:T(8,128)(2,1)S(1)}, u32[]{:S(2)}, u32[]{:S(2)}) %collective-permute-start.20) | collective-permute-done | bytes 393248 | tf_op jit(solution)/shard_map/ppermute | solution.py:352
  150.8 1.0 shard_map.143
  151.7 6.8 %all-to-all-start.5 = ((bf16[8,192,128]{2,1,0:T(8,128)(2,1)}), bf16[8,192,128]{2,1,0:T(8,128)(2,1)S(1)}, u32[]{:S(2)}, u32[]{:S(2)}) async-start(bf16[8,192,128]{2,1,0:T(8,128)(2,1)} %get-tuple-element.87), calls=%async_computation.5 | async-start | bytes 786432 | tf_op jit(solution)/shard_map/all_to_all | solution.py:356
  158.5 1.3 collective-permute-start.17
  159.8 2.0 %collective-permute-start.21 = (bf16[64,128]{1,0:T(8,128)(2,1)S(1)}, bf16[64,128]{1,0:T(8,128)(2,1)S(1)}, u32[]{:S(2)}, u32[]{:S(2)}) collective-permute-start(bf16[64,128]{1,0:T(8,128)(2,1)S(1)} %get-tuple-element.89), channel_id=1, source_target_pairs={{0,24},{8,0},{16,8},{24,16},{1,25},{9,1},{17,9},{25,17},{2,26},{10... | collective-permute-start | bytes 49160 | tf_op jit(solution)/shard_map/ppermute | solution.py:352
  161.8 2.7 %collective-permute-start.22 = (bf16[64,128]{1,0:T(8,128)(2,1)S(1)}, bf16[64,128]{1,0:T(8,128)(2,1)S(1)}, u32[]{:S(2)}, u32[]{:S(2)}) collective-permute-start(bf16[64,128]{1,0:T(8,128)(2,1)S(1)} %get-tuple-element.90), channel_id=1, source_target_pairs={{0,16},{8,24},{16,0},{24,8},{1,17},{9,25},{17,1},{25,9},{2,18},{10... | collective-permute-start | bytes 49160 | tf_op jit(solution)/shard_map/ppermute | solution.py:352
  164.6 0.5 slice.3
  165.1 2.0 %collective-permute-done.22.l2 = bf16[64,128]{1,0:T(8,128)(2,1)S(1)} collective-permute-done((bf16[64,128]{1,0:T(8,128)(2,1)S(1)}, bf16[64,128]{1,0:T(8,128)(2,1)S(1)}, u32[]{:S(2)}, u32[]{:S(2)}) %collective-permute-start.22) | collective-permute-done | bytes 16416 | tf_op jit(solution)/shard_map/ppermute | solution.py:352
  167.1 2.5 %collective-permute-done.23.l3 = bf16[64,128]{1,0:T(8,128)(2,1)S(1)} collective-permute-done((bf16[64,128]{1,0:T(8,128)(2,1)S(1)}, bf16[64,128]{1,0:T(8,128)(2,1)S(1)}, u32[]{:S(2)}, u32[]{:S(2)}) %collective-permute-start.23) | collective-permute-done | bytes 16416 | tf_op jit(solution)/shard_map/ppermute | solution.py:352
  169.5 2.3 %all-to-all-done.5.top = bf16[8,192,128]{2,1,0:T(8,128)(2,1)S(1)} async-done(((bf16[8,192,128]{2,1,0:T(8,128)(2,1)}), bf16[8,192,128]{2,1,0:T(8,128)(2,1)S(1)}, u32[]{:S(2)}, u32[]{:S(2)}) %all-to-all-start.5) | async-done | bytes 393248 | tf_op jit(solution)/shard_map/all_to_all | solution.py:356
  171.9 1.4 shard_map.144
  (45 shorter events, 0.9 us)
Async XLA Ops:
  0.6 0.7 copy-start.16
  1.5 0.9 copy-start.2
  2.4 0.9 copy-start.4
  5.1 23.2 %all-to-all-start = ((bf16[8,192,128]{2,1,0:T(8,128)(2,1)}), bf16[8,192,128]{2,1,0:T(8,128)(2,1)S(1)}, u32[]{:S(2)}, u32[]{:S(2)}) async-start(bf16[8,192,128]{2,1,0:T(8,128)(2,1)} %get-tuple-element.52), calls=%async_computation | async-start | bytes 786432 | tf_op jit(solution)/shard_map/all_to_all | solution.py:356
  13.5 8.2 %collective-permute-start.2 = (bf16[64,128]{1,0:T(8,128)(2,1)S(1)}, bf16[64,128]{1,0:T(8,128)(2,1)S(1)}, u32[]{:S(2)}, u32[]{:S(2)}) collective-permute-start(bf16[64,128]{1,0:T(8,128)(2,1)S(1)} %get-tuple-element.53), channel_id=1, source_target_pairs={{0,24},{8,0},{16,8},{24,16},{1,25},{9,1},{17,9},{25,17},{2,26},{10... | collective-permute-start | bytes 49160 | tf_op jit(solution)/shard_map/ppermute | solution.py:352
  16.3 5.4 %collective-permute-start.1 = (bf16[64,128]{1,0:T(8,128)(2,1)S(1)}, bf16[64,128]{1,0:T(8,128)(2,1)S(1)}, u32[]{:S(2)}, u32[]{:S(2)}) collective-permute-start(bf16[64,128]{1,0:T(8,128)(2,1)S(1)} %get-tuple-element.53), channel_id=1, source_target_pairs={{0,16},{8,24},{16,0},{24,8},{1,17},{9,25},{17,1},{25,9},{2,18},{10... | collective-permute-start | bytes 49160 | tf_op jit(solution)/shard_map/ppermute | solution.py:352
  17.1 4.9 %collective-permute-start = (bf16[64,128]{1,0:T(8,128)(2,1)S(1)}, bf16[64,128]{1,0:T(8,128)(2,1)S(1)}, u32[]{:S(2)}, u32[]{:S(2)}) collective-permute-start(bf16[64,128]{1,0:T(8,128)(2,1)S(1)} %get-tuple-element.53), channel_id=1, source_target_pairs={{0,8},{8,16},{16,24},{24,0},{1,9},{9,17},{17,25},{25,1},{2,10},{10... | collective-permute-start | bytes 49160 | tf_op jit(solution)/shard_map/ppermute | solution.py:352
  18.0 5.6 %collective-permute-start.3 = (bf16[256,128]{1,0:T(8,128)(2,1)S(1)}, bf16[256,128]{1,0:T(8,128)(2,1)S(1)}, u32[]{:S(2)}, u32[]{:S(2)}) collective-permute-start(bf16[256,128]{1,0:T(8,128)(2,1)S(1)} %get-tuple-element.54), channel_id=1, source_target_pairs={{0,8},{8,16},{16,24},{24,32},{32,40},{40,48},{48,56},{56,64},{64,7... | collective-permute-start | bytes 196616 | tf_op jit(solution)/shard_map/ppermute | solution.py:387
  29.2 26.3 %copy-start.1 = (bf16[1,512,128]{2,1,0:T(8,128)(2,1)S(1)}, bf16[1,512,128]{2,1,0:T(8,128)(2,1)}, u32[]{:S(2)}) copy-start(bf16[1,512,128]{2,1,0:T(8,128)(2,1)} %param.12) | copy-start | bytes 393220
  29.2 26.3 %copy-start.3 = (bf16[1,512,128]{2,1,0:T(8,128)(2,1)S(1)}, bf16[1,512,128]{2,1,0:T(8,128)(2,1)}, u32[]{:S(2)}) copy-start(bf16[1,512,128]{2,1,0:T(8,128)(2,1)} %param.9) | copy-start | bytes 393220
  29.2 26.3 %copy-start.5 = (bf16[1,512,128]{2,1,0:T(8,128)(2,1)S(1)}, bf16[1,512,128]{2,1,0:T(8,128)(2,1)}, u32[]{:S(2)}) copy-start(bf16[1,512,128]{2,1,0:T(8,128)(2,1)} %param.10) | copy-start | bytes 393220
  29.2 26.3 %copy-start.7 = (bf16[1,512,128]{2,1,0:T(8,128)(2,1)S(1)}, bf16[1,512,128]{2,1,0:T(8,128)(2,1)}, u32[]{:S(2)}) copy-start(bf16[1,512,128]{2,1,0:T(8,128)(2,1)} %param.8) | copy-start | bytes 393220
  29.2 26.3 %all-to-all-start.1 = ((bf16[8,4,64,128]{3,2,1,0:T(8,128)(2,1)}), bf16[8,4,64,128]{3,2,1,0:T(8,128)(2,1)S(1)}, u32[]{:S(2)}, u32[]{:S(2)}) async-start(bf16[8,4,64,128]{3,2,1,0:T(8,128)(2,1)} %broadcast_in_dim.24), calls=%async_computation.1 | async-start | bytes 1048576 | tf_op jit(solution)/shard_map/all_to_all | solution.py:356
  35.8 12.0 %collective-permute-start.6 = (bf16[8,192,128]{2,1,0:T(8,128)(2,1)S(1)}, bf16[8,192,128]{2,1,0:T(8,128)(2,1)S(1)}, u32[]{:S(2)}, u32[]{:S(2)}) collective-permute-start(bf16[8,192,128]{2,1,0:T(8,128)(2,1)S(1)} %all-to-all-done.f0), channel_id=1, source_target_pairs={{0,24},{8,0},{16,8},{24,16},{1,25},{9,1},{17,9},{25,17},{2,26},{10... | collective-permute-start | bytes 1179656 | tf_op jit(solution)/shard_map/ppermute | solution.py:352
  36.0 13.5 %collective-permute-start.5 = (bf16[8,192,128]{2,1,0:T(8,128)(2,1)S(1)}, bf16[8,192,128]{2,1,0:T(8,128)(2,1)S(1)}, u32[]{:S(2)}, u32[]{:S(2)}) collective-permute-start(bf16[8,192,128]{2,1,0:T(8,128)(2,1)S(1)} %all-to-all-done.f0), channel_id=1, source_target_pairs={{0,16},{8,24},{16,0},{24,8},{1,17},{9,25},{17,1},{25,9},{2,18},{10... | collective-permute-start | bytes 1179656 | tf_op jit(solution)/shard_map/ppermute | solution.py:352
  36.5 19.0 %collective-permute-start.4 = (bf16[8,192,128]{2,1,0:T(8,128)(2,1)S(1)}, bf16[8,192,128]{2,1,0:T(8,128)(2,1)S(1)}, u32[]{:S(2)}, u32[]{:S(2)}) collective-permute-start(bf16[8,192,128]{2,1,0:T(8,128)(2,1)S(1)} %all-to-all-done.f0), channel_id=1, source_target_pairs={{0,8},{8,16},{16,24},{24,0},{1,9},{9,17},{17,25},{25,1},{2,10},{10... | collective-permute-start | bytes 1179656 | tf_op jit(solution)/shard_map/ppermute | solution.py:352
  60.1 4.0 %collective-permute-start.9 = (bf16[128,128]{1,0:T(8,128)(2,1)S(1)}, bf16[128,128]{1,0:T(8,128)(2,1)S(1)}, u32[]{:S(2)}, u32[]{:S(2)}) collective-permute-start(bf16[128,128]{1,0:T(8,128)(2,1)S(1)} %get-tuple-element.59.x0), channel_id=1, source_target_pairs={{0,24},{8,0},{16,8},{24,16},{1,25},{9,1},{17,9},{25,17},{2,26},{10... | collective-permute-start | bytes 98312 | tf_op jit(solution)/shard_map/ppermute | solution.py:352
  61.1 5.6 %collective-permute-start.8 = (bf16[128,128]{1,0:T(8,128)(2,1)S(1)}, bf16[128,128]{1,0:T(8,128)(2,1)S(1)}, u32[]{:S(2)}, u32[]{:S(2)}) collective-permute-start(bf16[128,128]{1,0:T(8,128)(2,1)S(1)} %get-tuple-element.59.x0), channel_id=1, source_target_pairs={{0,16},{8,24},{16,0},{24,8},{1,17},{9,25},{17,1},{25,9},{2,18},{10... | collective-permute-start | bytes 98312 | tf_op jit(solution)/shard_map/ppermute | solution.py:352
  61.6 5.3 %collective-permute-start.7 = (bf16[128,128]{1,0:T(8,128)(2,1)S(1)}, bf16[128,128]{1,0:T(8,128)(2,1)S(1)}, u32[]{:S(2)}, u32[]{:S(2)}) collective-permute-start(bf16[128,128]{1,0:T(8,128)(2,1)S(1)} %get-tuple-element.59.x0), channel_id=1, source_target_pairs={{0,8},{8,16},{16,24},{24,0},{1,9},{9,17},{17,25},{25,1},{2,10},{10... | collective-permute-start | bytes 98312 | tf_op jit(solution)/shard_map/ppermute | solution.py:352
  67.0 17.4 %copy-start = (bf16[1,512,128]{2,1,0:T(8,128)(2,1)S(1)}, bf16[1,512,128]{2,1,0:T(8,128)(2,1)}, u32[]{:S(2)}) copy-start(bf16[1,512,128]{2,1,0:T(8,128)(2,1)} %param.11) | copy-start | bytes 393220
  67.0 17.4 %copy-start.6 = (bf16[1,512,128]{2,1,0:T(8,128)(2,1)S(1)}, bf16[1,512,128]{2,1,0:T(8,128)(2,1)}, u32[]{:S(2)}) copy-start(bf16[1,512,128]{2,1,0:T(8,128)(2,1)} %param.14) | copy-start | bytes 393220
  84.3 0.7 copy-start.11
  86.4 1.2 collective-permute-start.10
  87.7 4.9 %collective-permute-start.13 = (f32[8,128]{1,0:T(8,128)S(1)}, f32[8,128]{1,0:T(8,128)S(1)}, u32[]{:S(2)}, u32[]{:S(2)}) collective-permute-start(f32[8,128]{1,0:T(8,128)S(1)} %add.11.s0), channel_id=1, source_target_pairs={{0,6},{2,0},{4,2},{6,4},{1,7},{3,1},{5,3},{7,5},{8,14},{10,8},{12,... | collective-permute-start | bytes 12296 | tf_op jit(solution)/shard_map/ppermute | solution.py:352
  88.1 5.1 %collective-permute-start.12 = (f32[8,128]{1,0:T(8,128)S(1)}, f32[8,128]{1,0:T(8,128)S(1)}, u32[]{:S(2)}, u32[]{:S(2)}) collective-permute-start(f32[8,128]{1,0:T(8,128)S(1)} %add.11.s0), channel_id=1, source_target_pairs={{0,4},{2,6},{4,0},{6,2},{1,5},{3,7},{5,1},{7,3},{8,12},{10,14},{12... | collective-permute-start | bytes 12296 | tf_op jit(solution)/shard_map/ppermute | solution.py:352
  90.7 3.6 %collective-permute-start.11 = (f32[8,128]{1,0:T(8,128)S(1)}, f32[8,128]{1,0:T(8,128)S(1)}, u32[]{:S(2)}, u32[]{:S(2)}) collective-permute-start(f32[8,128]{1,0:T(8,128)S(1)} %add.11.s0), channel_id=1, source_target_pairs={{0,2},{2,4},{4,6},{6,0},{1,3},{3,5},{5,7},{7,1},{8,10},{10,12},{12... | collective-permute-start | bytes 12296 | tf_op jit(solution)/shard_map/ppermute | solution.py:352
  94.7 5.9 %collective-permute-start.16 = (bf16[144,128]{1,0:T(8,128)(2,1)S(1)}, bf16[144,128]{1,0:T(8,128)(2,1)S(1)}, u32[]{:S(2)}, u32[]{:S(2)}) collective-permute-start(bf16[144,128]{1,0:T(8,128)(2,1)S(1)} %get-tuple-element.75.x0), channel_id=1, source_target_pairs={{0,8},{8,16},{16,24},{24,0},{1,9},{9,17},{17,25},{25,1},{2,10},{10... | collective-permute-start | bytes 110600 | tf_op jit(solution)/shard_map/ppermute | solution.py:352
  95.7 5.5 %collective-permute-start.15 = (bf16[144,128]{1,0:T(8,128)(2,1)S(1)}, bf16[144,128]{1,0:T(8,128)(2,1)S(1)}, u32[]{:S(2)}, u32[]{:S(2)}) collective-permute-start(bf16[144,128]{1,0:T(8,128)(2,1)S(1)} %get-tuple-element.75.x0), channel_id=1, source_target_pairs={{0,16},{8,24},{16,0},{24,8},{1,17},{9,25},{17,1},{25,9},{2,18},{10... | collective-permute-start | bytes 110600 | tf_op jit(solution)/shard_map/ppermute | solution.py:352
  98.3 4.0 %collective-permute-start.14 = (bf16[144,128]{1,0:T(8,128)(2,1)S(1)}, bf16[144,128]{1,0:T(8,128)(2,1)S(1)}, u32[]{:S(2)}, u32[]{:S(2)}) collective-permute-start(bf16[144,128]{1,0:T(8,128)(2,1)S(1)} %get-tuple-element.75.x0), channel_id=1, source_target_pairs={{0,24},{8,0},{16,8},{24,16},{1,25},{9,1},{17,9},{25,17},{2,26},{10... | collective-permute-start | bytes 110600 | tf_op jit(solution)/shard_map/ppermute | solution.py:352
  124.4 0.8 copy-start.8
  125.2 0.8 copy-start.9
  126.0 0.8 copy-start.12
  126.7 0.8 copy-start.14
  127.5 0.7 copy-start.15
  128.2 6.5 %copy-start.13 = (bf16[8,192,128]{2,1,0:T(8,128)(2,1)S(1)}, bf16[8,192,128]{2,1,0:T(8,128)(2,1)}, u32[]{:S(2)}) copy-start(bf16[8,192,128]{2,1,0:T(8,128)(2,1)} %copy-done.12) | copy-start | bytes 1179652
  128.2 22.5 %copy-start.10 = (bf16[8,192,128]{2,1,0:T(8,128)(2,1)S(1)}, bf16[8,192,128]{2,1,0:T(8,128)(2,1)}, u32[]{:S(2)}) copy-start(bf16[8,192,128]{2,1,0:T(8,128)(2,1)} %copy-done.9) | copy-start | bytes 1179652
  128.2 22.5 %all-to-all-start.4 = ((bf16[8,4,64,128]{3,2,1,0:T(8,128)(2,1)}), bf16[8,4,64,128]{3,2,1,0:T(8,128)(2,1)S(1)}, u32[]{:S(2)}, u32[]{:S(2)}) async-start(bf16[8,4,64,128]{3,2,1,0:T(8,128)(2,1)} %copy-done.8), calls=%async_computation.4 | async-start | bytes 1048576 | tf_op jit(solution)/shard_map/all_to_all | solution.py:356
  131.9 15.4 %collective-permute-start.18 = (bf16[8,192,128]{2,1,0:T(8,128)(2,1)}, bf16[8,192,128]{2,1,0:T(8,128)(2,1)S(1)}, u32[]{:S(2)}, u32[]{:S(2)}) collective-permute-start(bf16[8,192,128]{2,1,0:T(8,128)(2,1)} %copy-done.15), channel_id=1, source_target_pairs={{0,24},{8,0},{16,8},{24,16},{1,25},{9,1},{17,9},{25,17},{2,26},{10... | collective-permute-start | bytes 1179656 | tf_op jit(solution)/shard_map/ppermute | solution.py:352
  134.1 13.2 %collective-permute-start.19 = (bf16[8,192,128]{2,1,0:T(8,128)(2,1)}, bf16[8,192,128]{2,1,0:T(8,128)(2,1)S(1)}, u32[]{:S(2)}, u32[]{:S(2)}) collective-permute-start(bf16[8,192,128]{2,1,0:T(8,128)(2,1)} %copy-done.14), channel_id=1, source_target_pairs={{0,16},{8,24},{16,0},{24,8},{1,17},{9,25},{17,1},{25,9},{2,18},{10... | collective-permute-start | bytes 1179656 | tf_op jit(solution)/shard_map/ppermute | solution.py:352
  134.7 16.0 %collective-permute-start.20 = (bf16[8,192,128]{2,1,0:T(8,128)(2,1)S(1)}, bf16[8,192,128]{2,1,0:T(8,128)(2,1)S(1)}, u32[]{:S(2)}, u32[]{:S(2)}) collective-permute-start(bf16[8,192,128]{2,1,0:T(8,128)(2,1)S(1)} %copy-done.13), channel_id=1, source_target_pairs={{0,8},{8,16},{16,24},{24,0},{1,9},{9,17},{17,25},{25,1},{2,10},{10... | collective-permute-start | bytes 1179656 | tf_op jit(solution)/shard_map/ppermute | solution.py:352
  151.7 20.1 %all-to-all-start.5 = ((bf16[8,192,128]{2,1,0:T(8,128)(2,1)}), bf16[8,192,128]{2,1,0:T(8,128)(2,1)S(1)}, u32[]{:S(2)}, u32[]{:S(2)}) async-start(bf16[8,192,128]{2,1,0:T(8,128)(2,1)} %get-tuple-element.87), calls=%async_computation.5 | async-start | bytes 786432 | tf_op jit(solution)/shard_map/all_to_all | solution.py:356
  158.5 6.6 %collective-permute-start.17 = (bf16[256,128]{1,0:T(8,128)(2,1)S(1)}, bf16[256,128]{1,0:T(8,128)(2,1)S(1)}, u32[]{:S(2)}, u32[]{:S(2)}) collective-permute-start(bf16[256,128]{1,0:T(8,128)(2,1)S(1)} %get-tuple-element.81), channel_id=1, source_target_pairs={{8,0},{16,8},{24,16},{32,24},{40,32},{48,40},{56,48},{64,56},{72,6... | collective-permute-start | bytes 196616 | tf_op jit(solution)/shard_map/ppermute | solution.py:445
  159.8 5.3 %collective-permute-start.21 = (bf16[64,128]{1,0:T(8,128)(2,1)S(1)}, bf16[64,128]{1,0:T(8,128)(2,1)S(1)}, u32[]{:S(2)}, u32[]{:S(2)}) collective-permute-start(bf16[64,128]{1,0:T(8,128)(2,1)S(1)} %get-tuple-element.89), channel_id=1, source_target_pairs={{0,24},{8,0},{16,8},{24,16},{1,25},{9,1},{17,9},{25,17},{2,26},{10... | collective-permute-start | bytes 49160 | tf_op jit(solution)/shard_map/ppermute | solution.py:352
  161.8 5.2 %collective-permute-start.22 = (bf16[64,128]{1,0:T(8,128)(2,1)S(1)}, bf16[64,128]{1,0:T(8,128)(2,1)S(1)}, u32[]{:S(2)}, u32[]{:S(2)}) collective-permute-start(bf16[64,128]{1,0:T(8,128)(2,1)S(1)} %get-tuple-element.90), channel_id=1, source_target_pairs={{0,16},{8,24},{16,0},{24,8},{1,17},{9,25},{17,1},{25,9},{2,18},{10... | collective-permute-start | bytes 49160 | tf_op jit(solution)/shard_map/ppermute | solution.py:352
  164.6 4.9 %collective-permute-start.23 = (bf16[64,128]{1,0:T(8,128)(2,1)S(1)}, bf16[64,128]{1,0:T(8,128)(2,1)S(1)}, u32[]{:S(2)}, u32[]{:S(2)}) collective-permute-start(bf16[64,128]{1,0:T(8,128)(2,1)S(1)} %get-tuple-element.91), channel_id=1, source_target_pairs={{0,8},{8,16},{16,24},{24,0},{1,9},{9,17},{17,25},{25,1},{2,10},{10... | collective-permute-start | bytes 49160 | tf_op jit(solution)/shard_map/ppermute | solution.py:352
where the time goes:
time: 175 us; the launch traced here: 173 us
  starting transfers between devices  56.7 us (32%)
  waiting for transfers between devices  55.7 us (32%)
  blocking collectives  30.6 us (17%)
  Pallas kernels  20.9 us (12%)
  local copies, waits for them, and re-layouts  8.56 us (5%)
    ppermute x22, waiting for transfers between devices, turn(): lax.ppermute(value, axis, [(i, (i + by) % size) for i in range(size)])  47.2 us
    all_to_all x2, blocking collectives, swap(): return lax.all_to_all(value, 'z', 0, 0, tiled=True)  30.6 us
    ppermute x22, starting transfers between devices, turn(): lax.ppermute(value, axis, [(i, (i + by) % size) for i in range(size)])  26.2 us
    all_to_all x4, starting transfers between devices, swap(): return lax.all_to_all(value, 'z', 0, 0, tiled=True)  25.4 us
    pallas_call x10, Pallas kernels, call(): pl.pallas_call(body, out_shape=[jax.ShapeDtypeStruct(s, d) for s, d in ou...  20.9 us
    unnamed x35, local copies, waits for them, and re-layouts  7.11 us
    all_to_all x4, waiting for transfers between devices, swap(): return lax.all_to_all(value, 'z', 0, 0, tiled=True)  6.99 us
    ppermute x1, starting transfers between devices, per_device(): prev = lax.ppermute(last, seq, [(i, i + 1) for i in range(NZ * NX - 1)])  3.7 us
  transfers between devices with their start and end apart: 28, of which 19 were waited for; matrix products, arithmetic and copies ran while one was open for 0% of the time, Pallas kernels for 1%

commit v1 on v0

--- a/solution.py
+++ b/solution.py
@@ -35,14 +35,14 @@
     return lax.dot_general(a, b, dims, preferred_element_type=f32)
 
 
-def call(body, outs, ins, specs, scratch=(), out_specs=None):
+def call(body, outs, ins, specs, scratch=(), out_specs=None, vmem=8):
     return pl.pallas_call(
         body,
         out_shape=[jax.ShapeDtypeStruct(s, d) for s, d in outs],
         in_specs=list(specs),
         out_specs=out_specs or [VM] * len(outs),
         scratch_shapes=list(scratch),
-        compiler_params=pltpu.CompilerParams(vmem_limit_bytes=40 << 20),
+        compiler_params=pltpu.CompilerParams(vmem_limit_bytes=vmem << 20),
     )(*ins)
 
 
@@ -76,17 +76,13 @@
     mine = chosen_block(pos, names)
     pairs = [
         (v.at[mine, pl.ds(HALF, HALF)], low),
-        (k.at[3], last.at[pl.ds(0, BLK)]),
-        (v.at[3], last.at[pl.ds(BLK, BLK)]),
+        (k.at[3], last.at[:, pl.ds(0, BLK)]),
+        (v.at[3], last.at[:, pl.ds(BLK, BLK)]),
     ]
     for i in range(NZ):
         pairs.append((k.at[mine], top.at[i, pl.ds(0, BLK)]))
         pairs.append((v.at[mine, pl.ds(0, HALF)], top.at[i, pl.ds(BLK, HALF)]))
-    copies = [pltpu.make_async_copy(a, b, sems.at[i]) for i, (a, b) in enumerate(pairs)]
-    for c in copies:
-        c.start()
-    for c in copies:
-        c.wait()
+    run_copies(pairs, sems)
 
 
 def place_of(pos, names, b, j):
@@ -102,16 +98,7 @@
     return jnp.where(live, back_x * NZ + jnp.right_shift(name, 4), OWN), live
 
 
-def pool_copies(far, low, k, v, prev, pool, sems):
-    pairs = [(f, pool.at[pl.ds(NZ * j, NZ), pl.ds(0, TOP)]) for j, f in enumerate(far)]
-    pairs += [
-        (low.at[:, j], pool.at[pl.ds(NZ * j, NZ), pl.ds(TOP, HALF)]) for j in range(NX)
-    ]
-    pairs += [
-        (k, pool.at[pl.ds(OWN, 4), pl.ds(0, BLK)]),
-        (v, pool.at[pl.ds(OWN, 4), pl.ds(BLK, BLK)]),
-        (prev, pool.at[PREV]),
-    ]
+def run_copies(pairs, sems):
     copies = [pltpu.make_async_copy(a, b, sems.at[i]) for i, (a, b) in enumerate(pairs)]
     for c in copies:
         c.start()
@@ -119,11 +106,24 @@
         c.wait()
 
 
+def pool_pairs(far, low, k, v, prev, pool):
+    left, right = pl.ds(0, BLK), pl.ds(BLK, BLK)
+    pairs = [(prev, pool.at[PREV])]
+    pairs.append((k, pool.at[pl.ds(OWN, 4), :, left]))
+    pairs.append((v, pool.at[pl.ds(OWN, 4), :, right]))
+    for j, f in enumerate(far):
+        spot = pl.ds(NZ * j, NZ)
+        pairs.append((f.at[:, pl.ds(0, BLK)], pool.at[spot, :, left]))
+        pairs.append((f.at[:, pl.ds(BLK, HALF)], pool.at[spot, pl.ds(0, HALF), right]))
+        pairs.append((low.at[:, j], pool.at[spot, pl.ds(HALF, HALF), right]))
+    return pairs
+
+
 GROUP = 4
 
 
 def attend_kernel(pos, names, q, lk, f0, f1, f2, f3, low, k, v, prev, att, lse, state, pool, s_scr, sems):
-    pool_copies((f0, f1, f2, f3), low, k, v, prev, pool, sems)
+    run_copies(pool_pairs((f0, f1, f2, f3), low, k, v, prev, pool), sems)
     nsel = names.shape[1]
     scale = BLK ** (-0.5)
 
@@ -132,7 +132,7 @@
         top = None
         for g in range(0, nsel, GROUP):
             spots = [place_of(pos, names, b, j) for j in range(g, g + GROUP)]
-            keys = jnp.concatenate([pool[p, 0:BLK, :] for p, _ in spots], axis=0)
+            keys = jnp.concatenate([pool[p, :, 0:BLK] for p, _ in spots], axis=0)
             s = mm(qb, keys, NT)
             for i, (_, live) in enumerate(spots):
                 j = g + i
@@ -149,7 +149,7 @@
             for i in range(GROUP):
                 part = part + w[:, i * BLK : (i + 1) * BLK]
             vals = jnp.concatenate(
-                [pool[place_of(pos, names, b, j)[0], BLK:, :] for j in range(g, g + GROUP)], axis=0
+                [pool[place_of(pos, names, b, j)[0], :, BLK:] for j in range(g, g + GROUP)], axis=0
             )
             acc = acc + mm(w.astype(bf16), vals)
         total = jnp.sum(part, axis=1, keepdims=True)
@@ -168,6 +168,12 @@
     total = total.astype(bf16)
     for i in range(NZ):
         out[i] = total
+
+
+def spread_kernel(l0, l1, l2, l3, out, block, sems):
+    for j, r in enumerate((l0, l1, l2, l3)):
+        block[j] = r[...]
+    run_copies([(block, out.at[i]) for i in range(NZ)], sems)
 
 
 def linear_kernel(pos, lq, lk, att, gain, cot, x0, x1, x2, x3, zs, lin, prior, sums):
@@ -253,9 +259,9 @@
 
 
 def backward_kernel(pos, names, q, lse, att, cot, lq, lk, glin, pairs_t, mix_t, local,
-                    x0, x1, x2, x3, zs, f0, f1, f2, f3, low, k, v, prev,
-                    dlk, dq, o0, o1, o2, o3, olow, own, back, ggain, pool, acc, gatt, delta, sems):
-    pool_copies((f0, f1, f2, f3), low, k, v, prev, pool, sems)
+                    x0, x1, x2, x3, zs, pool,
+                    dlk, dq, o0, o1, o2, o3, olow, own, back, ggain,
+                    acc, gatt, delta, near, lows, sems):
     nsel = names.shape[1]
     scale = BLK ** (-0.5)
     later = jnp.zeros((BLK, BLK), f32)
@@ -284,43 +290,50 @@
         lse_b = lse[pl.ds(b, 1), :]
         delta_b = delta[pl.ds(b, 1), :]
         dqb = jnp.zeros((BLK, BLK), f32)
+        zero = jnp.zeros((BLK, BLK), bf16)
+        both = jnp.concatenate(
+            [jnp.concatenate([qb, zero], axis=1), jnp.concatenate([zero, gb], axis=1)], axis=0
+        )
         for g in range(0, nsel, GROUP):
             spots = [place_of(pos, names, b, j) for j in range(g, g + GROUP)]
-            keys = jnp.concatenate([pool[p, 0:BLK, :] for p, _ in spots], axis=0)
-            vals = jnp.concatenate([pool[p, BLK:, :] for p, _ in spots], axis=0)
-            s = mm(keys, qb, NT)
-            dp = mm(vals, gb, NT)
+            keyval = jnp.concatenate([pool[p] for p, _ in spots], axis=0)
+            sdp = mm(keyval, both, NT)
             pieces = []
             for i, (_, live) in enumerate(spots):
                 r = slice(i * BLK, (i + 1) * BLK)
-                piece = s[r] * scale + jnp.where(live, 0.0, masked_value)
+                piece = sdp[r, 0:BLK] * scale + (jnp.where(live, 0.0, masked_value) - lse_b)
                 if g + i == 0:
                     keep = lax.broadcasted_iota(jnp.int32, (BLK, BLK), 0) <= lax.broadcasted_iota(
                         jnp.int32, (BLK, BLK), 1
                     )
                     piece = jnp.where(keep, piece, masked_value)
-                pieces.append(jnp.exp(piece - lse_b))
+                pieces.append(jnp.exp(piece))
             p = jnp.concatenate(pieces, axis=0)
-            ds = (p * (dp - delta_b)).astype(bf16)
-            dv = mm(p.astype(bf16), gb)
-            dk = mm(ds, qb)
-            dqb = dqb + mm(ds, keys, TN)
+            ds = (p * (sdp[:, BLK:] - delta_b)).astype(bf16)
+            grads = mm(jnp.concatenate([ds, p.astype(bf16)], axis=1), both)
+            dqb = dqb + mm(ds, keyval[:, 0:BLK], TN)
             for i, (spot, _) in enumerate(spots):
-                r = slice(i * BLK, (i + 1) * BLK)
-                acc[spot, 0:BLK, :] += dk[r]
-                acc[spot, BLK:, :] += dv[r]
+                acc[spot] += grads[i * BLK : (i + 1) * BLK]
         dq[rows(b), :] = (dqb * scale).astype(bf16)
         return carry
 
     lax.fori_loop(0, 4, block, 0)
-    for j, o in enumerate((o0, o1, o2, o3)):
-        o[:, 0:BLK, :] = (acc[NZ * j : NZ * (j + 1), 0:BLK, :] * scale).astype(bf16)
-        o[:, BLK:, :] = acc[NZ * j : NZ * (j + 1), BLK:TOP, :].astype(bf16)
-        olow[:, j] = acc[NZ * j : NZ * (j + 1), TOP:, :].astype(bf16)
-    own[:, 0:BLK, :] = acc[OWN : OWN + 4, 0:BLK, :] * scale
-    own[:, BLK:, :] = acc[OWN : OWN + 4, BLK:, :]
-    back[0:BLK] = (acc[PREV, 0:BLK, :] * scale).astype(bf16)
-    back[BLK:] = acc[PREV, BLK:, :].astype(bf16)
+    for j in range(NX):
+        lows[:, j] = acc[NZ * j : NZ * (j + 1), HALF:, BLK:].astype(bf16)
+    near[:, 0:BLK] = (acc[0:NZ, :, 0:BLK] * scale).astype(bf16)
+    near[:, BLK:] = acc[0:NZ, 0:HALF, BLK:].astype(bf16)
+    copies = [pltpu.make_async_copy(lows, olow, sems.at[0]), pltpu.make_async_copy(near, o0, sems.at[1])]
+    for c in copies:
+        c.start()
+    for j, o in ((1, o1), (2, o2), (3, o3)):
+        o[:, 0:BLK] = (acc[NZ * j : NZ * (j + 1), :, 0:BLK] * scale).astype(bf16)
+        o[:, BLK:] = acc[NZ * j : NZ * (j + 1), 0:HALF, BLK:].astype(bf16)
+    own[:, :, 0:BLK] = acc[OWN : OWN + 4, :, 0:BLK] * scale
+    own[:, :, BLK:] = acc[OWN : OWN + 4, :, BLK:]
+    back[:, 0:BLK] = (acc[PREV, :, 0:BLK] * scale).astype(bf16)
+    back[:, BLK:] = acc[PREV, :, BLK:].astype(bf16)
+    for c in copies:
+        c.wait()
 
 
 def fold_kernel(a0, a1, a2, a3, low, top, l0, l1, l2, l3):
@@ -339,17 +352,24 @@
     for i in range(1, NZ):
         total = total + top[i].astype(f32)
     part = l0[...].astype(f32) + l1[...].astype(f32) + l2[...].astype(f32) + l3[...].astype(f32)
-    gathered = jnp.concatenate([total, part], axis=0)
+    far_key, far_value = total[0:BLK], jnp.concatenate([total[BLK:], part], axis=0)
     for b in range(4):
-        whole = own[b] + jnp.where(mine == b, gathered, 0.0)
+        r = slice(b * BLK, (b + 1) * BLK)
+        dk = own[b, :, 0:BLK] + jnp.where(mine == b, far_key, 0.0)
+        dv = own[b, :, BLK:] + jnp.where(mine == b, far_value, 0.0)
         if b == 3:
-            whole = whole + back[...].astype(f32)
-        gk[b * BLK : (b + 1) * BLK] = whole[0:BLK].astype(bf16)
-        gv[b * BLK : (b + 1) * BLK] = whole[BLK:].astype(bf16)
+            dk = dk + back[:, 0:BLK].astype(f32)
+            dv = dv + back[:, BLK:].astype(f32)
+        gk[r] = dk.astype(bf16)
+        gv[r] = dv.astype(bf16)
 
 
 def turn(value, axis, size, by):
     return lax.ppermute(value, axis, [(i, (i + by) % size) for i in range(size)])
+
+
+def in_hbm(value):
+    return pltpu.with_memory_space_constraint(value, pltpu.HBM)
 
 
 def swap(value):
@@ -378,28 +398,34 @@
 
     tops, low, last = call(
         pick_kernel,
-        [((NZ, TOP, width), bf16), ((HALF, width), bf16), ((2 * BLK, width), bf16)],
-        (pos, key_block, k4, v4),
+        [((NZ, TOP, width), bf16), ((HALF, width), bf16), ((BLK, 2 * BLK), bf16)],
+        (pos, key_block, in_hbm(k4), in_hbm(v4)),
         [SM, VM, HB, HB],
         [pltpu.SemaphoreType.DMA((2 * NZ + 3,))],
         [HB, VM, VM],
     )
     prev = lax.ppermute(last, seq, [(i, i + 1) for i in range(NZ * NX - 1)])
-    lows = jnp.stack([low] + [turn(low, "x", NX, j) for j in range(1, NX)])
+    lows = [low] + [turn(low, "x", NX, j) for j in range(1, NX)]
+    (lows,) = call(
+        spread_kernel,
+        [((NZ, NX, HALF, width), bf16)],
+        lows,
+        [VM] * 4,
+        [pltpu.VMEM((NX, HALF, width), bf16), pltpu.SemaphoreType.DMA((NZ,))],
+        [HB],
+    )
     tops = swap(tops)
-    lows = jnp.broadcast_to(lows[None], (NZ, NX, HALF, width))
-    tops, lows, prev = lax.optimization_barrier((tops, lows, prev))
+    tops, lows = lax.optimization_barrier((tops, lows))
     far = [tops] + turns([tops] * 3, 1)
     lows = swap(lows)
 
-    pool_scratch = [pltpu.VMEM((POOL, 2 * BLK, width), bf16)]
-    sems = [pltpu.SemaphoreType.DMA((2 * NX + 3,))]
-    att, lse, state = call(
+    att, lse, state, pool = call(
         attend_kernel,
-        [((512, width), bf16), ((8, BLK), f32), (tile, bf16)],
+        [((512, width), bf16), ((8, BLK), f32), (tile, bf16), ((POOL, BLK, 2 * BLK), bf16)],
         (pos, names, q, lk, *far, lows, k4, v4, prev),
         [SM, SM, VM, VM] + [AN] * 8,
-        pool_scratch + [pltpu.VMEM((BLK, names.shape[1] * BLK), f32)] + sems,
+        [pltpu.VMEM((BLK, names.shape[1] * BLK), f32), pltpu.SemaphoreType.DMA((3 * NX + 3,))],
+        vmem=16,
     )
 
     xs = [state] + [turn(state, "x", NX, j) for j in range(1, NX)]
@@ -431,14 +457,20 @@
         backward_kernel,
         [((512, width), bf16), ((512, width), bf16)]
         + [((NZ, TOP, width), bf16)] * 4
-        + [((NZ, NX, HALF, width), bf16), ((4, 2 * BLK, width), f32)]
-        + [((2 * BLK, width), bf16), ((8, BLK), f32)],
-        (pos, names, q, lse, att, cot, lq, lk, glin, pairs_t, mix_t, local, *ex, swap(wide))
-        + (*far, lows, k4, v4, prev),
-        [SM, SM] + [VM] * 15 + [AN] * 8,
-        pool_scratch
-        + [pltpu.VMEM((POOL, 2 * BLK, width), f32), pltpu.VMEM((512, width), bf16), pltpu.VMEM((8, BLK), f32)]
-        + sems,
+        + [((NZ, NX, HALF, width), bf16), ((4, BLK, 2 * BLK), f32)]
+        + [((BLK, 2 * BLK), bf16), ((8, BLK), f32)],
+        (pos, names, q, lse, att, cot, lq, lk, glin, pairs_t, mix_t, local, *ex, swap(wide), pool),
+        [SM, SM] + [VM] * 16,
+        [
+            pltpu.VMEM((POOL, BLK, 2 * BLK), f32),
+            pltpu.VMEM((512, width), bf16),
+            pltpu.VMEM((8, BLK), f32),
+            pltpu.VMEM((NZ, TOP, width), bf16),
+            pltpu.VMEM((NZ, NX, HALF, width), bf16),
+            pltpu.SemaphoreType.DMA((2,)),
+        ],
+        [VM, VM, HB, VM, VM, VM, HB, VM, VM, VM],
+        vmem=24,
     )
     dlk, dq = outs[0], outs[1]
     far_out, low_out, own, back, gg = outs[2:6], outs[6], outs[7], outs[8], outs[9]

time: 175 us -> 183 us (1.046)
  Pallas kernels: 20.9 us -> 35.5 us
  local copies, waits for them, and re-layouts: 8.56 us -> 2.19 us
    pallas_call x10 -> x11, Pallas kernels: 20.9 us -> 35.5 us  [call(): pl.pallas_call(body, out_shape=[jax.ShapeDtypeStruct(s, d) for s, d in ou...]
    ppermute x22, waiting for transfers between devices: 47.2 us -> 35.3 us  [turn(): lax.ppermute(value, axis, [(i, (i + by) % size) for i in range(size)])]
    ppermute x1, waiting for transfers between devices: 1.51 us -> 12.6 us  [per_device(): prev = lax.ppermute(last, seq, [(i, i + 1) for i in range(NZ * NX - 1)])]
    unnamed x35 -> x17, local copies, waits for them, and re-layouts: 7.11 us -> 1.67 us
    ppermute x22, starting transfers between devices: 26.2 us -> 29.7 us  [turn(): lax.ppermute(value, axis, [(i, (i + by) % size) for i in range(size)])]
    all_to_all x4, starting transfers between devices: 25.4 us -> 22.2 us  [swap(): return lax.all_to_all(value, 'z', 0, 0, tiled=True)]
  transfers between devices with their start and end apart: 28 -> 28, of which waited for: 19 -> 18; matrix products, arithmetic and copies ran while one was open for 0% -> 0% of each run, Pallas kernels for 1% -> 1%
where the time goes in v1:
time: 183 us; the launch traced here: 182 us
  starting transfers between devices  56.9 us (31%)
  waiting for transfers between devices  55.7 us (30%)
  Pallas kernels  35.5 us (19%)
  blocking collectives  30.5 us (17%)
  local copies, waits for them, and re-layouts  2.19 us (1%)
    pallas_call x11, Pallas kernels, call(): pl.pallas_call(body, out_shape=[jax.ShapeDtypeStruct(s, d) for s, d in ou...  35.5 us
    ppermute x22, waiting for transfers between devices, turn(): lax.ppermute(value, axis, [(i, (i + by) % size) for i in range(size)])  35.3 us
    all_to_all x2, blocking collectives, swap(): return lax.all_to_all(value, 'z', 0, 0, tiled=True)  30.5 us
    ppermute x22, starting transfers between devices, turn(): lax.ppermute(value, axis, [(i, (i + by) % size) for i in range(size)])  29.7 us
    all_to_all x4, starting transfers between devices, swap(): return lax.all_to_all(value, 'z', 0, 0, tiled=True)  22.2 us
    ppermute x1, waiting for transfers between devices, per_device(): prev = lax.ppermute(last, seq, [(i, i + 1) for i in range(NZ * NX - 1)])  12.6 us
    all_to_all x4, waiting for transfers between devices, swap(): return lax.all_to_all(value, 'z', 0, 0, tiled=True)  7.78 us
    ppermute x1, starting transfers between devices, per_device(): prev = lax.ppermute(last, seq, [(i, i + 1) for i in range(NZ * NX - 1)])  3.7 us
  transfers between devices with their start and end apart: 28, of which 18 were waited for; matrix products, arithmetic and copies ran while one was open for 0% of the time, Pallas kernels for 1%

profile of v1, /device:TPU:8, one launch (start us, length us, event | category | flops | bytes accessed | tf_op | source)
XLA Modules:
  0.0 181.7 jit_solution(2344825376819366759)
XLA Ops:
  0.6 0.0 copy-start.4
  0.6 0.0 copy-start.3
  0.7 0.9 copy.15.names
  1.6 0.1 pad_add_fusion.pos
  1.6 13.9 %shard_map.135 = (bf16[8,192,128]{2,1,0:T(8,128)(2,1)}, bf16[64,128]{1,0:T(8,128)(2,1)S(1)}, bf16[128,256]{1,0:T(8,128)(2,1)S(1)}) custom-call(s32[2]{0:T(128)S(1)} %pad_add_fusion.pos, s32[128,20]{1,0:T(8,128)S(1)} %copy.15.names, bf16[4,128,128]{2,1,0:T(8,128)(2,1)} %bitcast.25, bf16[4,128,128]{2,1,0:T(8,128)(2,1)} %bitcast.27), custom_call_target="tpu_custom_call" | custom-call | tf_op jit(solution)/shard_map/pallas_call | solution.py:39
  15.5 8.5 %all-to-all-start = ((bf16[8,192,128]{2,1,0:T(8,128)(2,1)}), bf16[8,192,128]{2,1,0:T(8,128)(2,1)S(1)}, u32[]{:S(2)}, u32[]{:S(2)}) async-start(bf16[8,192,128]{2,1,0:T(8,128)(2,1)} %get-tuple-element.52), calls=%async_computation | async-start | bytes 786432 | tf_op jit(solution)/shard_map/all_to_all | solution.py:376
  24.0 2.8 %collective-permute-start.2 = (bf16[64,128]{1,0:T(8,128)(2,1)S(1)}, bf16[64,128]{1,0:T(8,128)(2,1)S(1)}, u32[]{:S(2)}, u32[]{:S(2)}) collective-permute-start(bf16[64,128]{1,0:T(8,128)(2,1)S(1)} %get-tuple-element.53.l0), channel_id=1, source_target_pairs={{0,24},{8,0},{16,8},{24,16},{1,25},{9,1},{17,9},{25,17},{2,26},{10... | collective-permute-start | bytes 49160 | tf_op jit(solution)/shard_map/ppermute | solution.py:368
  26.7 0.8 collective-permute-start.1
  27.5 0.9 collective-permute-start
  28.4 3.6 %collective-permute-done.1.l2 = bf16[64,128]{1,0:T(8,128)(2,1)S(1)} collective-permute-done((bf16[64,128]{1,0:T(8,128)(2,1)S(1)}, bf16[64,128]{1,0:T(8,128)(2,1)S(1)}, u32[]{:S(2)}, u32[]{:S(2)}) %collective-permute-start.1) | collective-permute-done | bytes 16416 | tf_op jit(solution)/shard_map/ppermute | solution.py:368
  32.0 0.5 collective-permute-done.l1
  32.5 0.9 shard_map.136
  33.4 0.0 copy-start.2
  33.4 0.0 copy-start.6
  33.4 5.3 %all-to-all-done.f0 = bf16[8,192,128]{2,1,0:T(8,128)(2,1)S(1)} async-done(((bf16[8,192,128]{2,1,0:T(8,128)(2,1)}), bf16[8,192,128]{2,1,0:T(8,128)(2,1)S(1)}, u32[]{:S(2)}, u32[]{:S(2)}) %all-to-all-start) | async-done | bytes 393248 | tf_op jit(solution)/shard_map/all_to_all | solution.py:376
  38.7 3.5 %all-to-all-start.1 = ((bf16[8,4,64,128]{3,2,1,0:T(8,128)(2,1)}), bf16[8,4,64,128]{3,2,1,0:T(8,128)(2,1)S(1)}, u32[]{:S(2)}, u32[]{:S(2)}) async-start(bf16[8,4,64,128]{3,2,1,0:T(8,128)(2,1)} %shard_map.136), calls=%async_computation.1 | async-start | bytes 1048576 | tf_op jit(solution)/shard_map/all_to_all | solution.py:376
  42.2 2.8 %collective-permute-start.5 = (bf16[8,192,128]{2,1,0:T(8,128)(2,1)S(1)}, bf16[8,192,128]{2,1,0:T(8,128)(2,1)S(1)}, u32[]{:S(2)}, u32[]{:S(2)}) collective-permute-start(bf16[8,192,128]{2,1,0:T(8,128)(2,1)S(1)} %all-to-all-done.f0), channel_id=1, source_target_pairs={{0,24},{8,0},{16,8},{24,16},{1,25},{9,1},{17,9},{25,17},{2,26},{10... | collective-permute-start | bytes 1179656 | tf_op jit(solution)/shard_map/ppermute | solution.py:368
  45.0 0.8 collective-permute-start.4
  45.8 0.9 collective-permute-start.3
  46.7 3.7 %collective-permute-start.6 = (bf16[128,256]{1,0:T(8,128)(2,1)S(1)}, bf16[128,256]{1,0:T(8,128)(2,1)S(1)}, u32[]{:S(2)}, u32[]{:S(2)}) collective-permute-start(bf16[128,256]{1,0:T(8,128)(2,1)S(1)} %get-tuple-element.56), channel_id=1, source_target_pairs={{0,8},{8,16},{16,24},{24,32},{32,40},{40,48},{48,56},{56,64},{64,7... | collective-permute-start | bytes 196616 | tf_op jit(solution)/shard_map/ppermute | solution.py:407
  50.4 12.6 %collective-permute-done.6.prev = bf16[128,256]{1,0:T(8,128)(2,1)S(1)} collective-permute-done((bf16[128,256]{1,0:T(8,128)(2,1)S(1)}, bf16[128,256]{1,0:T(8,128)(2,1)S(1)}, u32[]{:S(2)}, u32[]{:S(2)}) %collective-permute-start.6) | collective-permute-done | bytes 65568 | tf_op jit(solution)/shard_map/ppermute | solution.py:407
  63.1 1.7 collective-permute-done.3.f1
  64.8 4.9 %shard_map.137 = (bf16[512,128]{1,0:T(8,128)(2,1)S(1)}, f32[8,128]{1,0:T(8,128)S(1)}, bf16[128,128]{1,0:T(8,128)(2,1)S(1)}, bf16[37,128,256]{2,1,0:T(8,128)(2,1)S(1)}) custom-call(s32[2]{0:T(128)S(1)} %pad_add_fusion.pos, s32[4,20]{1,0:T(4,128)S(1)} %constant_dynamic-slice_fusion.names, bf16[512,128]{1,0:T(8,128)(2,1)S(1)} %bitcast.29, ...), custom_call_target="tpu_custom_call" | custom-call | tf_op jit(solution)/shard_map/pallas_call | solution.py:39
  69.7 2.1 %collective-permute-start.9 = (bf16[128,128]{1,0:T(8,128)(2,1)S(1)}, bf16[128,128]{1,0:T(8,128)(2,1)S(1)}, u32[]{:S(2)}, u32[]{:S(2)}) collective-permute-start(bf16[128,128]{1,0:T(8,128)(2,1)S(1)} %get-tuple-element.58.x0), channel_id=1, source_target_pairs={{0,24},{8,0},{16,8},{24,16},{1,25},{9,1},{17,9},{25,17},{2,26},{10... | collective-permute-start | bytes 98312 | tf_op jit(solution)/shard_map/ppermute | solution.py:368
  71.9 0.8 collective-permute-start.8
  72.6 0.8 collective-permute-start.7
  73.5 0.3 collective-permute-done.9.x3
  73.7 3.6 %collective-permute-done.8.x2 = bf16[128,128]{1,0:T(8,128)(2,1)S(1)} collective-permute-done((bf16[128,128]{1,0:T(8,128)(2,1)S(1)}, bf16[128,128]{1,0:T(8,128)(2,1)S(1)}, u32[]{:S(2)}, u32[]{:S(2)}) %collective-permute-start.8) | collective-permute-done | bytes 32800 | tf_op jit(solution)/shard_map/ppermute | solution.py:368
  77.3 0.5 collective-permute-done.7.x1
  77.8 17.3 %all_to_all.30.zs = bf16[8,128,128]{2,1,0:T(8,128)(2,1)S(1)} all-to-all(bf16[8,128,128]{2,1,0:T(8,128)(2,1)S(1)} %shard_map.138), channel_id=1, replica_groups=mesh['z'=8,'x'=4,'y'=4,'c'=2] {'z'}, dimensions={0} | all-to-all | bytes 524288 | tf_op jit(solution)/shard_map/all_to_all | solution.py:376
  95.1 1.4 shard_map.139
  96.5 0.1 collective-permute-start.10
  96.6 1.2 collective-permute-done.10
  97.7 0.4 collective-permute-start.13
  98.2 2.6 %collective-permute-start.12 = (f32[8,128]{1,0:T(8,128)S(1)}, f32[8,128]{1,0:T(8,128)S(1)}, u32[]{:S(2)}, u32[]{:S(2)}) collective-permute-start(f32[8,128]{1,0:T(8,128)S(1)} %add.11.s0), channel_id=1, source_target_pairs={{0,4},{2,6},{4,0},{6,2},{1,5},{3,7},{5,1},{7,3},{8,12},{10,14},{12... | collective-permute-start | bytes 12296 | tf_op jit(solution)/shard_map/ppermute | solution.py:368
  100.8 1.9 %collective-permute-start.11 = (f32[8,128]{1,0:T(8,128)S(1)}, f32[8,128]{1,0:T(8,128)S(1)}, u32[]{:S(2)}, u32[]{:S(2)}) collective-permute-start(f32[8,128]{1,0:T(8,128)S(1)} %add.11.s0), channel_id=1, source_target_pairs={{0,2},{2,4},{4,6},{6,0},{1,3},{3,5},{5,7},{7,1},{8,10},{10,12},{12... | collective-permute-start | bytes 12296 | tf_op jit(solution)/shard_map/ppermute | solution.py:368
  102.7 0.6 collective-permute-done.12.s2
  103.3 1.1 collective-permute-done.11.s1
  104.4 0.4 shard_map.140
  104.8 1.1 collective-permute-start.16
  105.9 2.4 %collective-permute-start.15 = (bf16[144,128]{1,0:T(8,128)(2,1)S(1)}, bf16[144,128]{1,0:T(8,128)(2,1)S(1)}, u32[]{:S(2)}, u32[]{:S(2)}) collective-permute-start(bf16[144,128]{1,0:T(8,128)(2,1)S(1)} %get-tuple-element.74.x0), channel_id=1, source_target_pairs={{0,16},{8,24},{16,0},{24,8},{1,17},{9,25},{17,1},{25,9},{2,18},{10... | collective-permute-start | bytes 110600 | tf_op jit(solution)/shard_map/ppermute | solution.py:368
  108.3 0.7 collective-permute-start.14
  109.0 1.3 shard_map.141
  110.4 1.0 collective-permute-done.15.x2
  111.4 0.9 collective-permute-done.14.x1
  112.3 13.2 %all_to_all.31.zs = bf16[8,144,128]{2,1,0:T(8,128)(2,1)S(1)} all-to-all(bf16[8,144,128]{2,1,0:T(8,128)(2,1)S(1)} %shard_map.142), channel_id=1, replica_groups=mesh['z'=8,'x'=4,'y'=4,'c'=2] {'z'}, dimensions={0} | all-to-all | bytes 589824 | tf_op jit(solution)/shard_map/all_to_all | solution.py:376
  125.5 10.3 %shard_map.143 = (bf16[512,128]{1,0:T(8,128)(2,1)}, bf16[512,128]{1,0:T(8,128)(2,1)}, bf16[8,192,128]{2,1,0:T(8,128)(2,1)S(1)}, bf16[8,192,128]{2,1,0:T(8,128)(2...) custom-call(s32[2]{0:T(128)S(1)} %pad_add_fusion.pos, ...), custom_call_target="tpu_custom_call" | custom-call | tf_op jit(solution)/shard_map/pallas_call | solution.py:39
  135.8 0.7 copy-done.7
  136.6 3.5 %all-to-all-start.4 = ((bf16[8,4,64,128]{3,2,1,0:T(8,128)(2,1)}), bf16[8,4,64,128]{3,2,1,0:T(8,128)(2,1)S(1)}, u32[]{:S(2)}, u32[]{:S(2)}) async-start(bf16[8,4,64,128]{3,2,1,0:T(8,128)(2,1)} %get-tuple-element.86), calls=%async_computation.4 | async-start | bytes 1048576 | tf_op jit(solution)/shard_map/all_to_all | solution.py:376
  140.1 2.0 %collective-permute-start.18 = (bf16[8,192,128]{2,1,0:T(8,128)(2,1)}, bf16[8,192,128]{2,1,0:T(8,128)(2,1)S(1)}, u32[]{:S(2)}, u32[]{:S(2)}) collective-permute-start(bf16[8,192,128]{2,1,0:T(8,128)(2,1)} %get-tuple-element.83), channel_id=1, source_target_pairs={{0,24},{8,0},{16,8},{24,16},{1,25},{9,1},{17,9},{25,17},{2,26},{10... | collective-permute-start | bytes 1179656 | tf_op jit(solution)/shard_map/ppermute | solution.py:368
  142.0 1.0 collective-permute-start.19
  143.0 0.1 collective-permute-start.20
  143.1 12.4 %collective-permute-done.18.a1 = bf16[8,192,128]{2,1,0:T(8,128)(2,1)S(1)} collective-permute-done((bf16[8,192,128]{2,1,0:T(8,128)(2,1)}, bf16[8,192,128]{2,1,0:T(8,128)(2,1)S(1)}, u32[]{:S(2)}, u32[]{:S(2)}) %collective-permute-start.18) | collective-permute-done | bytes 393248 | tf_op jit(solution)/shard_map/ppermute | solution.py:368
  155.5 3.6 %collective-permute-done.20.a3 = bf16[8,192,128]{2,1,0:T(8,128)(2,1)S(1)} collective-permute-done((bf16[8,192,128]{2,1,0:T(8,128)(2,1)S(1)}, bf16[8,192,128]{2,1,0:T(8,128)(2,1)S(1)}, u32[]{:S(2)}, u32[]{:S(2)}) %collective-permute-start.20) | collective-permute-done | bytes 393248 | tf_op jit(solution)/shard_map/ppermute | solution.py:368
  159.0 0.9 shard_map.144
  160.0 6.8 %all-to-all-start.5 = ((bf16[8,192,128]{2,1,0:T(8,128)(2,1)}), bf16[8,192,128]{2,1,0:T(8,128)(2,1)S(1)}, u32[]{:S(2)}, u32[]{:S(2)}) async-start(bf16[8,192,128]{2,1,0:T(8,128)(2,1)} %get-tuple-element.87), calls=%async_computation.5 | async-start | bytes 786432 | tf_op jit(solution)/shard_map/all_to_all | solution.py:376
  166.7 1.3 collective-permute-start.17
  168.0 2.2 %collective-permute-start.21 = (bf16[64,128]{1,0:T(8,128)(2,1)S(1)}, bf16[64,128]{1,0:T(8,128)(2,1)S(1)}, u32[]{:S(2)}, u32[]{:S(2)}) collective-permute-start(bf16[64,128]{1,0:T(8,128)(2,1)S(1)} %get-tuple-element.89), channel_id=1, source_target_pairs={{0,24},{8,0},{16,8},{24,16},{1,25},{9,1},{17,9},{25,17},{2,26},{10... | collective-permute-start | bytes 49160 | tf_op jit(solution)/shard_map/ppermute | solution.py:368
  170.2 2.6 %collective-permute-start.22 = (bf16[64,128]{1,0:T(8,128)(2,1)S(1)}, bf16[64,128]{1,0:T(8,128)(2,1)S(1)}, u32[]{:S(2)}, u32[]{:S(2)}) collective-permute-start(bf16[64,128]{1,0:T(8,128)(2,1)S(1)} %get-tuple-element.90), channel_id=1, source_target_pairs={{0,16},{8,24},{16,0},{24,8},{1,17},{9,25},{17,1},{25,9},{2,18},{10... | collective-permute-start | bytes 49160 | tf_op jit(solution)/shard_map/ppermute | solution.py:368
  172.8 0.5 slice.3
  173.3 2.1 %collective-permute-done.22.l2 = bf16[64,128]{1,0:T(8,128)(2,1)S(1)} collective-permute-done((bf16[64,128]{1,0:T(8,128)(2,1)S(1)}, bf16[64,128]{1,0:T(8,128)(2,1)S(1)}, u32[]{:S(2)}, u32[]{:S(2)}) %collective-permute-start.22) | collective-permute-done | bytes 16416 | tf_op jit(solution)/shard_map/ppermute | solution.py:368
  175.5 2.3 %collective-permute-done.23.l3 = bf16[64,128]{1,0:T(8,128)(2,1)S(1)} collective-permute-done((bf16[64,128]{1,0:T(8,128)(2,1)S(1)}, bf16[64,128]{1,0:T(8,128)(2,1)S(1)}, u32[]{:S(2)}, u32[]{:S(2)}) %collective-permute-start.23) | collective-permute-done | bytes 16416 | tf_op jit(solution)/shard_map/ppermute | solution.py:368
  177.8 2.5 %all-to-all-done.5.top = bf16[8,192,128]{2,1,0:T(8,128)(2,1)S(1)} async-done(((bf16[8,192,128]{2,1,0:T(8,128)(2,1)}), bf16[8,192,128]{2,1,0:T(8,128)(2,1)S(1)}, u32[]{:S(2)}, u32[]{:S(2)}) %all-to-all-start.5) | async-done | bytes 393248 | tf_op jit(solution)/shard_map/all_to_all | solution.py:376
  180.3 1.4 shard_map.145
  (26 shorter events, 0.1 us)
Async XLA Ops:
  0.6 64.2 %copy-start.4 = (bf16[1,512,128]{2,1,0:T(8,128)(2,1)S(1)}, bf16[1,512,128]{2,1,0:T(8,128)(2,1)}, u32[]{:S(2)}) copy-start(bf16[1,512,128]{2,1,0:T(8,128)(2,1)} %param.10) | copy-start | bytes 393220
  0.6 64.2 %copy-start.3 = (bf16[1,512,128]{2,1,0:T(8,128)(2,1)S(1)}, bf16[1,512,128]{2,1,0:T(8,128)(2,1)}, u32[]{:S(2)}) copy-start(bf16[1,512,128]{2,1,0:T(8,128)(2,1)} %param.9) | copy-start | bytes 393220
  0.7 64.2 %copy-start.1 = (bf16[1,512,128]{2,1,0:T(8,128)(2,1)S(1)}, bf16[1,512,128]{2,1,0:T(8,128)(2,1)}, u32[]{:S(2)}) copy-start(bf16[1,512,128]{2,1,0:T(8,128)(2,1)} %param.12) | copy-start | bytes 393220
  0.7 64.2 %copy-start.5 = (bf16[1,512,128]{2,1,0:T(8,128)(2,1)S(1)}, bf16[1,512,128]{2,1,0:T(8,128)(2,1)}, u32[]{:S(2)}) copy-start(bf16[1,512,128]{2,1,0:T(8,128)(2,1)} %param.8) | copy-start | bytes 393220
  15.5 23.2 %all-to-all-start = ((bf16[8,192,128]{2,1,0:T(8,128)(2,1)}), bf16[8,192,128]{2,1,0:T(8,128)(2,1)S(1)}, u32[]{:S(2)}, u32[]{:S(2)}) async-start(bf16[8,192,128]{2,1,0:T(8,128)(2,1)} %get-tuple-element.52), calls=%async_computation | async-start | bytes 786432 | tf_op jit(solution)/shard_map/all_to_all | solution.py:376
  24.0 4.4 %collective-permute-start.2 = (bf16[64,128]{1,0:T(8,128)(2,1)S(1)}, bf16[64,128]{1,0:T(8,128)(2,1)S(1)}, u32[]{:S(2)}, u32[]{:S(2)}) collective-permute-start(bf16[64,128]{1,0:T(8,128)(2,1)S(1)} %get-tuple-element.53.l0), channel_id=1, source_target_pairs={{0,24},{8,0},{16,8},{24,16},{1,25},{9,1},{17,9},{25,17},{2,26},{10... | collective-permute-start | bytes 49160 | tf_op jit(solution)/shard_map/ppermute | solution.py:368
  26.7 5.2 %collective-permute-start.1 = (bf16[64,128]{1,0:T(8,128)(2,1)S(1)}, bf16[64,128]{1,0:T(8,128)(2,1)S(1)}, u32[]{:S(2)}, u32[]{:S(2)}) collective-permute-start(bf16[64,128]{1,0:T(8,128)(2,1)S(1)} %get-tuple-element.53.l0), channel_id=1, source_target_pairs={{0,16},{8,24},{16,0},{24,8},{1,17},{9,25},{17,1},{25,9},{2,18},{10... | collective-permute-start | bytes 49160 | tf_op jit(solution)/shard_map/ppermute | solution.py:368
  27.5 4.9 %collective-permute-start = (bf16[64,128]{1,0:T(8,128)(2,1)S(1)}, bf16[64,128]{1,0:T(8,128)(2,1)S(1)}, u32[]{:S(2)}, u32[]{:S(2)}) collective-permute-start(bf16[64,128]{1,0:T(8,128)(2,1)S(1)} %get-tuple-element.53.l0), channel_id=1, source_target_pairs={{0,8},{8,16},{16,24},{24,0},{1,9},{9,17},{17,25},{25,1},{2,10},{10... | collective-permute-start | bytes 49160 | tf_op jit(solution)/shard_map/ppermute | solution.py:368
  33.4 61.7 %copy-start = (bf16[1,512,128]{2,1,0:T(8,128)(2,1)S(1)}, bf16[1,512,128]{2,1,0:T(8,128)(2,1)}, u32[]{:S(2)}) copy-start(bf16[1,512,128]{2,1,0:T(8,128)(2,1)} %param.11) | copy-start | bytes 393220
  33.4 61.7 %copy-start.2 = (bf16[1,512,128]{2,1,0:T(8,128)(2,1)S(1)}, bf16[1,512,128]{2,1,0:T(8,128)(2,1)}, u32[]{:S(2)}) copy-start(bf16[1,512,128]{2,1,0:T(8,128)(2,1)} %param.14) | copy-start | bytes 393220
  33.4 61.6 %copy-start.6 = (f32[1,128]{1,0:T(1,128)S(1)}, f32[1,128]{1,0:T(1,128)}, u32[]{:S(2)}) copy-start(f32[1,128]{1,0:T(1,128)} %gain.5) | copy-start | bytes 1540
  38.7 26.1 %all-to-all-start.1 = ((bf16[8,4,64,128]{3,2,1,0:T(8,128)(2,1)}), bf16[8,4,64,128]{3,2,1,0:T(8,128)(2,1)S(1)}, u32[]{:S(2)}, u32[]{:S(2)}) async-start(bf16[8,4,64,128]{3,2,1,0:T(8,128)(2,1)} %shard_map.136), calls=%async_computation.1 | async-start | bytes 1048576 | tf_op jit(solution)/shard_map/all_to_all | solution.py:376
  42.2 20.9 %collective-permute-start.5 = (bf16[8,192,128]{2,1,0:T(8,128)(2,1)S(1)}, bf16[8,192,128]{2,1,0:T(8,128)(2,1)S(1)}, u32[]{:S(2)}, u32[]{:S(2)}) collective-permute-start(bf16[8,192,128]{2,1,0:T(8,128)(2,1)S(1)} %all-to-all-done.f0), channel_id=1, source_target_pairs={{0,24},{8,0},{16,8},{24,16},{1,25},{9,1},{17,9},{25,17},{2,26},{10... | collective-permute-start | bytes 1179656 | tf_op jit(solution)/shard_map/ppermute | solution.py:368
  45.0 18.1 %collective-permute-start.4 = (bf16[8,192,128]{2,1,0:T(8,128)(2,1)S(1)}, bf16[8,192,128]{2,1,0:T(8,128)(2,1)S(1)}, u32[]{:S(2)}, u32[]{:S(2)}) collective-permute-start(bf16[8,192,128]{2,1,0:T(8,128)(2,1)S(1)} %all-to-all-done.f0), channel_id=1, source_target_pairs={{0,16},{8,24},{16,0},{24,8},{1,17},{9,25},{17,1},{25,9},{2,18},{10... | collective-permute-start | bytes 1179656 | tf_op jit(solution)/shard_map/ppermute | solution.py:368
  45.8 19.0 %collective-permute-start.3 = (bf16[8,192,128]{2,1,0:T(8,128)(2,1)S(1)}, bf16[8,192,128]{2,1,0:T(8,128)(2,1)S(1)}, u32[]{:S(2)}, u32[]{:S(2)}) collective-permute-start(bf16[8,192,128]{2,1,0:T(8,128)(2,1)S(1)} %all-to-all-done.f0), channel_id=1, source_target_pairs={{0,8},{8,16},{16,24},{24,0},{1,9},{9,17},{17,25},{25,1},{2,10},{10... | collective-permute-start | bytes 1179656 | tf_op jit(solution)/shard_map/ppermute | solution.py:368
  46.7 16.4 %collective-permute-start.6 = (bf16[128,256]{1,0:T(8,128)(2,1)S(1)}, bf16[128,256]{1,0:T(8,128)(2,1)S(1)}, u32[]{:S(2)}, u32[]{:S(2)}) collective-permute-start(bf16[128,256]{1,0:T(8,128)(2,1)S(1)} %get-tuple-element.56), channel_id=1, source_target_pairs={{0,8},{8,16},{16,24},{24,32},{32,40},{40,48},{48,56},{56,64},{64,7... | collective-permute-start | bytes 196616 | tf_op jit(solution)/shard_map/ppermute | solution.py:407
  69.7 4.0 %collective-permute-start.9 = (bf16[128,128]{1,0:T(8,128)(2,1)S(1)}, bf16[128,128]{1,0:T(8,128)(2,1)S(1)}, u32[]{:S(2)}, u32[]{:S(2)}) collective-permute-start(bf16[128,128]{1,0:T(8,128)(2,1)S(1)} %get-tuple-element.58.x0), channel_id=1, source_target_pairs={{0,24},{8,0},{16,8},{24,16},{1,25},{9,1},{17,9},{25,17},{2,26},{10... | collective-permute-start | bytes 98312 | tf_op jit(solution)/shard_map/ppermute | solution.py:368
  71.9 5.4 %collective-permute-start.8 = (bf16[128,128]{1,0:T(8,128)(2,1)S(1)}, bf16[128,128]{1,0:T(8,128)(2,1)S(1)}, u32[]{:S(2)}, u32[]{:S(2)}) collective-permute-start(bf16[128,128]{1,0:T(8,128)(2,1)S(1)} %get-tuple-element.58.x0), channel_id=1, source_target_pairs={{0,16},{8,24},{16,0},{24,8},{1,17},{9,25},{17,1},{25,9},{2,18},{10... | collective-permute-start | bytes 98312 | tf_op jit(solution)/shard_map/ppermute | solution.py:368
  72.6 5.1 %collective-permute-start.7 = (bf16[128,128]{1,0:T(8,128)(2,1)S(1)}, bf16[128,128]{1,0:T(8,128)(2,1)S(1)}, u32[]{:S(2)}, u32[]{:S(2)}) collective-permute-start(bf16[128,128]{1,0:T(8,128)(2,1)S(1)} %get-tuple-element.58.x0), channel_id=1, source_target_pairs={{0,8},{8,16},{16,24},{24,0},{1,9},{9,17},{17,25},{25,1},{2,10},{10... | collective-permute-start | bytes 98312 | tf_op jit(solution)/shard_map/ppermute | solution.py:368
  96.5 1.2 collective-permute-start.10
  97.7 4.9 %collective-permute-start.13 = (f32[8,128]{1,0:T(8,128)S(1)}, f32[8,128]{1,0:T(8,128)S(1)}, u32[]{:S(2)}, u32[]{:S(2)}) collective-permute-start(f32[8,128]{1,0:T(8,128)S(1)} %add.11.s0), channel_id=1, source_target_pairs={{0,6},{2,0},{4,2},{6,4},{1,7},{3,1},{5,3},{7,5},{8,14},{10,8},{12,... | collective-permute-start | bytes 12296 | tf_op jit(solution)/shard_map/ppermute | solution.py:368
  98.2 5.1 %collective-permute-start.12 = (f32[8,128]{1,0:T(8,128)S(1)}, f32[8,128]{1,0:T(8,128)S(1)}, u32[]{:S(2)}, u32[]{:S(2)}) collective-permute-start(f32[8,128]{1,0:T(8,128)S(1)} %add.11.s0), channel_id=1, source_target_pairs={{0,4},{2,6},{4,0},{6,2},{1,5},{3,7},{5,1},{7,3},{8,12},{10,14},{12... | collective-permute-start | bytes 12296 | tf_op jit(solution)/shard_map/ppermute | solution.py:368
  100.8 3.6 %collective-permute-start.11 = (f32[8,128]{1,0:T(8,128)S(1)}, f32[8,128]{1,0:T(8,128)S(1)}, u32[]{:S(2)}, u32[]{:S(2)}) collective-permute-start(f32[8,128]{1,0:T(8,128)S(1)} %add.11.s0), channel_id=1, source_target_pairs={{0,2},{2,4},{4,6},{6,0},{1,3},{3,5},{5,7},{7,1},{8,10},{10,12},{12... | collective-permute-start | bytes 12296 | tf_op jit(solution)/shard_map/ppermute | solution.py:368
  104.8 5.6 %collective-permute-start.16 = (bf16[144,128]{1,0:T(8,128)(2,1)S(1)}, bf16[144,128]{1,0:T(8,128)(2,1)S(1)}, u32[]{:S(2)}, u32[]{:S(2)}) collective-permute-start(bf16[144,128]{1,0:T(8,128)(2,1)S(1)} %get-tuple-element.74.x0), channel_id=1, source_target_pairs={{0,8},{8,16},{16,24},{24,0},{1,9},{9,17},{17,25},{25,1},{2,10},{10... | collective-permute-start | bytes 110600 | tf_op jit(solution)/shard_map/ppermute | solution.py:368
  105.9 5.5 %collective-permute-start.15 = (bf16[144,128]{1,0:T(8,128)(2,1)S(1)}, bf16[144,128]{1,0:T(8,128)(2,1)S(1)}, u32[]{:S(2)}, u32[]{:S(2)}) collective-permute-start(bf16[144,128]{1,0:T(8,128)(2,1)S(1)} %get-tuple-element.74.x0), channel_id=1, source_target_pairs={{0,16},{8,24},{16,0},{24,8},{1,17},{9,25},{17,1},{25,9},{2,18},{10... | collective-permute-start | bytes 110600 | tf_op jit(solution)/shard_map/ppermute | solution.py:368
  108.3 4.0 %collective-permute-start.14 = (bf16[144,128]{1,0:T(8,128)(2,1)S(1)}, bf16[144,128]{1,0:T(8,128)(2,1)S(1)}, u32[]{:S(2)}, u32[]{:S(2)}) collective-permute-start(bf16[144,128]{1,0:T(8,128)(2,1)S(1)} %get-tuple-element.74.x0), channel_id=1, source_target_pairs={{0,24},{8,0},{16,8},{24,16},{1,25},{9,1},{17,9},{25,17},{2,26},{10... | collective-permute-start | bytes 110600 | tf_op jit(solution)/shard_map/ppermute | solution.py:368
  135.8 0.8 copy-start.7
  136.6 22.5 %all-to-all-start.4 = ((bf16[8,4,64,128]{3,2,1,0:T(8,128)(2,1)}), bf16[8,4,64,128]{3,2,1,0:T(8,128)(2,1)S(1)}, u32[]{:S(2)}, u32[]{:S(2)}) async-start(bf16[8,4,64,128]{3,2,1,0:T(8,128)(2,1)} %get-tuple-element.86), calls=%async_computation.4 | async-start | bytes 1048576 | tf_op jit(solution)/shard_map/all_to_all | solution.py:376
  140.1 15.4 %collective-permute-start.18 = (bf16[8,192,128]{2,1,0:T(8,128)(2,1)}, bf16[8,192,128]{2,1,0:T(8,128)(2,1)S(1)}, u32[]{:S(2)}, u32[]{:S(2)}) collective-permute-start(bf16[8,192,128]{2,1,0:T(8,128)(2,1)} %get-tuple-element.83), channel_id=1, source_target_pairs={{0,24},{8,0},{16,8},{24,16},{1,25},{9,1},{17,9},{25,17},{2,26},{10... | collective-permute-start | bytes 1179656 | tf_op jit(solution)/shard_map/ppermute | solution.py:368
  142.0 13.5 %collective-permute-start.19 = (bf16[8,192,128]{2,1,0:T(8,128)(2,1)}, bf16[8,192,128]{2,1,0:T(8,128)(2,1)S(1)}, u32[]{:S(2)}, u32[]{:S(2)}) collective-permute-start(bf16[8,192,128]{2,1,0:T(8,128)(2,1)} %copy-done.7), channel_id=1, source_target_pairs={{0,16},{8,24},{16,0},{24,8},{1,17},{9,25},{17,1},{25,9},{2,18},{10... | collective-permute-start | bytes 1179656 | tf_op jit(solution)/shard_map/ppermute | solution.py:368
  143.0 16.0 %collective-permute-start.20 = (bf16[8,192,128]{2,1,0:T(8,128)(2,1)S(1)}, bf16[8,192,128]{2,1,0:T(8,128)(2,1)S(1)}, u32[]{:S(2)}, u32[]{:S(2)}) collective-permute-start(bf16[8,192,128]{2,1,0:T(8,128)(2,1)S(1)} %get-tuple-element.85), channel_id=1, source_target_pairs={{0,8},{8,16},{16,24},{24,0},{1,9},{9,17},{17,25},{25,1},{2,10},{10... | collective-permute-start | bytes 1179656 | tf_op jit(solution)/shard_map/ppermute | solution.py:368
  160.0 20.3 %all-to-all-start.5 = ((bf16[8,192,128]{2,1,0:T(8,128)(2,1)}), bf16[8,192,128]{2,1,0:T(8,128)(2,1)S(1)}, u32[]{:S(2)}, u32[]{:S(2)}) async-start(bf16[8,192,128]{2,1,0:T(8,128)(2,1)} %get-tuple-element.87), calls=%async_computation.5 | async-start | bytes 786432 | tf_op jit(solution)/shard_map/all_to_all | solution.py:376
  166.7 6.6 %collective-permute-start.17 = (bf16[128,256]{1,0:T(8,128)(2,1)S(1)}, bf16[128,256]{1,0:T(8,128)(2,1)S(1)}, u32[]{:S(2)}, u32[]{:S(2)}) collective-permute-start(bf16[128,256]{1,0:T(8,128)(2,1)S(1)} %get-tuple-element.81), channel_id=1, source_target_pairs={{8,0},{16,8},{24,16},{32,24},{40,32},{48,40},{56,48},{64,56},{72,6... | collective-permute-start | bytes 196616 | tf_op jit(solution)/shard_map/ppermute | solution.py:477
  168.0 5.3 %collective-permute-start.21 = (bf16[64,128]{1,0:T(8,128)(2,1)S(1)}, bf16[64,128]{1,0:T(8,128)(2,1)S(1)}, u32[]{:S(2)}, u32[]{:S(2)}) collective-permute-start(bf16[64,128]{1,0:T(8,128)(2,1)S(1)} %get-tuple-element.89), channel_id=1, source_target_pairs={{0,24},{8,0},{16,8},{24,16},{1,25},{9,1},{17,9},{25,17},{2,26},{10... | collective-permute-start | bytes 49160 | tf_op jit(solution)/shard_map/ppermute | solution.py:368
  170.2 5.2 %collective-permute-start.22 = (bf16[64,128]{1,0:T(8,128)(2,1)S(1)}, bf16[64,128]{1,0:T(8,128)(2,1)S(1)}, u32[]{:S(2)}, u32[]{:S(2)}) collective-permute-start(bf16[64,128]{1,0:T(8,128)(2,1)S(1)} %get-tuple-element.90), channel_id=1, source_target_pairs={{0,16},{8,24},{16,0},{24,8},{1,17},{9,25},{17,1},{25,9},{2,18},{10... | collective-permute-start | bytes 49160 | tf_op jit(solution)/shard_map/ppermute | solution.py:368
  172.8 4.9 %collective-permute-start.23 = (bf16[64,128]{1,0:T(8,128)(2,1)S(1)}, bf16[64,128]{1,0:T(8,128)(2,1)S(1)}, u32[]{:S(2)}, u32[]{:S(2)}) collective-permute-start(bf16[64,128]{1,0:T(8,128)(2,1)S(1)} %get-tuple-element.91), channel_id=1, source_target_pairs={{0,8},{8,16},{16,24},{24,0},{1,9},{9,17},{17,25},{25,1},{2,10},{10... | collective-permute-start | bytes 49160 | tf_op jit(solution)/shard_map/ppermute | solution.py:368

commit v2 on v1

--- a/solution.py
+++ b/solution.py
@@ -67,26 +67,28 @@
 def chosen_block(pos, names):
     base = pos[0] * 16 + pos[1] * 4
     far = names[...]
-    col = lax.broadcasted_iota(jnp.int32, far.shape, 1)
+    col = lax.broadcasted_iota(jnp.int32, far.shape, 0)
     hit = (col >= 2) & (far >= base) & (far < base + 4)
     return jnp.max(jnp.where(hit, far - base, 0).astype(f32)).astype(jnp.int32)
 
 
-def pick_kernel(pos, names, k, v, top, low, last, sems):
+def pick_kernel(pos, names, k, v, top, low, last, block, sems):
     mine = chosen_block(pos, names)
-    pairs = [
-        (v.at[mine, pl.ds(HALF, HALF)], low),
-        (k.at[3], last.at[:, pl.ds(0, BLK)]),
-        (v.at[3], last.at[:, pl.ds(BLK, BLK)]),
-    ]
-    for i in range(NZ):
-        pairs.append((k.at[mine], top.at[i, pl.ds(0, BLK)]))
-        pairs.append((v.at[mine, pl.ds(0, HALF)], top.at[i, pl.ds(BLK, HALF)]))
-    run_copies(pairs, sems)
+    run_copies(
+        [
+            (k.at[mine], block.at[pl.ds(0, BLK)]),
+            (v.at[mine, pl.ds(0, HALF)], block.at[pl.ds(BLK, HALF)]),
+            (v.at[mine, pl.ds(HALF, HALF)], low),
+            (k.at[3], last.at[:, pl.ds(0, BLK)]),
+            (v.at[3], last.at[:, pl.ds(BLK, BLK)]),
+        ],
+        sems,
+    )
+    run_copies([(block, top.at[i]) for i in range(NZ)], sems)
 
 
 def place_of(pos, names, b, j):
-    name = names[b, j]
+    name = names[j, b]
     base = pos[0] * 16 + pos[1] * 4
     live = name >= 0
     if j == 0:
@@ -120,11 +122,12 @@
 
 
 GROUP = 4
+BGROUP = 20
 
 
 def attend_kernel(pos, names, q, lk, f0, f1, f2, f3, low, k, v, prev, att, lse, state, pool, s_scr, sems):
     run_copies(pool_pairs((f0, f1, f2, f3), low, k, v, prev, pool), sems)
-    nsel = names.shape[1]
+    nsel = names.shape[0]
     scale = BLK ** (-0.5)
 
     def block(b, carry):
@@ -262,7 +265,7 @@
                     x0, x1, x2, x3, zs, pool,
                     dlk, dq, o0, o1, o2, o3, olow, own, back, ggain,
                     acc, gatt, delta, near, lows, sems):
-    nsel = names.shape[1]
+    nsel = names.shape[0]
     scale = BLK ** (-0.5)
     later = jnp.zeros((BLK, BLK), f32)
     for j, r in enumerate((x1, x2, x3)):
@@ -294,8 +297,8 @@
         both = jnp.concatenate(
             [jnp.concatenate([qb, zero], axis=1), jnp.concatenate([zero, gb], axis=1)], axis=0
         )
-        for g in range(0, nsel, GROUP):
-            spots = [place_of(pos, names, b, j) for j in range(g, g + GROUP)]
+        for g in range(0, nsel, BGROUP):
+            spots = [place_of(pos, names, b, j) for j in range(g, g + BGROUP)]
             keyval = jnp.concatenate([pool[p] for p, _ in spots], axis=0)
             sdp = mm(keyval, both, NT)
             pieces = []
@@ -346,22 +349,32 @@
         o[...] = part.astype(bf16)
 
 
-def finish_kernel(pos, names, own, back, top, l0, l1, l2, l3, gk, gv):
+def round_kernel(own, gk, gv):
+    for b in range(4):
+        r = slice(b * BLK, (b + 1) * BLK)
+        gk[r] = own[b, :, 0:BLK].astype(bf16)
+        gv[r] = own[b, :, BLK:].astype(bf16)
+
+
+def finish_kernel(pos, names, own, back, top, l0, l1, l2, l3, gk_in, gv_in, gk, gv):
     mine = chosen_block(pos, names)
     total = top[0].astype(f32)
     for i in range(1, NZ):
         total = total + top[i].astype(f32)
     part = l0[...].astype(f32) + l1[...].astype(f32) + l2[...].astype(f32) + l3[...].astype(f32)
     far_key, far_value = total[0:BLK], jnp.concatenate([total[BLK:], part], axis=0)
-    for b in range(4):
-        r = slice(b * BLK, (b + 1) * BLK)
-        dk = own[b, :, 0:BLK] + jnp.where(mine == b, far_key, 0.0)
-        dv = own[b, :, BLK:] + jnp.where(mine == b, far_value, 0.0)
-        if b == 3:
-            dk = dk + back[:, 0:BLK].astype(f32)
-            dv = dv + back[:, BLK:].astype(f32)
-        gk[r] = dk.astype(bf16)
-        gv[r] = dv.astype(bf16)
+    gk[...] = gk_in[...]
+    gv[...] = gv_in[...]
+    last = mine == 3
+    dk = own[3, :, 0:BLK] + back[:, 0:BLK].astype(f32)
+    dv = own[3, :, BLK:] + back[:, BLK:].astype(f32)
+    gk[rows(3), :] = (dk + jnp.where(last, far_key, 0.0)).astype(bf16)
+    gv[rows(3), :] = (dv + jnp.where(last, far_value, 0.0)).astype(bf16)
+
+    @pl.when(mine < 3)
+    def _():
+        gk[rows(mine), :] = (own[mine, :, 0:BLK] + far_key).astype(bf16)
+        gv[rows(mine), :] = (own[mine, :, BLK:] + far_value).astype(bf16)
 
 
 def turn(value, axis, size, by):
@@ -391,7 +404,8 @@
     xi = lax.axis_index("x")
     pos = jnp.stack([zi, xi]).astype(jnp.int32)
     features = float(NY * NC * width)
-    names = lax.dynamic_slice_in_dim(key_block, (zi * NX + xi) * 4, 4, 0)
+    key_block = key_block.T
+    names = lax.dynamic_slice_in_dim(key_block, (zi * NX + xi) * 4, 4, 1)
     k4 = k.reshape(4, BLK, width)
     v4 = v.reshape(4, BLK, width)
     tile = (BLK, BLK)
@@ -401,7 +415,7 @@
         [((NZ, TOP, width), bf16), ((HALF, width), bf16), ((BLK, 2 * BLK), bf16)],
         (pos, key_block, in_hbm(k4), in_hbm(v4)),
         [SM, VM, HB, HB],
-        [pltpu.SemaphoreType.DMA((2 * NZ + 3,))],
+        [pltpu.VMEM((TOP, width), bf16), pltpu.SemaphoreType.DMA((NZ,))],
         [HB, VM, VM],
     )
     prev = lax.ppermute(last, seq, [(i, i + 1) for i in range(NZ * NX - 1)])
@@ -424,7 +438,7 @@
         [((512, width), bf16), ((8, BLK), f32), (tile, bf16), ((POOL, BLK, 2 * BLK), bf16)],
         (pos, names, q, lk, *far, lows, k4, v4, prev),
         [SM, SM, VM, VM] + [AN] * 8,
-        [pltpu.VMEM((BLK, names.shape[1] * BLK), f32), pltpu.SemaphoreType.DMA((3 * NX + 3,))],
+        [pltpu.VMEM((BLK, names.shape[0] * BLK), f32), pltpu.SemaphoreType.DMA((3 * NX + 3,))],
         vmem=16,
     )
 
@@ -483,11 +497,12 @@
         [VM] * 5,
     )
     ends = [folded[1]] + turns(folded[2:], -1)
+    gk, gv = call(round_kernel, [((512, width), bf16)] * 2, (own,), [VM])
     gk, gv = call(
         finish_kernel,
         [((512, width), bf16), ((512, width), bf16)],
-        (pos, key_block, own, back, swap(folded[0]), *ends),
-        [SM] + [VM] * 8,
+        (pos, key_block, own, back, swap(folded[0]), *ends, gk, gv),
+        [SM] + [VM] * 10,
     )
     lead = lambda a: a[None]
     return (lead(mixed), lead(dq), lead(gk), lead(gv), lead(dlq), lead(dlk), gg[0:1])

time: 183 us -> 169 us (0.923)
  Pallas kernels: 35.5 us -> 22 us
    pallas_call x11 -> x12, Pallas kernels: 35.5 us -> 22 us  [call(): pl.pallas_call(body, out_shape=[jax.ShapeDtypeStruct(s, d) for s, d in ou...]
where the time goes in v2:
time: 169 us; the launch traced here: 167 us
  starting transfers between devices  57 us (34%)
  waiting for transfers between devices  55.6 us (33%)
  blocking collectives  30.4 us (18%)
  Pallas kernels  22 us (13%)
    ppermute x22, waiting for transfers between devices, turn(): lax.ppermute(value, axis, [(i, (i + by) % size) for i in range(size)])  35.3 us
    all_to_all x2, blocking collectives, swap(): return lax.all_to_all(value, 'z', 0, 0, tiled=True)  30.4 us
    ppermute x22, starting transfers between devices, turn(): lax.ppermute(value, axis, [(i, (i + by) % size) for i in range(size)])  29.7 us
    all_to_all x4, starting transfers between devices, swap(): return lax.all_to_all(value, 'z', 0, 0, tiled=True)  22.2 us
    pallas_call x12, Pallas kernels, call(): pl.pallas_call(body, out_shape=[jax.ShapeDtypeStruct(s, d) for s, d in ou...  22 us
    ppermute x1, waiting for transfers between devices, per_device(): prev = lax.ppermute(last, seq, [(i, i + 1) for i in range(NZ * NX - 1)])  12.6 us
    all_to_all x4, waiting for transfers between devices, swap(): return lax.all_to_all(value, 'z', 0, 0, tiled=True)  7.76 us
    ppermute x1, starting transfers between devices, per_device(): prev = lax.ppermute(last, seq, [(i, i + 1) for i in range(NZ * NX - 1)])  3.7 us
  transfers between devices with their start and end apart: 28, of which 18 were waited for; matrix products, arithmetic and copies ran while one was open for 0% of the time, Pallas kernels for 1%

profile of v2, /device:TPU:8, one launch (start us, length us, event | category | flops | bytes accessed | tf_op | source)
XLA Modules:
  0.0 167.4 jit_solution(6097514838419181868)
XLA Ops:
  0.6 0.0 copy-start.5
  0.6 0.0 copy-start.4
  0.7 0.1 pad_add_fusion.pos
  0.8 0.8 copy-done.6
  1.6 2.3 %shard_map.135 = (bf16[8,192,128]{2,1,0:T(8,128)(2,1)}, bf16[64,128]{1,0:T(8,128)(2,1)S(1)}, bf16[128,256]{1,0:T(8,128)(2,1)S(1)}) custom-call(s32[2]{0:T(128)S(1)} %pad_add_fusion.pos, s32[20,128]{1,0:T(8,128)S(1)} %bitcast.34, bf16[4,128,128]{2,1,0:T(8,128)(2,1)} %bitcast.30, bf16[4,128,128]{2,1,0:T(8,128)(2,1)} %bitcast.32), custom_call_target="tpu_custom_call" | custom-call | tf_op jit(solution)/shard_map/pallas_call | solution.py:39
  3.9 8.5 %all-to-all-start = ((bf16[8,192,128]{2,1,0:T(8,128)(2,1)}), bf16[8,192,128]{2,1,0:T(8,128)(2,1)S(1)}, u32[]{:S(2)}, u32[]{:S(2)}) async-start(bf16[8,192,128]{2,1,0:T(8,128)(2,1)} %get-tuple-element.54), calls=%async_computation | async-start | bytes 786432 | tf_op jit(solution)/shard_map/all_to_all | solution.py:389
  12.4 2.8 %collective-permute-start.2 = (bf16[64,128]{1,0:T(8,128)(2,1)S(1)}, bf16[64,128]{1,0:T(8,128)(2,1)S(1)}, u32[]{:S(2)}, u32[]{:S(2)}) collective-permute-start(bf16[64,128]{1,0:T(8,128)(2,1)S(1)} %get-tuple-element.55.l0), channel_id=1, source_target_pairs={{0,24},{8,0},{16,8},{24,16},{1,25},{9,1},{17,9},{25,17},{2,26},{10... | collective-permute-start | bytes 49160 | tf_op jit(solution)/shard_map/ppermute | solution.py:381
  15.2 0.8 collective-permute-start.1
  16.0 0.9 collective-permute-start
  16.9 3.6 %collective-permute-done.1.l2 = bf16[64,128]{1,0:T(8,128)(2,1)S(1)} collective-permute-done((bf16[64,128]{1,0:T(8,128)(2,1)S(1)}, bf16[64,128]{1,0:T(8,128)(2,1)S(1)}, u32[]{:S(2)}, u32[]{:S(2)}) %collective-permute-start.1) | collective-permute-done | bytes 16416 | tf_op jit(solution)/shard_map/ppermute | solution.py:381
  20.4 0.5 collective-permute-done.l1
  20.9 0.9 shard_map.136
  21.8 0.0 copy-start
  21.8 0.0 copy-start.8
  21.8 5.3 %all-to-all-done.f0 = bf16[8,192,128]{2,1,0:T(8,128)(2,1)S(1)} async-done(((bf16[8,192,128]{2,1,0:T(8,128)(2,1)}), bf16[8,192,128]{2,1,0:T(8,128)(2,1)S(1)}, u32[]{:S(2)}, u32[]{:S(2)}) %all-to-all-start) | async-done | bytes 393248 | tf_op jit(solution)/shard_map/all_to_all | solution.py:389
  27.1 3.5 %all-to-all-start.1 = ((bf16[8,4,64,128]{3,2,1,0:T(8,128)(2,1)}), bf16[8,4,64,128]{3,2,1,0:T(8,128)(2,1)S(1)}, u32[]{:S(2)}, u32[]{:S(2)}) async-start(bf16[8,4,64,128]{3,2,1,0:T(8,128)(2,1)} %shard_map.136), calls=%async_computation.1 | async-start | bytes 1048576 | tf_op jit(solution)/shard_map/all_to_all | solution.py:389
  30.6 2.8 %collective-permute-start.5 = (bf16[8,192,128]{2,1,0:T(8,128)(2,1)S(1)}, bf16[8,192,128]{2,1,0:T(8,128)(2,1)S(1)}, u32[]{:S(2)}, u32[]{:S(2)}) collective-permute-start(bf16[8,192,128]{2,1,0:T(8,128)(2,1)S(1)} %all-to-all-done.f0), channel_id=1, source_target_pairs={{0,24},{8,0},{16,8},{24,16},{1,25},{9,1},{17,9},{25,17},{2,26},{10... | collective-permute-start | bytes 1179656 | tf_op jit(solution)/shard_map/ppermute | solution.py:381
  33.4 0.8 collective-permute-start.4
  34.2 0.9 collective-permute-start.3
  35.1 3.7 %collective-permute-start.6 = (bf16[128,256]{1,0:T(8,128)(2,1)S(1)}, bf16[128,256]{1,0:T(8,128)(2,1)S(1)}, u32[]{:S(2)}, u32[]{:S(2)}) collective-permute-start(bf16[128,256]{1,0:T(8,128)(2,1)S(1)} %get-tuple-element.58), channel_id=1, source_target_pairs={{0,8},{8,16},{16,24},{24,32},{32,40},{40,48},{48,56},{56,64},{64,7... | collective-permute-start | bytes 196616 | tf_op jit(solution)/shard_map/ppermute | solution.py:421
  38.8 0.1 dynamic-slice_bitcast_fusion.names
  38.9 12.6 %collective-permute-done.6.prev = bf16[128,256]{1,0:T(8,128)(2,1)S(1)} collective-permute-done((bf16[128,256]{1,0:T(8,128)(2,1)S(1)}, bf16[128,256]{1,0:T(8,128)(2,1)S(1)}, u32[]{:S(2)}, u32[]{:S(2)}) %collective-permute-start.6) | collective-permute-done | bytes 65568 | tf_op jit(solution)/shard_map/ppermute | solution.py:421
  51.5 1.7 %collective-permute-done.3.f1 = bf16[8,192,128]{2,1,0:T(8,128)(2,1)S(1)} collective-permute-done((bf16[8,192,128]{2,1,0:T(8,128)(2,1)S(1)}, bf16[8,192,128]{2,1,0:T(8,128)(2,1)S(1)}, u32[]{:S(2)}, u32[]{:S(2)}) %collective-permute-start.3) | collective-permute-done | bytes 393248 | tf_op jit(solution)/shard_map/ppermute | solution.py:381
  53.3 5.1 %shard_map.137 = (bf16[512,128]{1,0:T(8,128)(2,1)S(1)}, f32[8,128]{1,0:T(8,128)S(1)}, bf16[128,128]{1,0:T(8,128)(2,1)S(1)}, bf16[37,128,256]{2,1,0:T(8,128)(2,1)S(1)}) custom-call(s32[2]{0:T(128)S(1)} %pad_add_fusion.pos, s32[20,4]{1,0:T(8,128)S(1)} %dynamic-slice_bitcast_fusion.names, bf16[512,128]{1,0:T(8,128)(2,1)S(1)} %bitcast.28, ...), custom_call_target="tpu_custom_call" | custom-call | tf_op jit(solution)/shard_map/pallas_call | solution.py:39
  58.4 2.1 %collective-permute-start.9 = (bf16[128,128]{1,0:T(8,128)(2,1)S(1)}, bf16[128,128]{1,0:T(8,128)(2,1)S(1)}, u32[]{:S(2)}, u32[]{:S(2)}) collective-permute-start(bf16[128,128]{1,0:T(8,128)(2,1)S(1)} %get-tuple-element.60.x0), channel_id=1, source_target_pairs={{0,24},{8,0},{16,8},{24,16},{1,25},{9,1},{17,9},{25,17},{2,26},{10... | collective-permute-start | bytes 98312 | tf_op jit(solution)/shard_map/ppermute | solution.py:381
  60.5 0.8 collective-permute-start.8
  61.3 0.8 collective-permute-start.7
  62.1 0.3 collective-permute-done.9.x3
  62.4 3.5 %collective-permute-done.8.x2 = bf16[128,128]{1,0:T(8,128)(2,1)S(1)} collective-permute-done((bf16[128,128]{1,0:T(8,128)(2,1)S(1)}, bf16[128,128]{1,0:T(8,128)(2,1)S(1)}, u32[]{:S(2)}, u32[]{:S(2)}) %collective-permute-start.8) | collective-permute-done | bytes 32800 | tf_op jit(solution)/shard_map/ppermute | solution.py:381
  65.9 0.5 collective-permute-done.7.x1
  66.5 17.2 %all_to_all.30.zs = bf16[8,128,128]{2,1,0:T(8,128)(2,1)S(1)} all-to-all(bf16[8,128,128]{2,1,0:T(8,128)(2,1)S(1)} %shard_map.138), channel_id=1, replica_groups=mesh['z'=8,'x'=4,'y'=4,'c'=2] {'z'}, dimensions={0} | all-to-all | bytes 524288 | tf_op jit(solution)/shard_map/all_to_all | solution.py:389
  83.7 1.4 shard_map.139
  85.1 0.1 collective-permute-start.10
  85.2 1.2 collective-permute-done.10
  86.3 0.5 collective-permute-start.13
  86.8 2.6 %collective-permute-start.12 = (f32[8,128]{1,0:T(8,128)S(1)}, f32[8,128]{1,0:T(8,128)S(1)}, u32[]{:S(2)}, u32[]{:S(2)}) collective-permute-start(f32[8,128]{1,0:T(8,128)S(1)} %add.11.s0), channel_id=1, source_target_pairs={{0,4},{2,6},{4,0},{6,2},{1,5},{3,7},{5,1},{7,3},{8,12},{10,14},{12... | collective-permute-start | bytes 12296 | tf_op jit(solution)/shard_map/ppermute | solution.py:381
  89.4 1.9 %collective-permute-start.11 = (f32[8,128]{1,0:T(8,128)S(1)}, f32[8,128]{1,0:T(8,128)S(1)}, u32[]{:S(2)}, u32[]{:S(2)}) collective-permute-start(f32[8,128]{1,0:T(8,128)S(1)} %add.11.s0), channel_id=1, source_target_pairs={{0,2},{2,4},{4,6},{6,0},{1,3},{3,5},{5,7},{7,1},{8,10},{10,12},{12... | collective-permute-start | bytes 12296 | tf_op jit(solution)/shard_map/ppermute | solution.py:381
  91.3 0.6 collective-permute-done.12.s2
  91.9 1.1 collective-permute-done.11.s1
  93.0 0.4 shard_map.140
  93.4 1.1 collective-permute-start.16
  94.5 2.5 %collective-permute-start.15 = (bf16[144,128]{1,0:T(8,128)(2,1)S(1)}, bf16[144,128]{1,0:T(8,128)(2,1)S(1)}, u32[]{:S(2)}, u32[]{:S(2)}) collective-permute-start(bf16[144,128]{1,0:T(8,128)(2,1)S(1)} %get-tuple-element.76.x0), channel_id=1, source_target_pairs={{0,16},{8,24},{16,0},{24,8},{1,17},{9,25},{17,1},{25,9},{2,18},{10... | collective-permute-start | bytes 110600 | tf_op jit(solution)/shard_map/ppermute | solution.py:381
  97.0 0.6 collective-permute-start.14
  97.6 1.3 shard_map.141
  99.0 1.0 collective-permute-done.15.x2
  100.0 1.0 collective-permute-done.14.x1
  101.0 13.2 %all_to_all.31.zs = bf16[8,144,128]{2,1,0:T(8,128)(2,1)S(1)} all-to-all(bf16[8,144,128]{2,1,0:T(8,128)(2,1)S(1)} %shard_map.142), channel_id=1, replica_groups=mesh['z'=8,'x'=4,'y'=4,'c'=2] {'z'}, dimensions={0} | all-to-all | bytes 589824 | tf_op jit(solution)/shard_map/all_to_all | solution.py:389
  114.2 8.1 %shard_map.143 = (bf16[512,128]{1,0:T(8,128)(2,1)}, bf16[512,128]{1,0:T(8,128)(2,1)}, bf16[8,192,128]{2,1,0:T(8,128)(2,1)S(1)}, bf16[8,192,128]{2,1,0:T(8,128)(2...) custom-call(s32[2]{0:T(128)S(1)} %pad_add_fusion.pos, ...), custom_call_target="tpu_custom_call" | custom-call | tf_op jit(solution)/shard_map/pallas_call | solution.py:39
  122.3 3.5 %all-to-all-start.4 = ((bf16[8,4,64,128]{3,2,1,0:T(8,128)(2,1)}), bf16[8,4,64,128]{3,2,1,0:T(8,128)(2,1)S(1)}, u32[]{:S(2)}, u32[]{:S(2)}) async-start(bf16[8,4,64,128]{3,2,1,0:T(8,128)(2,1)} %get-tuple-element.88), calls=%async_computation.4 | async-start | bytes 1048576 | tf_op jit(solution)/shard_map/all_to_all | solution.py:389
  125.8 1.9 %collective-permute-start.18 = (bf16[8,192,128]{2,1,0:T(8,128)(2,1)}, bf16[8,192,128]{2,1,0:T(8,128)(2,1)S(1)}, u32[]{:S(2)}, u32[]{:S(2)}) collective-permute-start(bf16[8,192,128]{2,1,0:T(8,128)(2,1)} %get-tuple-element.85), channel_id=1, source_target_pairs={{0,24},{8,0},{16,8},{24,16},{1,25},{9,1},{17,9},{25,17},{2,26},{10... | collective-permute-start | bytes 1179656 | tf_op jit(solution)/shard_map/ppermute | solution.py:381
  127.7 1.0 collective-permute-start.19
  128.7 0.1 collective-permute-start.20
  128.8 12.3 %collective-permute-done.18.a1 = bf16[8,192,128]{2,1,0:T(8,128)(2,1)S(1)} collective-permute-done((bf16[8,192,128]{2,1,0:T(8,128)(2,1)}, bf16[8,192,128]{2,1,0:T(8,128)(2,1)S(1)}, u32[]{:S(2)}, u32[]{:S(2)}) %collective-permute-start.18) | collective-permute-done | bytes 393248 | tf_op jit(solution)/shard_map/ppermute | solution.py:381
  141.2 3.6 %collective-permute-done.20.a3 = bf16[8,192,128]{2,1,0:T(8,128)(2,1)S(1)} collective-permute-done((bf16[8,192,128]{2,1,0:T(8,128)(2,1)S(1)}, bf16[8,192,128]{2,1,0:T(8,128)(2,1)S(1)}, u32[]{:S(2)}, u32[]{:S(2)}) %collective-permute-start.20) | collective-permute-done | bytes 393248 | tf_op jit(solution)/shard_map/ppermute | solution.py:381
  144.7 0.9 shard_map.144
  145.7 6.8 %all-to-all-start.5 = ((bf16[8,192,128]{2,1,0:T(8,128)(2,1)}), bf16[8,192,128]{2,1,0:T(8,128)(2,1)S(1)}, u32[]{:S(2)}, u32[]{:S(2)}) async-start(bf16[8,192,128]{2,1,0:T(8,128)(2,1)} %get-tuple-element.89), calls=%async_computation.5 | async-start | bytes 786432 | tf_op jit(solution)/shard_map/all_to_all | solution.py:389
  152.4 1.3 collective-permute-start.17
  153.7 2.2 %collective-permute-start.21 = (bf16[64,128]{1,0:T(8,128)(2,1)S(1)}, bf16[64,128]{1,0:T(8,128)(2,1)S(1)}, u32[]{:S(2)}, u32[]{:S(2)}) collective-permute-start(bf16[64,128]{1,0:T(8,128)(2,1)S(1)} %get-tuple-element.91), channel_id=1, source_target_pairs={{0,24},{8,0},{16,8},{24,16},{1,25},{9,1},{17,9},{25,17},{2,26},{10... | collective-permute-start | bytes 49160 | tf_op jit(solution)/shard_map/ppermute | solution.py:381
  156.0 2.6 %collective-permute-start.22 = (bf16[64,128]{1,0:T(8,128)(2,1)S(1)}, bf16[64,128]{1,0:T(8,128)(2,1)S(1)}, u32[]{:S(2)}, u32[]{:S(2)}) collective-permute-start(bf16[64,128]{1,0:T(8,128)(2,1)S(1)} %get-tuple-element.92), channel_id=1, source_target_pairs={{0,16},{8,24},{16,0},{24,8},{1,17},{9,25},{17,1},{25,9},{2,18},{10... | collective-permute-start | bytes 49160 | tf_op jit(solution)/shard_map/ppermute | solution.py:381
  158.5 0.5 slice.3
  159.1 2.1 %collective-permute-done.22.l2 = bf16[64,128]{1,0:T(8,128)(2,1)S(1)} collective-permute-done((bf16[64,128]{1,0:T(8,128)(2,1)S(1)}, bf16[64,128]{1,0:T(8,128)(2,1)S(1)}, u32[]{:S(2)}, u32[]{:S(2)}) %collective-permute-start.22) | collective-permute-done | bytes 16416 | tf_op jit(solution)/shard_map/ppermute | solution.py:381
  161.2 2.3 %collective-permute-done.23.l3 = bf16[64,128]{1,0:T(8,128)(2,1)S(1)} collective-permute-done((bf16[64,128]{1,0:T(8,128)(2,1)S(1)}, bf16[64,128]{1,0:T(8,128)(2,1)S(1)}, u32[]{:S(2)}, u32[]{:S(2)}) %collective-permute-start.23) | collective-permute-done | bytes 16416 | tf_op jit(solution)/shard_map/ppermute | solution.py:381
  163.5 2.5 %all-to-all-done.5.top = bf16[8,192,128]{2,1,0:T(8,128)(2,1)S(1)} async-done(((bf16[8,192,128]{2,1,0:T(8,128)(2,1)}), bf16[8,192,128]{2,1,0:T(8,128)(2,1)S(1)}, u32[]{:S(2)}, u32[]{:S(2)}) %all-to-all-start.5) | async-done | bytes 393248 | tf_op jit(solution)/shard_map/all_to_all | solution.py:389
  166.0 1.4 shard_map.146
  (28 shorter events, 0.1 us)
Async XLA Ops:
  0.6 52.6 %copy-start.5 = (bf16[1,512,128]{2,1,0:T(8,128)(2,1)S(1)}, bf16[1,512,128]{2,1,0:T(8,128)(2,1)}, u32[]{:S(2)}) copy-start(bf16[1,512,128]{2,1,0:T(8,128)(2,1)} %param.10) | copy-start | bytes 393220
  0.6 52.6 %copy-start.4 = (bf16[1,512,128]{2,1,0:T(8,128)(2,1)S(1)}, bf16[1,512,128]{2,1,0:T(8,128)(2,1)}, u32[]{:S(2)}) copy-start(bf16[1,512,128]{2,1,0:T(8,128)(2,1)} %param.9) | copy-start | bytes 393220
  0.7 52.6 %copy-start.1 = (bf16[1,512,128]{2,1,0:T(8,128)(2,1)S(1)}, bf16[1,512,128]{2,1,0:T(8,128)(2,1)}, u32[]{:S(2)}) copy-start(bf16[1,512,128]{2,1,0:T(8,128)(2,1)} %param.12) | copy-start | bytes 393220
  0.7 52.6 %copy-start.3 = (bf16[1,512,128]{2,1,0:T(8,128)(2,1)S(1)}, bf16[1,512,128]{2,1,0:T(8,128)(2,1)}, u32[]{:S(2)}) copy-start(bf16[1,512,128]{2,1,0:T(8,128)(2,1)} %param.8) | copy-start | bytes 393220
  0.8 0.8 copy-start.6
  1.6 37.2 %copy-start.7 = (s32[128,20]{0,1:T(8,128)S(1)}, s32[128,20]{0,1:T(8,128)}, u32[]{:S(2)}) copy-start(s32[128,20]{0,1:T(8,128)} %param.15) | copy-start | bytes 30724
  3.9 23.2 %all-to-all-start = ((bf16[8,192,128]{2,1,0:T(8,128)(2,1)}), bf16[8,192,128]{2,1,0:T(8,128)(2,1)S(1)}, u32[]{:S(2)}, u32[]{:S(2)}) async-start(bf16[8,192,128]{2,1,0:T(8,128)(2,1)} %get-tuple-element.54), calls=%async_computation | async-start | bytes 786432 | tf_op jit(solution)/shard_map/all_to_all | solution.py:389
  12.4 4.4 %collective-permute-start.2 = (bf16[64,128]{1,0:T(8,128)(2,1)S(1)}, bf16[64,128]{1,0:T(8,128)(2,1)S(1)}, u32[]{:S(2)}, u32[]{:S(2)}) collective-permute-start(bf16[64,128]{1,0:T(8,128)(2,1)S(1)} %get-tuple-element.55.l0), channel_id=1, source_target_pairs={{0,24},{8,0},{16,8},{24,16},{1,25},{9,1},{17,9},{25,17},{2,26},{10... | collective-permute-start | bytes 49160 | tf_op jit(solution)/shard_map/ppermute | solution.py:381
  15.2 5.2 %collective-permute-start.1 = (bf16[64,128]{1,0:T(8,128)(2,1)S(1)}, bf16[64,128]{1,0:T(8,128)(2,1)S(1)}, u32[]{:S(2)}, u32[]{:S(2)}) collective-permute-start(bf16[64,128]{1,0:T(8,128)(2,1)S(1)} %get-tuple-element.55.l0), channel_id=1, source_target_pairs={{0,16},{8,24},{16,0},{24,8},{1,17},{9,25},{17,1},{25,9},{2,18},{10... | collective-permute-start | bytes 49160 | tf_op jit(solution)/shard_map/ppermute | solution.py:381
  16.0 4.9 %collective-permute-start = (bf16[64,128]{1,0:T(8,128)(2,1)S(1)}, bf16[64,128]{1,0:T(8,128)(2,1)S(1)}, u32[]{:S(2)}, u32[]{:S(2)}) collective-permute-start(bf16[64,128]{1,0:T(8,128)(2,1)S(1)} %get-tuple-element.55.l0), channel_id=1, source_target_pairs={{0,8},{8,16},{16,24},{24,0},{1,9},{9,17},{17,25},{25,1},{2,10},{10... | collective-permute-start | bytes 49160 | tf_op jit(solution)/shard_map/ppermute | solution.py:381
  21.8 61.9 %copy-start = (bf16[1,512,128]{2,1,0:T(8,128)(2,1)S(1)}, bf16[1,512,128]{2,1,0:T(8,128)(2,1)}, u32[]{:S(2)}) copy-start(bf16[1,512,128]{2,1,0:T(8,128)(2,1)} %param.11) | copy-start | bytes 393220
  21.8 61.9 %copy-start.2 = (bf16[1,512,128]{2,1,0:T(8,128)(2,1)S(1)}, bf16[1,512,128]{2,1,0:T(8,128)(2,1)}, u32[]{:S(2)}) copy-start(bf16[1,512,128]{2,1,0:T(8,128)(2,1)} %param.14) | copy-start | bytes 393220
  21.8 61.8 %copy-start.8 = (f32[1,128]{1,0:T(1,128)S(1)}, f32[1,128]{1,0:T(1,128)}, u32[]{:S(2)}) copy-start(f32[1,128]{1,0:T(1,128)} %gain.5) | copy-start | bytes 1540
  27.1 26.1 %all-to-all-start.1 = ((bf16[8,4,64,128]{3,2,1,0:T(8,128)(2,1)}), bf16[8,4,64,128]{3,2,1,0:T(8,128)(2,1)S(1)}, u32[]{:S(2)}, u32[]{:S(2)}) async-start(bf16[8,4,64,128]{3,2,1,0:T(8,128)(2,1)} %shard_map.136), calls=%async_computation.1 | async-start | bytes 1048576 | tf_op jit(solution)/shard_map/all_to_all | solution.py:389
  30.6 20.9 %collective-permute-start.5 = (bf16[8,192,128]{2,1,0:T(8,128)(2,1)S(1)}, bf16[8,192,128]{2,1,0:T(8,128)(2,1)S(1)}, u32[]{:S(2)}, u32[]{:S(2)}) collective-permute-start(bf16[8,192,128]{2,1,0:T(8,128)(2,1)S(1)} %all-to-all-done.f0), channel_id=1, source_target_pairs={{0,24},{8,0},{16,8},{24,16},{1,25},{9,1},{17,9},{25,17},{2,26},{10... | collective-permute-start | bytes 1179656 | tf_op jit(solution)/shard_map/ppermute | solution.py:381
  33.4 18.1 %collective-permute-start.4 = (bf16[8,192,128]{2,1,0:T(8,128)(2,1)S(1)}, bf16[8,192,128]{2,1,0:T(8,128)(2,1)S(1)}, u32[]{:S(2)}, u32[]{:S(2)}) collective-permute-start(bf16[8,192,128]{2,1,0:T(8,128)(2,1)S(1)} %all-to-all-done.f0), channel_id=1, source_target_pairs={{0,16},{8,24},{16,0},{24,8},{1,17},{9,25},{17,1},{25,9},{2,18},{10... | collective-permute-start | bytes 1179656 | tf_op jit(solution)/shard_map/ppermute | solution.py:381
  34.2 19.0 %collective-permute-start.3 = (bf16[8,192,128]{2,1,0:T(8,128)(2,1)S(1)}, bf16[8,192,128]{2,1,0:T(8,128)(2,1)S(1)}, u32[]{:S(2)}, u32[]{:S(2)}) collective-permute-start(bf16[8,192,128]{2,1,0:T(8,128)(2,1)S(1)} %all-to-all-done.f0), channel_id=1, source_target_pairs={{0,8},{8,16},{16,24},{24,0},{1,9},{9,17},{17,25},{25,1},{2,10},{10... | collective-permute-start | bytes 1179656 | tf_op jit(solution)/shard_map/ppermute | solution.py:381
  35.1 16.4 %collective-permute-start.6 = (bf16[128,256]{1,0:T(8,128)(2,1)S(1)}, bf16[128,256]{1,0:T(8,128)(2,1)S(1)}, u32[]{:S(2)}, u32[]{:S(2)}) collective-permute-start(bf16[128,256]{1,0:T(8,128)(2,1)S(1)} %get-tuple-element.58), channel_id=1, source_target_pairs={{0,8},{8,16},{16,24},{24,32},{32,40},{40,48},{48,56},{56,64},{64,7... | collective-permute-start | bytes 196616 | tf_op jit(solution)/shard_map/ppermute | solution.py:421
  58.4 4.0 %collective-permute-start.9 = (bf16[128,128]{1,0:T(8,128)(2,1)S(1)}, bf16[128,128]{1,0:T(8,128)(2,1)S(1)}, u32[]{:S(2)}, u32[]{:S(2)}) collective-permute-start(bf16[128,128]{1,0:T(8,128)(2,1)S(1)} %get-tuple-element.60.x0), channel_id=1, source_target_pairs={{0,24},{8,0},{16,8},{24,16},{1,25},{9,1},{17,9},{25,17},{2,26},{10... | collective-permute-start | bytes 98312 | tf_op jit(solution)/shard_map/ppermute | solution.py:381
  60.5 5.4 %collective-permute-start.8 = (bf16[128,128]{1,0:T(8,128)(2,1)S(1)}, bf16[128,128]{1,0:T(8,128)(2,1)S(1)}, u32[]{:S(2)}, u32[]{:S(2)}) collective-permute-start(bf16[128,128]{1,0:T(8,128)(2,1)S(1)} %get-tuple-element.60.x0), channel_id=1, source_target_pairs={{0,16},{8,24},{16,0},{24,8},{1,17},{9,25},{17,1},{25,9},{2,18},{10... | collective-permute-start | bytes 98312 | tf_op jit(solution)/shard_map/ppermute | solution.py:381
  61.3 5.1 %collective-permute-start.7 = (bf16[128,128]{1,0:T(8,128)(2,1)S(1)}, bf16[128,128]{1,0:T(8,128)(2,1)S(1)}, u32[]{:S(2)}, u32[]{:S(2)}) collective-permute-start(bf16[128,128]{1,0:T(8,128)(2,1)S(1)} %get-tuple-element.60.x0), channel_id=1, source_target_pairs={{0,8},{8,16},{16,24},{24,0},{1,9},{9,17},{17,25},{25,1},{2,10},{10... | collective-permute-start | bytes 98312 | tf_op jit(solution)/shard_map/ppermute | solution.py:381
  85.1 1.2 collective-permute-start.10
  86.3 4.9 %collective-permute-start.13 = (f32[8,128]{1,0:T(8,128)S(1)}, f32[8,128]{1,0:T(8,128)S(1)}, u32[]{:S(2)}, u32[]{:S(2)}) collective-permute-start(f32[8,128]{1,0:T(8,128)S(1)} %add.11.s0), channel_id=1, source_target_pairs={{0,6},{2,0},{4,2},{6,4},{1,7},{3,1},{5,3},{7,5},{8,14},{10,8},{12,... | collective-permute-start | bytes 12296 | tf_op jit(solution)/shard_map/ppermute | solution.py:381
  86.8 5.1 %collective-permute-start.12 = (f32[8,128]{1,0:T(8,128)S(1)}, f32[8,128]{1,0:T(8,128)S(1)}, u32[]{:S(2)}, u32[]{:S(2)}) collective-permute-start(f32[8,128]{1,0:T(8,128)S(1)} %add.11.s0), channel_id=1, source_target_pairs={{0,4},{2,6},{4,0},{6,2},{1,5},{3,7},{5,1},{7,3},{8,12},{10,14},{12... | collective-permute-start | bytes 12296 | tf_op jit(solution)/shard_map/ppermute | solution.py:381
  89.4 3.6 %collective-permute-start.11 = (f32[8,128]{1,0:T(8,128)S(1)}, f32[8,128]{1,0:T(8,128)S(1)}, u32[]{:S(2)}, u32[]{:S(2)}) collective-permute-start(f32[8,128]{1,0:T(8,128)S(1)} %add.11.s0), channel_id=1, source_target_pairs={{0,2},{2,4},{4,6},{6,0},{1,3},{3,5},{5,7},{7,1},{8,10},{10,12},{12... | collective-permute-start | bytes 12296 | tf_op jit(solution)/shard_map/ppermute | solution.py:381
  93.4 5.6 %collective-permute-start.16 = (bf16[144,128]{1,0:T(8,128)(2,1)S(1)}, bf16[144,128]{1,0:T(8,128)(2,1)S(1)}, u32[]{:S(2)}, u32[]{:S(2)}) collective-permute-start(bf16[144,128]{1,0:T(8,128)(2,1)S(1)} %get-tuple-element.76.x0), channel_id=1, source_target_pairs={{0,8},{8,16},{16,24},{24,0},{1,9},{9,17},{17,25},{25,1},{2,10},{10... | collective-permute-start | bytes 110600 | tf_op jit(solution)/shard_map/ppermute | solution.py:381
  94.5 5.5 %collective-permute-start.15 = (bf16[144,128]{1,0:T(8,128)(2,1)S(1)}, bf16[144,128]{1,0:T(8,128)(2,1)S(1)}, u32[]{:S(2)}, u32[]{:S(2)}) collective-permute-start(bf16[144,128]{1,0:T(8,128)(2,1)S(1)} %get-tuple-element.76.x0), channel_id=1, source_target_pairs={{0,16},{8,24},{16,0},{24,8},{1,17},{9,25},{17,1},{25,9},{2,18},{10... | collective-permute-start | bytes 110600 | tf_op jit(solution)/shard_map/ppermute | solution.py:381
  97.0 4.0 %collective-permute-start.14 = (bf16[144,128]{1,0:T(8,128)(2,1)S(1)}, bf16[144,128]{1,0:T(8,128)(2,1)S(1)}, u32[]{:S(2)}, u32[]{:S(2)}) collective-permute-start(bf16[144,128]{1,0:T(8,128)(2,1)S(1)} %get-tuple-element.76.x0), channel_id=1, source_target_pairs={{0,24},{8,0},{16,8},{24,16},{1,25},{9,1},{17,9},{25,17},{2,26},{10... | collective-permute-start | bytes 110600 | tf_op jit(solution)/shard_map/ppermute | solution.py:381
  122.3 22.4 %all-to-all-start.4 = ((bf16[8,4,64,128]{3,2,1,0:T(8,128)(2,1)}), bf16[8,4,64,128]{3,2,1,0:T(8,128)(2,1)S(1)}, u32[]{:S(2)}, u32[]{:S(2)}) async-start(bf16[8,4,64,128]{3,2,1,0:T(8,128)(2,1)} %get-tuple-element.88), calls=%async_computation.4 | async-start | bytes 1048576 | tf_op jit(solution)/shard_map/all_to_all | solution.py:389
  125.8 15.4 %collective-permute-start.18 = (bf16[8,192,128]{2,1,0:T(8,128)(2,1)}, bf16[8,192,128]{2,1,0:T(8,128)(2,1)S(1)}, u32[]{:S(2)}, u32[]{:S(2)}) collective-permute-start(bf16[8,192,128]{2,1,0:T(8,128)(2,1)} %get-tuple-element.85), channel_id=1, source_target_pairs={{0,24},{8,0},{16,8},{24,16},{1,25},{9,1},{17,9},{25,17},{2,26},{10... | collective-permute-start | bytes 1179656 | tf_op jit(solution)/shard_map/ppermute | solution.py:381
  127.7 13.4 %collective-permute-start.19 = (bf16[8,192,128]{2,1,0:T(8,128)(2,1)}, bf16[8,192,128]{2,1,0:T(8,128)(2,1)S(1)}, u32[]{:S(2)}, u32[]{:S(2)}) collective-permute-start(bf16[8,192,128]{2,1,0:T(8,128)(2,1)} %get-tuple-element.86), channel_id=1, source_target_pairs={{0,16},{8,24},{16,0},{24,8},{1,17},{9,25},{17,1},{25,9},{2,18},{10... | collective-permute-start | bytes 1179656 | tf_op jit(solution)/shard_map/ppermute | solution.py:381
  128.7 16.0 %collective-permute-start.20 = (bf16[8,192,128]{2,1,0:T(8,128)(2,1)S(1)}, bf16[8,192,128]{2,1,0:T(8,128)(2,1)S(1)}, u32[]{:S(2)}, u32[]{:S(2)}) collective-permute-start(bf16[8,192,128]{2,1,0:T(8,128)(2,1)S(1)} %get-tuple-element.87), channel_id=1, source_target_pairs={{0,8},{8,16},{16,24},{24,0},{1,9},{9,17},{17,25},{25,1},{2,10},{10... | collective-permute-start | bytes 1179656 | tf_op jit(solution)/shard_map/ppermute | solution.py:381
  145.7 20.3 %all-to-all-start.5 = ((bf16[8,192,128]{2,1,0:T(8,128)(2,1)}), bf16[8,192,128]{2,1,0:T(8,128)(2,1)S(1)}, u32[]{:S(2)}, u32[]{:S(2)}) async-start(bf16[8,192,128]{2,1,0:T(8,128)(2,1)} %get-tuple-element.89), calls=%async_computation.5 | async-start | bytes 786432 | tf_op jit(solution)/shard_map/all_to_all | solution.py:389
  152.4 6.6 %collective-permute-start.17 = (bf16[128,256]{1,0:T(8,128)(2,1)S(1)}, bf16[128,256]{1,0:T(8,128)(2,1)S(1)}, u32[]{:S(2)}, u32[]{:S(2)}) collective-permute-start(bf16[128,256]{1,0:T(8,128)(2,1)S(1)} %get-tuple-element.83), channel_id=1, source_target_pairs={{8,0},{16,8},{24,16},{32,24},{40,32},{48,40},{56,48},{64,56},{72,6... | collective-permute-start | bytes 196616 | tf_op jit(solution)/shard_map/ppermute | solution.py:491
  153.7 5.3 %collective-permute-start.21 = (bf16[64,128]{1,0:T(8,128)(2,1)S(1)}, bf16[64,128]{1,0:T(8,128)(2,1)S(1)}, u32[]{:S(2)}, u32[]{:S(2)}) collective-permute-start(bf16[64,128]{1,0:T(8,128)(2,1)S(1)} %get-tuple-element.91), channel_id=1, source_target_pairs={{0,24},{8,0},{16,8},{24,16},{1,25},{9,1},{17,9},{25,17},{2,26},{10... | collective-permute-start | bytes 49160 | tf_op jit(solution)/shard_map/ppermute | solution.py:381
  156.0 5.2 %collective-permute-start.22 = (bf16[64,128]{1,0:T(8,128)(2,1)S(1)}, bf16[64,128]{1,0:T(8,128)(2,1)S(1)}, u32[]{:S(2)}, u32[]{:S(2)}) collective-permute-start(bf16[64,128]{1,0:T(8,128)(2,1)S(1)} %get-tuple-element.92), channel_id=1, source_target_pairs={{0,16},{8,24},{16,0},{24,8},{1,17},{9,25},{17,1},{25,9},{2,18},{10... | collective-permute-start | bytes 49160 | tf_op jit(solution)/shard_map/ppermute | solution.py:381
  158.5 4.9 %collective-permute-start.23 = (bf16[64,128]{1,0:T(8,128)(2,1)S(1)}, bf16[64,128]{1,0:T(8,128)(2,1)S(1)}, u32[]{:S(2)}, u32[]{:S(2)}) collective-permute-start(bf16[64,128]{1,0:T(8,128)(2,1)S(1)} %get-tuple-element.93), channel_id=1, source_target_pairs={{0,8},{8,16},{16,24},{24,0},{1,9},{9,17},{17,25},{25,1},{2,10},{10... | collective-permute-start | bytes 49160 | tf_op jit(solution)/shard_map/ppermute | solution.py:381

commit v3 on v2

--- a/solution.py
+++ b/solution.py
@@ -72,19 +72,21 @@
     return jnp.max(jnp.where(hit, far - base, 0).astype(f32)).astype(jnp.int32)
 
 
-def pick_kernel(pos, names, k, v, top, low, last, block, sems):
-    mine = chosen_block(pos, names)
-    run_copies(
-        [
-            (k.at[mine], block.at[pl.ds(0, BLK)]),
-            (v.at[mine, pl.ds(0, HALF)], block.at[pl.ds(BLK, HALF)]),
-            (v.at[mine, pl.ds(HALF, HALF)], low),
-            (k.at[3], last.at[:, pl.ds(0, BLK)]),
-            (v.at[3], last.at[:, pl.ds(BLK, BLK)]),
-        ],
-        sems,
-    )
-    run_copies([(block, top.at[i]) for i in range(NZ)], sems)
+def pick_kernel(pos, names, k, v, top, low, last, table, keys, values, sems):
+    run_copies([(names, table), (k, keys), (v, values)], sems)
+    mine = chosen_block(pos, table)
+    pairs = []
+    for i in range(NZ):
+        pairs.append((keys.at[mine], top.at[i, pl.ds(0, BLK)]))
+        pairs.append((values.at[mine, pl.ds(0, HALF)], top.at[i, pl.ds(BLK, HALF)]))
+    copies = [pltpu.make_async_copy(a, b, sems.at[i]) for i, (a, b) in enumerate(pairs)]
+    for c in copies:
+        c.start()
+    low[...] = values[mine, HALF:, :]
+    last[:, 0:BLK] = keys[3]
+    last[:, BLK:] = values[3]
+    for c in copies:
+        c.wait()
 
 
 def place_of(pos, names, b, j):
@@ -179,8 +181,19 @@
     run_copies([(block, out.at[i]) for i in range(NZ)], sems)
 
 
-def linear_kernel(pos, lq, lk, att, gain, cot, x0, x1, x2, x3, zs, lin, prior, sums):
+def within_kernel(lq, lk, att, inner, local):
     lower = lower_mask()
+    run = jnp.zeros((BLK, BLK), f32)
+    for b in range(4):
+        r = slice(b * BLK, (b + 1) * BLK)
+        local[b] = run
+        mixing = jnp.where(lower, mm(lq[r], lk[r], NT), 0.0).astype(bf16)
+        inner[r] = mm(mixing, att[r])
+        if b < 3:
+            run = run + mm(lk[r], att[r], TN)
+
+
+def linear_kernel(pos, lq, inner, local, gain, cot, x0, x1, x2, x3, zs, lin, prior, sums):
     run = jnp.zeros((BLK, BLK), f32)
     for j, r in enumerate((x1, x2, x3)):
         run = run + jnp.where(pos[1] > j, r[...].astype(f32), 0.0)
@@ -189,13 +202,10 @@
     sums[...] = jnp.zeros((8, BLK), f32)
     for b in range(4):
         r = slice(b * BLK, (b + 1) * BLK)
-        before = run.astype(bf16)
+        before = (run + local[b]).astype(bf16)
         prior[b] = before
-        mixing = jnp.where(lower, mm(lq[r], lk[r], NT), 0.0).astype(bf16)
-        out = mm(mixing, att[r]) + mm(lq[r], before)
+        out = inner[r] + mm(lq[r], before)
         lin[r] = out
-        if b < 3:
-            run = run + mm(lk[r], att[r], TN)
         scaled = cot[r].astype(f32) * gain[...]
         sums[b : b + 1] = as_row(jnp.sum(out * out, axis=1, keepdims=True))
         sums[4 + b : 5 + b] = as_row(jnp.sum(out * scaled, axis=1, keepdims=True))
@@ -246,7 +256,7 @@
         out[i, BLK + 8 :] = rest
 
 
-def side_kernel(inv, lin, gain, att, glin, lk, lq, prior, mixed, dlq, pairs_t, mix_t):
+def side_kernel(inv, lin, gain, att, glin, lk, lq, prior, cot, mixed, dlq, dlk_in, gatt_in):
     lower = lower_mask()
     upper = lax.broadcasted_iota(jnp.int32, (BLK, BLK), 0) <= lax.broadcasted_iota(
         jnp.int32, (BLK, BLK), 1
@@ -257,11 +267,13 @@
         mixed[r] = (att[r].astype(f32) + gain[...] * normed).astype(bf16)
         pairs = jnp.where(lower, mm(glin[r], att[r], NT), 0.0).astype(bf16)
         dlq[r] = (mm(pairs, lk[r]) + mm(glin[r], prior[b], NT)).astype(bf16)
-        pairs_t[b] = jnp.where(upper, mm(att[r], glin[r], NT), 0.0).astype(bf16)
-        mix_t[b] = jnp.where(upper, mm(lk[r], lq[r], NT), 0.0).astype(bf16)
-
-
-def backward_kernel(pos, names, q, lse, att, cot, lq, lk, glin, pairs_t, mix_t, local,
+        pairs_t = jnp.where(upper, mm(att[r], glin[r], NT), 0.0).astype(bf16)
+        mix_t = jnp.where(upper, mm(lk[r], lq[r], NT), 0.0).astype(bf16)
+        dlk_in[r] = mm(pairs_t, lq[r])
+        gatt_in[r] = cot[r].astype(f32) + mm(mix_t, glin[r])
+
+
+def backward_kernel(pos, names, q, lse, att, lk, dlk_in, gatt_in, local,
                     x0, x1, x2, x3, zs, pool,
                     dlk, dq, o0, o1, o2, o3, olow, own, back, ggain,
                     acc, gatt, delta, near, lows, sems):
@@ -278,9 +290,8 @@
     for b in range(4):
         r = slice(b * BLK, (b + 1) * BLK)
         after = (later + local[b]).astype(bf16)
-        dlk[r] = (mm(pairs_t[b], lq[r]) + mm(att[r], after, NT)).astype(bf16)
-        g = cot[r].astype(f32) + mm(mix_t[b], glin[r]) + mm(lk[r], after)
-        g = g.astype(bf16)
+        dlk[r] = (dlk_in[r] + mm(att[r], after, NT)).astype(bf16)
+        g = (gatt_in[r] + mm(lk[r], after)).astype(bf16)
         gatt[r] = g
         delta[b : b + 1] = as_row(
             jnp.sum(g.astype(f32) * att[r].astype(f32), axis=1, keepdims=True)
@@ -349,14 +360,17 @@
         o[...] = part.astype(bf16)
 
 
-def round_kernel(own, gk, gv):
+def round_kernel(pos, names, own, gk, gv, rest):
+    mine = chosen_block(pos, names)
     for b in range(4):
         r = slice(b * BLK, (b + 1) * BLK)
         gk[r] = own[b, :, 0:BLK].astype(bf16)
         gv[r] = own[b, :, BLK:].astype(bf16)
-
-
-def finish_kernel(pos, names, own, back, top, l0, l1, l2, l3, gk_in, gv_in, gk, gv):
+    rest[0] = own[mine]
+    rest[1] = own[3]
+
+
+def finish_kernel(pos, names, rest, back, top, l0, l1, l2, l3, gk_in, gv_in, gk, gv):
     mine = chosen_block(pos, names)
     total = top[0].astype(f32)
     for i in range(1, NZ):
@@ -366,15 +380,15 @@
     gk[...] = gk_in[...]
     gv[...] = gv_in[...]
     last = mine == 3
-    dk = own[3, :, 0:BLK] + back[:, 0:BLK].astype(f32)
-    dv = own[3, :, BLK:] + back[:, BLK:].astype(f32)
+    dk = rest[1, :, 0:BLK] + back[:, 0:BLK].astype(f32)
+    dv = rest[1, :, BLK:] + back[:, BLK:].astype(f32)
     gk[rows(3), :] = (dk + jnp.where(last, far_key, 0.0)).astype(bf16)
     gv[rows(3), :] = (dv + jnp.where(last, far_value, 0.0)).astype(bf16)
 
     @pl.when(mine < 3)
     def _():
-        gk[rows(mine), :] = (own[mine, :, 0:BLK] + far_key).astype(bf16)
-        gv[rows(mine), :] = (own[mine, :, BLK:] + far_value).astype(bf16)
+        gk[rows(mine), :] = (rest[0, :, 0:BLK] + far_key).astype(bf16)
+        gv[rows(mine), :] = (rest[0, :, BLK:] + far_value).astype(bf16)
 
 
 def turn(value, axis, size, by):
@@ -413,9 +427,14 @@
     tops, low, last = call(
         pick_kernel,
         [((NZ, TOP, width), bf16), ((HALF, width), bf16), ((BLK, 2 * BLK), bf16)],
-        (pos, key_block, in_hbm(k4), in_hbm(v4)),
-        [SM, VM, HB, HB],
-        [pltpu.VMEM((TOP, width), bf16), pltpu.SemaphoreType.DMA((NZ,))],
+        (pos, in_hbm(key_block), in_hbm(k4), in_hbm(v4)),
+        [SM, HB, HB, HB],
+        [
+            pltpu.VMEM(key_block.shape, jnp.int32),
+            pltpu.VMEM((4, BLK, width), bf16),
+            pltpu.VMEM((4, BLK, width), bf16),
+            pltpu.SemaphoreType.DMA((2 * NZ,)),
+        ],
         [HB, VM, VM],
     )
     prev = lax.ppermute(last, seq, [(i, i + 1) for i in range(NZ * NX - 1)])
@@ -443,11 +462,18 @@
     )
 
     xs = [state] + [turn(state, "x", NX, j) for j in range(1, NX)]
+    inner, local = call(
+        within_kernel,
+        [((512, width), f32), ((4, BLK, width), f32)],
+        (lq, lk, att),
+        [VM] * 3,
+    )
+    *xs, inner, local = lax.optimization_barrier((*xs, inner, local))
     (wide,) = call(row_kernel, [((NZ, BLK, width), bf16)], xs, [VM] * 4)
     lin, prior, sums = call(
         linear_kernel,
         [((512, width), f32), ((4, BLK, width), bf16), ((8, BLK), f32)],
-        (pos, lq, lk, att, gain, cot, *xs, swap(wide)),
+        (pos, lq, inner, local, gain, cot, *xs, swap(wide)),
         [SM] + [VM] * 10,
     )
     sums = sums + turn(sums, "c", NC, 1)
@@ -459,13 +485,13 @@
         [VM] * 8,
     )
     ex = [send] + [turn(send, "x", NX, -j) for j in range(1, NX)]
-    mixed, dlq, pairs_t, mix_t = call(
+    mixed, dlq, dlk_in, gatt_in = call(
         side_kernel,
-        [((512, width), bf16), ((512, width), bf16), ((4, BLK, BLK), bf16), ((4, BLK, BLK), bf16)],
-        (inv, lin, gain, att, glin, lk, lq, prior),
-        [VM] * 8,
-    )
-    *ex, mixed, dlq, pairs_t, mix_t = lax.optimization_barrier((*ex, mixed, dlq, pairs_t, mix_t))
+        [((512, width), bf16), ((512, width), bf16), ((512, width), f32), ((512, width), f32)],
+        (inv, lin, gain, att, glin, lk, lq, prior, cot),
+        [VM] * 9,
+    )
+    *ex, mixed, dlq, dlk_in, gatt_in = lax.optimization_barrier((*ex, mixed, dlq, dlk_in, gatt_in))
     (wide,) = call(sent_kernel, [((NZ, SENT, width), bf16)], ex, [VM] * 4)
     outs = call(
         backward_kernel,
@@ -473,8 +499,8 @@
         + [((NZ, TOP, width), bf16)] * 4
         + [((NZ, NX, HALF, width), bf16), ((4, BLK, 2 * BLK), f32)]
         + [((BLK, 2 * BLK), bf16), ((8, BLK), f32)],
-        (pos, names, q, lse, att, cot, lq, lk, glin, pairs_t, mix_t, local, *ex, swap(wide), pool),
-        [SM, SM] + [VM] * 16,
+        (pos, names, q, lse, att, lk, dlk_in, gatt_in, local, *ex, swap(wide), pool),
+        [SM, SM] + [VM] * 13,
         [
             pltpu.VMEM((POOL, BLK, 2 * BLK), f32),
             pltpu.VMEM((512, width), bf16),
@@ -497,11 +523,16 @@
         [VM] * 5,
     )
     ends = [folded[1]] + turns(folded[2:], -1)
-    gk, gv = call(round_kernel, [((512, width), bf16)] * 2, (own,), [VM])
+    gk, gv, rest = call(
+        round_kernel,
+        [((512, width), bf16)] * 2 + [((2, BLK, 2 * BLK), f32)],
+        (pos, key_block, own),
+        [SM, VM, VM],
+    )
     gk, gv = call(
         finish_kernel,
         [((512, width), bf16), ((512, width), bf16)],
-        (pos, key_block, own, back, swap(folded[0]), *ends, gk, gv),
+        (pos, key_block, rest, back, swap(folded[0]), *ends, gk, gv),
         [SM] + [VM] * 10,
     )
     lead = lambda a: a[None]

time: 169 us -> 168 us (level)
    pallas_call x12 -> x13, Pallas kernels: 22 us -> 23.2 us  [call(): pl.pallas_call(body, out_shape=[jax.ShapeDtypeStruct(s, d) for s, d in ou...]
  transfers between devices with their start and end apart: 28 -> 28, of which waited for: 18 -> 17; matrix products, arithmetic and copies ran while one was open for 0% -> 0% of each run, Pallas kernels for 1% -> 2%
where the time goes in v3:
time: 168 us; the launch traced here: 167 us
  starting transfers between devices  57.1 us (34%)
  waiting for transfers between devices  54.3 us (32%)
  blocking collectives  30.4 us (18%)
  Pallas kernels  23.2 us (14%)
    ppermute x22, waiting for transfers between devices, turn(): lax.ppermute(value, axis, [(i, (i + by) % size) for i in range(size)])  33.9 us
    all_to_all x2, blocking collectives, swap(): return lax.all_to_all(value, 'z', 0, 0, tiled=True)  30.4 us
    ppermute x22, starting transfers between devices, turn(): lax.ppermute(value, axis, [(i, (i + by) % size) for i in range(size)])  29.7 us
    pallas_call x13, Pallas kernels, call(): pl.pallas_call(body, out_shape=[jax.ShapeDtypeStruct(s, d) for s, d in ou...  23.2 us
    all_to_all x4, starting transfers between devices, swap(): return lax.all_to_all(value, 'z', 0, 0, tiled=True)  22.4 us
    ppermute x1, waiting for transfers between devices, per_device(): prev = lax.ppermute(last, seq, [(i, i + 1) for i in range(NZ * NX - 1)])  12.6 us
    all_to_all x4, waiting for transfers between devices, swap(): return lax.all_to_all(value, 'z', 0, 0, tiled=True)  7.79 us
    ppermute x1, starting transfers between devices, per_device(): prev = lax.ppermute(last, seq, [(i, i + 1) for i in range(NZ * NX - 1)])  3.7 us
  transfers between devices with their start and end apart: 28, of which 17 were waited for; matrix products, arithmetic and copies ran while one was open for 0% of the time, Pallas kernels for 2%

profile of v3, /device:TPU:8, one launch (start us, length us, event | category | flops | bytes accessed | tf_op | source)
XLA Modules:
  0.0 166.5 jit_solution(17649128137293215414)
XLA Ops:
  0.6 0.0 copy-start.6
  0.6 0.0 copy-start.5
  0.7 0.0 copy-start.4
  0.7 0.1 pad_add_fusion.pos
  0.8 2.6 %shard_map.135 = (bf16[8,192,128]{2,1,0:T(8,128)(2,1)}, bf16[64,128]{1,0:T(8,128)(2,1)S(1)}, bf16[128,256]{1,0:T(8,128)(2,1)S(1)}) custom-call(s32[2]{0:T(128)S(1)} %pad_add_fusion.pos, s32[20,128]{1,0:T(8,128)} %bitcast.34, bf16[4,128,128]{2,1,0:T(8,128)(2,1)} %bitcast.30, bf16[4,128,128]{2,1,0:T(8,128)(2,1)} %bitcast.32), custom_call_target="tpu_custom_call" | custom-call | tf_op jit(solution)/shard_map/pallas_call | solution.py:39
  3.3 0.0 copy-start.1
  3.4 8.6 %all-to-all-start = ((bf16[8,192,128]{2,1,0:T(8,128)(2,1)}), bf16[8,192,128]{2,1,0:T(8,128)(2,1)S(1)}, u32[]{:S(2)}, u32[]{:S(2)}) async-start(bf16[8,192,128]{2,1,0:T(8,128)(2,1)} %get-tuple-element.63), calls=%async_computation | async-start | bytes 786432 | tf_op jit(solution)/shard_map/all_to_all | solution.py:403
  12.0 2.8 %collective-permute-start.2 = (bf16[64,128]{1,0:T(8,128)(2,1)S(1)}, bf16[64,128]{1,0:T(8,128)(2,1)S(1)}, u32[]{:S(2)}, u32[]{:S(2)}) collective-permute-start(bf16[64,128]{1,0:T(8,128)(2,1)S(1)} %get-tuple-element.64.l0), channel_id=1, source_target_pairs={{0,24},{8,0},{16,8},{24,16},{1,25},{9,1},{17,9},{25,17},{2,26},{10... | collective-permute-start | bytes 49160 | tf_op jit(solution)/shard_map/ppermute | solution.py:395
  14.7 0.8 collective-permute-start.1
  15.5 0.9 collective-permute-start
  16.4 3.6 %collective-permute-done.1.l2 = bf16[64,128]{1,0:T(8,128)(2,1)S(1)} collective-permute-done((bf16[64,128]{1,0:T(8,128)(2,1)S(1)}, bf16[64,128]{1,0:T(8,128)(2,1)S(1)}, u32[]{:S(2)}, u32[]{:S(2)}) %collective-permute-start.1) | collective-permute-done | bytes 16416 | tf_op jit(solution)/shard_map/ppermute | solution.py:395
  20.0 0.5 collective-permute-done.l1
  20.5 0.9 shard_map.136
  21.4 5.3 %all-to-all-done.f0 = bf16[8,192,128]{2,1,0:T(8,128)(2,1)S(1)} async-done(((bf16[8,192,128]{2,1,0:T(8,128)(2,1)}), bf16[8,192,128]{2,1,0:T(8,128)(2,1)S(1)}, u32[]{:S(2)}, u32[]{:S(2)}) %all-to-all-start) | async-done | bytes 393248 | tf_op jit(solution)/shard_map/all_to_all | solution.py:403
  26.6 3.5 %all-to-all-start.1 = ((bf16[8,4,64,128]{3,2,1,0:T(8,128)(2,1)}), bf16[8,4,64,128]{3,2,1,0:T(8,128)(2,1)S(1)}, u32[]{:S(2)}, u32[]{:S(2)}) async-start(bf16[8,4,64,128]{3,2,1,0:T(8,128)(2,1)} %shard_map.136), calls=%async_computation.1 | async-start | bytes 1048576 | tf_op jit(solution)/shard_map/all_to_all | solution.py:403
  30.1 2.8 %collective-permute-start.5 = (bf16[8,192,128]{2,1,0:T(8,128)(2,1)S(1)}, bf16[8,192,128]{2,1,0:T(8,128)(2,1)S(1)}, u32[]{:S(2)}, u32[]{:S(2)}) collective-permute-start(bf16[8,192,128]{2,1,0:T(8,128)(2,1)S(1)} %all-to-all-done.f0), channel_id=1, source_target_pairs={{0,24},{8,0},{16,8},{24,16},{1,25},{9,1},{17,9},{25,17},{2,26},{10... | collective-permute-start | bytes 1179656 | tf_op jit(solution)/shard_map/ppermute | solution.py:395
  33.0 0.8 collective-permute-start.4
  33.8 0.9 collective-permute-start.3
  34.7 3.7 %collective-permute-start.6 = (bf16[128,256]{1,0:T(8,128)(2,1)S(1)}, bf16[128,256]{1,0:T(8,128)(2,1)S(1)}, u32[]{:S(2)}, u32[]{:S(2)}) collective-permute-start(bf16[128,256]{1,0:T(8,128)(2,1)S(1)} %get-tuple-element.67), channel_id=1, source_target_pairs={{0,8},{8,16},{16,24},{24,32},{32,40},{40,48},{48,56},{56,64},{64,7... | collective-permute-start | bytes 196616 | tf_op jit(solution)/shard_map/ppermute | solution.py:440
  38.4 0.1 dynamic-slice_bitcast_fusion.names
  38.5 12.6 %collective-permute-done.6.prev = bf16[128,256]{1,0:T(8,128)(2,1)S(1)} collective-permute-done((bf16[128,256]{1,0:T(8,128)(2,1)S(1)}, bf16[128,256]{1,0:T(8,128)(2,1)S(1)}, u32[]{:S(2)}, u32[]{:S(2)}) %collective-permute-start.6) | collective-permute-done | bytes 65568 | tf_op jit(solution)/shard_map/ppermute | solution.py:440
  51.1 1.7 %collective-permute-done.3.f1 = bf16[8,192,128]{2,1,0:T(8,128)(2,1)S(1)} collective-permute-done((bf16[8,192,128]{2,1,0:T(8,128)(2,1)S(1)}, bf16[8,192,128]{2,1,0:T(8,128)(2,1)S(1)}, u32[]{:S(2)}, u32[]{:S(2)}) %collective-permute-start.3) | collective-permute-done | bytes 393248 | tf_op jit(solution)/shard_map/ppermute | solution.py:395
  52.8 5.1 %shard_map.137 = (bf16[512,128]{1,0:T(8,128)(2,1)S(1)}, f32[8,128]{1,0:T(8,128)S(1)}, bf16[128,128]{1,0:T(8,128)(2,1)S(1)}, bf16[37,128,256]{2,1,0:T(8,128)(2,1)S(1)}) custom-call(s32[2]{0:T(128)S(1)} %pad_add_fusion.pos, s32[20,4]{1,0:T(8,128)S(1)} %dynamic-slice_bitcast_fusion.names, bf16[512,128]{1,0:T(8,128)(2,1)S(1)} %bitcast.28, ...), custom_call_target="tpu_custom_call" | custom-call | tf_op jit(solution)/shard_map/pallas_call | solution.py:39
  57.9 2.1 %collective-permute-start.9 = (bf16[128,128]{1,0:T(8,128)(2,1)S(1)}, bf16[128,128]{1,0:T(8,128)(2,1)S(1)}, u32[]{:S(2)}, u32[]{:S(2)}) collective-permute-start(bf16[128,128]{1,0:T(8,128)(2,1)S(1)} %get-tuple-element.74.x0), channel_id=1, source_target_pairs={{0,24},{8,0},{16,8},{24,16},{1,25},{9,1},{17,9},{25,17},{2,26},{10... | collective-permute-start | bytes 98312 | tf_op jit(solution)/shard_map/ppermute | solution.py:395
  60.0 0.8 collective-permute-start.8
  60.9 0.8 collective-permute-start.7
  61.7 0.4 shard_map.138
  62.1 3.4 %collective-permute-done.8.x2 = bf16[128,128]{1,0:T(8,128)(2,1)S(1)} collective-permute-done((bf16[128,128]{1,0:T(8,128)(2,1)S(1)}, bf16[128,128]{1,0:T(8,128)(2,1)S(1)}, u32[]{:S(2)}, u32[]{:S(2)}) %collective-permute-start.8) | collective-permute-done | bytes 32800 | tf_op jit(solution)/shard_map/ppermute | solution.py:395
  65.5 0.5 collective-permute-done.7.x1
  66.0 17.2 %all_to_all.30.zs = bf16[8,128,128]{2,1,0:T(8,128)(2,1)S(1)} all-to-all(bf16[8,128,128]{2,1,0:T(8,128)(2,1)S(1)} %shard_map.139), channel_id=1, replica_groups=mesh['z'=8,'x'=4,'y'=4,'c'=2] {'z'}, dimensions={0} | all-to-all | bytes 524288 | tf_op jit(solution)/shard_map/all_to_all | solution.py:403
  83.2 1.1 shard_map.140
  84.3 0.1 collective-permute-start.10
  84.4 1.2 collective-permute-done.10
  85.5 0.4 collective-permute-start.13
  86.0 2.6 %collective-permute-start.12 = (f32[8,128]{1,0:T(8,128)S(1)}, f32[8,128]{1,0:T(8,128)S(1)}, u32[]{:S(2)}, u32[]{:S(2)}) collective-permute-start(f32[8,128]{1,0:T(8,128)S(1)} %add.11.s0), channel_id=1, source_target_pairs={{0,4},{2,6},{4,0},{6,2},{1,5},{3,7},{5,1},{7,3},{8,12},{10,14},{12... | collective-permute-start | bytes 12296 | tf_op jit(solution)/shard_map/ppermute | solution.py:395
  88.6 1.9 %collective-permute-start.11 = (f32[8,128]{1,0:T(8,128)S(1)}, f32[8,128]{1,0:T(8,128)S(1)}, u32[]{:S(2)}, u32[]{:S(2)}) collective-permute-start(f32[8,128]{1,0:T(8,128)S(1)} %add.11.s0), channel_id=1, source_target_pairs={{0,2},{2,4},{4,6},{6,0},{1,3},{3,5},{5,7},{7,1},{8,10},{10,12},{12... | collective-permute-start | bytes 12296 | tf_op jit(solution)/shard_map/ppermute | solution.py:395
  90.5 0.6 collective-permute-done.12.s2
  91.1 1.1 collective-permute-done.11.s1
  92.2 0.4 shard_map.141
  92.6 1.1 collective-permute-start.16
  93.7 2.5 %collective-permute-start.15 = (bf16[144,128]{1,0:T(8,128)(2,1)S(1)}, bf16[144,128]{1,0:T(8,128)(2,1)S(1)}, u32[]{:S(2)}, u32[]{:S(2)}) collective-permute-start(bf16[144,128]{1,0:T(8,128)(2,1)S(1)} %get-tuple-element.93.x0), channel_id=1, source_target_pairs={{0,16},{8,24},{16,0},{24,8},{1,17},{9,25},{17,1},{25,9},{2,18},{10... | collective-permute-start | bytes 110600 | tf_op jit(solution)/shard_map/ppermute | solution.py:395
  96.2 0.6 collective-permute-start.14
  96.8 1.7 %shard_map.142 = (bf16[512,128]{1,0:T(8,128)(2,1)}, bf16[512,128]{1,0:T(8,128)(2,1)}, f32[512,128]{1,0:T(8,128)S(1)}, f32[512,128]{1,0:T(8,128)S(1)}) custom-call(f32[8,128]{1,0:T(8,128)S(1)} %get-tuple-element.81.inv, f32[512,128]{1,0:T(8,128)S(1)} %get-tuple-element.78.lin, f32[1,128]{1,0:T(1,128)S(1)} %copy-done.7, ...), custom_call_target="tpu_custom_call" | custom-call | tf_op jit(solution)/shard_map/pallas_call | solution.py:39
  98.5 0.7 collective-permute-done.15.x2
  99.2 1.0 collective-permute-done.14.x1
  100.2 13.2 %all_to_all.31.zs = bf16[8,144,128]{2,1,0:T(8,128)(2,1)S(1)} all-to-all(bf16[8,144,128]{2,1,0:T(8,128)(2,1)S(1)} %shard_map.143), channel_id=1, replica_groups=mesh['z'=8,'x'=4,'y'=4,'c'=2] {'z'}, dimensions={0} | all-to-all | bytes 589824 | tf_op jit(solution)/shard_map/all_to_all | solution.py:403
  113.4 8.0 %shard_map.144 = (bf16[512,128]{1,0:T(8,128)(2,1)}, bf16[512,128]{1,0:T(8,128)(2,1)}, bf16[8,192,128]{2,1,0:T(8,128)(2,1)S(1)}, bf16[8,192,128]{2,1,0:T(8,128)(2...) custom-call(s32[2]{0:T(128)S(1)} %pad_add_fusion.pos, ...), custom_call_target="tpu_custom_call" | custom-call | tf_op jit(solution)/shard_map/pallas_call | solution.py:39
  121.4 3.5 %all-to-all-start.4 = ((bf16[8,4,64,128]{3,2,1,0:T(8,128)(2,1)}), bf16[8,4,64,128]{3,2,1,0:T(8,128)(2,1)S(1)}, u32[]{:S(2)}, u32[]{:S(2)}) async-start(bf16[8,4,64,128]{3,2,1,0:T(8,128)(2,1)} %get-tuple-element.106), calls=%async_computation.4 | async-start | bytes 1048576 | tf_op jit(solution)/shard_map/all_to_all | solution.py:403
  125.0 1.9 %collective-permute-start.18 = (bf16[8,192,128]{2,1,0:T(8,128)(2,1)}, bf16[8,192,128]{2,1,0:T(8,128)(2,1)S(1)}, u32[]{:S(2)}, u32[]{:S(2)}) collective-permute-start(bf16[8,192,128]{2,1,0:T(8,128)(2,1)} %get-tuple-element.103), channel_id=1, source_target_pairs={{0,24},{8,0},{16,8},{24,16},{1,25},{9,1},{17,9},{25,17},{2,26},{10... | collective-permute-start | bytes 1179656 | tf_op jit(solution)/shard_map/ppermute | solution.py:395
  126.9 1.0 collective-permute-start.19
  127.9 0.1 collective-permute-start.20
  128.0 12.4 %collective-permute-done.18.a1 = bf16[8,192,128]{2,1,0:T(8,128)(2,1)S(1)} collective-permute-done((bf16[8,192,128]{2,1,0:T(8,128)(2,1)}, bf16[8,192,128]{2,1,0:T(8,128)(2,1)S(1)}, u32[]{:S(2)}, u32[]{:S(2)}) %collective-permute-start.18) | collective-permute-done | bytes 393248 | tf_op jit(solution)/shard_map/ppermute | solution.py:395
  140.3 3.6 %collective-permute-done.20.a3 = bf16[8,192,128]{2,1,0:T(8,128)(2,1)S(1)} collective-permute-done((bf16[8,192,128]{2,1,0:T(8,128)(2,1)S(1)}, bf16[8,192,128]{2,1,0:T(8,128)(2,1)S(1)}, u32[]{:S(2)}, u32[]{:S(2)}) %collective-permute-start.20) | collective-permute-done | bytes 393248 | tf_op jit(solution)/shard_map/ppermute | solution.py:395
  143.9 0.9 shard_map.146
  144.8 6.8 %all-to-all-start.5 = ((bf16[8,192,128]{2,1,0:T(8,128)(2,1)}), bf16[8,192,128]{2,1,0:T(8,128)(2,1)S(1)}, u32[]{:S(2)}, u32[]{:S(2)}) async-start(bf16[8,192,128]{2,1,0:T(8,128)(2,1)} %get-tuple-element.107), calls=%async_computation.5 | async-start | bytes 786432 | tf_op jit(solution)/shard_map/all_to_all | solution.py:403
  151.6 1.3 collective-permute-start.17
  152.9 2.2 %collective-permute-start.21 = (bf16[64,128]{1,0:T(8,128)(2,1)S(1)}, bf16[64,128]{1,0:T(8,128)(2,1)S(1)}, u32[]{:S(2)}, u32[]{:S(2)}) collective-permute-start(bf16[64,128]{1,0:T(8,128)(2,1)S(1)} %get-tuple-element.109), channel_id=1, source_target_pairs={{0,24},{8,0},{16,8},{24,16},{1,25},{9,1},{17,9},{25,17},{2,26},{10... | collective-permute-start | bytes 49160 | tf_op jit(solution)/shard_map/ppermute | solution.py:395
  155.1 2.6 %collective-permute-start.22 = (bf16[64,128]{1,0:T(8,128)(2,1)S(1)}, bf16[64,128]{1,0:T(8,128)(2,1)S(1)}, u32[]{:S(2)}, u32[]{:S(2)}) collective-permute-start(bf16[64,128]{1,0:T(8,128)(2,1)S(1)} %get-tuple-element.110), channel_id=1, source_target_pairs={{0,16},{8,24},{16,0},{24,8},{1,17},{9,25},{17,1},{25,9},{2,18},{10... | collective-permute-start | bytes 49160 | tf_op jit(solution)/shard_map/ppermute | solution.py:395
  157.7 0.5 slice.3
  158.2 0.7 shard_map.145
  158.9 1.5 collective-permute-done.22.l2
  160.3 2.3 %collective-permute-done.23.l3 = bf16[64,128]{1,0:T(8,128)(2,1)S(1)} collective-permute-done((bf16[64,128]{1,0:T(8,128)(2,1)S(1)}, bf16[64,128]{1,0:T(8,128)(2,1)S(1)}, u32[]{:S(2)}, u32[]{:S(2)}) %collective-permute-start.23) | collective-permute-done | bytes 16416 | tf_op jit(solution)/shard_map/ppermute | solution.py:395
  162.6 2.5 %all-to-all-done.5.top = bf16[8,192,128]{2,1,0:T(8,128)(2,1)S(1)} async-done(((bf16[8,192,128]{2,1,0:T(8,128)(2,1)}), bf16[8,192,128]{2,1,0:T(8,128)(2,1)S(1)}, u32[]{:S(2)}, u32[]{:S(2)}) %all-to-all-start.5) | async-done | bytes 393248 | tf_op jit(solution)/shard_map/all_to_all | solution.py:403
  165.1 1.4 shard_map.147
  (27 shorter events, 0.1 us)
Async XLA Ops:
  0.6 37.8 %copy-start.6 = (s32[128,20]{0,1:T(8,128)S(1)}, s32[128,20]{0,1:T(8,128)}, u32[]{:S(2)}) copy-start(s32[128,20]{0,1:T(8,128)} %param.15) | copy-start | bytes 30724
  0.6 52.2 %copy-start.5 = (bf16[1,512,128]{2,1,0:T(8,128)(2,1)S(1)}, bf16[1,512,128]{2,1,0:T(8,128)(2,1)}, u32[]{:S(2)}) copy-start(bf16[1,512,128]{2,1,0:T(8,128)(2,1)} %param.10) | copy-start | bytes 393220
  0.7 52.1 %copy-start.4 = (bf16[1,512,128]{2,1,0:T(8,128)(2,1)S(1)}, bf16[1,512,128]{2,1,0:T(8,128)(2,1)}, u32[]{:S(2)}) copy-start(bf16[1,512,128]{2,1,0:T(8,128)(2,1)} %param.9) | copy-start | bytes 393220
  0.7 52.1 %copy-start = (bf16[1,512,128]{2,1,0:T(8,128)(2,1)S(1)}, bf16[1,512,128]{2,1,0:T(8,128)(2,1)}, u32[]{:S(2)}) copy-start(bf16[1,512,128]{2,1,0:T(8,128)(2,1)} %param.12) | copy-start | bytes 393220
  0.7 52.1 %copy-start.3 = (bf16[1,512,128]{2,1,0:T(8,128)(2,1)S(1)}, bf16[1,512,128]{2,1,0:T(8,128)(2,1)}, u32[]{:S(2)}) copy-start(bf16[1,512,128]{2,1,0:T(8,128)(2,1)} %param.8) | copy-start | bytes 393220
  3.3 58.3 %copy-start.1 = (bf16[1,512,128]{2,1,0:T(8,128)(2,1)S(1)}, bf16[1,512,128]{2,1,0:T(8,128)(2,1)}, u32[]{:S(2)}) copy-start(bf16[1,512,128]{2,1,0:T(8,128)(2,1)} %param.11) | copy-start | bytes 393220
  3.4 23.3 %all-to-all-start = ((bf16[8,192,128]{2,1,0:T(8,128)(2,1)}), bf16[8,192,128]{2,1,0:T(8,128)(2,1)S(1)}, u32[]{:S(2)}, u32[]{:S(2)}) async-start(bf16[8,192,128]{2,1,0:T(8,128)(2,1)} %get-tuple-element.63), calls=%async_computation | async-start | bytes 786432 | tf_op jit(solution)/shard_map/all_to_all | solution.py:403
  12.0 4.4 %collective-permute-start.2 = (bf16[64,128]{1,0:T(8,128)(2,1)S(1)}, bf16[64,128]{1,0:T(8,128)(2,1)S(1)}, u32[]{:S(2)}, u32[]{:S(2)}) collective-permute-start(bf16[64,128]{1,0:T(8,128)(2,1)S(1)} %get-tuple-element.64.l0), channel_id=1, source_target_pairs={{0,24},{8,0},{16,8},{24,16},{1,25},{9,1},{17,9},{25,17},{2,26},{10... | collective-permute-start | bytes 49160 | tf_op jit(solution)/shard_map/ppermute | solution.py:395
  14.7 5.2 %collective-permute-start.1 = (bf16[64,128]{1,0:T(8,128)(2,1)S(1)}, bf16[64,128]{1,0:T(8,128)(2,1)S(1)}, u32[]{:S(2)}, u32[]{:S(2)}) collective-permute-start(bf16[64,128]{1,0:T(8,128)(2,1)S(1)} %get-tuple-element.64.l0), channel_id=1, source_target_pairs={{0,16},{8,24},{16,0},{24,8},{1,17},{9,25},{17,1},{25,9},{2,18},{10... | collective-permute-start | bytes 49160 | tf_op jit(solution)/shard_map/ppermute | solution.py:395
  15.5 4.9 %collective-permute-start = (bf16[64,128]{1,0:T(8,128)(2,1)S(1)}, bf16[64,128]{1,0:T(8,128)(2,1)S(1)}, u32[]{:S(2)}, u32[]{:S(2)}) collective-permute-start(bf16[64,128]{1,0:T(8,128)(2,1)S(1)} %get-tuple-element.64.l0), channel_id=1, source_target_pairs={{0,8},{8,16},{16,24},{24,0},{1,9},{9,17},{17,25},{25,1},{2,10},{10... | collective-permute-start | bytes 49160 | tf_op jit(solution)/shard_map/ppermute | solution.py:395
  21.4 61.9 %copy-start.2 = (bf16[1,512,128]{2,1,0:T(8,128)(2,1)S(1)}, bf16[1,512,128]{2,1,0:T(8,128)(2,1)}, u32[]{:S(2)}) copy-start(bf16[1,512,128]{2,1,0:T(8,128)(2,1)} %param.14) | copy-start | bytes 393220
  21.4 61.9 %copy-start.7 = (f32[1,128]{1,0:T(1,128)S(1)}, f32[1,128]{1,0:T(1,128)}, u32[]{:S(2)}) copy-start(f32[1,128]{1,0:T(1,128)} %gain.5) | copy-start | bytes 1540
  26.6 26.1 %all-to-all-start.1 = ((bf16[8,4,64,128]{3,2,1,0:T(8,128)(2,1)}), bf16[8,4,64,128]{3,2,1,0:T(8,128)(2,1)S(1)}, u32[]{:S(2)}, u32[]{:S(2)}) async-start(bf16[8,4,64,128]{3,2,1,0:T(8,128)(2,1)} %shard_map.136), calls=%async_computation.1 | async-start | bytes 1048576 | tf_op jit(solution)/shard_map/all_to_all | solution.py:403
  30.1 20.9 %collective-permute-start.5 = (bf16[8,192,128]{2,1,0:T(8,128)(2,1)S(1)}, bf16[8,192,128]{2,1,0:T(8,128)(2,1)S(1)}, u32[]{:S(2)}, u32[]{:S(2)}) collective-permute-start(bf16[8,192,128]{2,1,0:T(8,128)(2,1)S(1)} %all-to-all-done.f0), channel_id=1, source_target_pairs={{0,24},{8,0},{16,8},{24,16},{1,25},{9,1},{17,9},{25,17},{2,26},{10... | collective-permute-start | bytes 1179656 | tf_op jit(solution)/shard_map/ppermute | solution.py:395
  33.0 18.1 %collective-permute-start.4 = (bf16[8,192,128]{2,1,0:T(8,128)(2,1)S(1)}, bf16[8,192,128]{2,1,0:T(8,128)(2,1)S(1)}, u32[]{:S(2)}, u32[]{:S(2)}) collective-permute-start(bf16[8,192,128]{2,1,0:T(8,128)(2,1)S(1)} %all-to-all-done.f0), channel_id=1, source_target_pairs={{0,16},{8,24},{16,0},{24,8},{1,17},{9,25},{17,1},{25,9},{2,18},{10... | collective-permute-start | bytes 1179656 | tf_op jit(solution)/shard_map/ppermute | solution.py:395
  33.8 19.0 %collective-permute-start.3 = (bf16[8,192,128]{2,1,0:T(8,128)(2,1)S(1)}, bf16[8,192,128]{2,1,0:T(8,128)(2,1)S(1)}, u32[]{:S(2)}, u32[]{:S(2)}) collective-permute-start(bf16[8,192,128]{2,1,0:T(8,128)(2,1)S(1)} %all-to-all-done.f0), channel_id=1, source_target_pairs={{0,8},{8,16},{16,24},{24,0},{1,9},{9,17},{17,25},{25,1},{2,10},{10... | collective-permute-start | bytes 1179656 | tf_op jit(solution)/shard_map/ppermute | solution.py:395
  34.7 16.4 %collective-permute-start.6 = (bf16[128,256]{1,0:T(8,128)(2,1)S(1)}, bf16[128,256]{1,0:T(8,128)(2,1)S(1)}, u32[]{:S(2)}, u32[]{:S(2)}) collective-permute-start(bf16[128,256]{1,0:T(8,128)(2,1)S(1)} %get-tuple-element.67), channel_id=1, source_target_pairs={{0,8},{8,16},{16,24},{24,32},{32,40},{40,48},{48,56},{56,64},{64,7... | collective-permute-start | bytes 196616 | tf_op jit(solution)/shard_map/ppermute | solution.py:440
  57.9 4.1 %collective-permute-start.9 = (bf16[128,128]{1,0:T(8,128)(2,1)S(1)}, bf16[128,128]{1,0:T(8,128)(2,1)S(1)}, u32[]{:S(2)}, u32[]{:S(2)}) collective-permute-start(bf16[128,128]{1,0:T(8,128)(2,1)S(1)} %get-tuple-element.74.x0), channel_id=1, source_target_pairs={{0,24},{8,0},{16,8},{24,16},{1,25},{9,1},{17,9},{25,17},{2,26},{10... | collective-permute-start | bytes 98312 | tf_op jit(solution)/shard_map/ppermute | solution.py:395
  60.0 5.4 %collective-permute-start.8 = (bf16[128,128]{1,0:T(8,128)(2,1)S(1)}, bf16[128,128]{1,0:T(8,128)(2,1)S(1)}, u32[]{:S(2)}, u32[]{:S(2)}) collective-permute-start(bf16[128,128]{1,0:T(8,128)(2,1)S(1)} %get-tuple-element.74.x0), channel_id=1, source_target_pairs={{0,16},{8,24},{16,0},{24,8},{1,17},{9,25},{17,1},{25,9},{2,18},{10... | collective-permute-start | bytes 98312 | tf_op jit(solution)/shard_map/ppermute | solution.py:395
  60.9 5.1 %collective-permute-start.7 = (bf16[128,128]{1,0:T(8,128)(2,1)S(1)}, bf16[128,128]{1,0:T(8,128)(2,1)S(1)}, u32[]{:S(2)}, u32[]{:S(2)}) collective-permute-start(bf16[128,128]{1,0:T(8,128)(2,1)S(1)} %get-tuple-element.74.x0), channel_id=1, source_target_pairs={{0,8},{8,16},{16,24},{24,0},{1,9},{9,17},{17,25},{25,1},{2,10},{10... | collective-permute-start | bytes 98312 | tf_op jit(solution)/shard_map/ppermute | solution.py:395
  84.3 1.2 collective-permute-start.10
  85.5 4.9 %collective-permute-start.13 = (f32[8,128]{1,0:T(8,128)S(1)}, f32[8,128]{1,0:T(8,128)S(1)}, u32[]{:S(2)}, u32[]{:S(2)}) collective-permute-start(f32[8,128]{1,0:T(8,128)S(1)} %add.11.s0), channel_id=1, source_target_pairs={{0,6},{2,0},{4,2},{6,4},{1,7},{3,1},{5,3},{7,5},{8,14},{10,8},{12,... | collective-permute-start | bytes 12296 | tf_op jit(solution)/shard_map/ppermute | solution.py:395
  86.0 5.1 %collective-permute-start.12 = (f32[8,128]{1,0:T(8,128)S(1)}, f32[8,128]{1,0:T(8,128)S(1)}, u32[]{:S(2)}, u32[]{:S(2)}) collective-permute-start(f32[8,128]{1,0:T(8,128)S(1)} %add.11.s0), channel_id=1, source_target_pairs={{0,4},{2,6},{4,0},{6,2},{1,5},{3,7},{5,1},{7,3},{8,12},{10,14},{12... | collective-permute-start | bytes 12296 | tf_op jit(solution)/shard_map/ppermute | solution.py:395
  88.6 3.6 %collective-permute-start.11 = (f32[8,128]{1,0:T(8,128)S(1)}, f32[8,128]{1,0:T(8,128)S(1)}, u32[]{:S(2)}, u32[]{:S(2)}) collective-permute-start(f32[8,128]{1,0:T(8,128)S(1)} %add.11.s0), channel_id=1, source_target_pairs={{0,2},{2,4},{4,6},{6,0},{1,3},{3,5},{5,7},{7,1},{8,10},{10,12},{12... | collective-permute-start | bytes 12296 | tf_op jit(solution)/shard_map/ppermute | solution.py:395
  92.6 5.9 %collective-permute-start.16 = (bf16[144,128]{1,0:T(8,128)(2,1)S(1)}, bf16[144,128]{1,0:T(8,128)(2,1)S(1)}, u32[]{:S(2)}, u32[]{:S(2)}) collective-permute-start(bf16[144,128]{1,0:T(8,128)(2,1)S(1)} %get-tuple-element.93.x0), channel_id=1, source_target_pairs={{0,8},{8,16},{16,24},{24,0},{1,9},{9,17},{17,25},{25,1},{2,10},{10... | collective-permute-start | bytes 110600 | tf_op jit(solution)/shard_map/ppermute | solution.py:395
  93.7 5.5 %collective-permute-start.15 = (bf16[144,128]{1,0:T(8,128)(2,1)S(1)}, bf16[144,128]{1,0:T(8,128)(2,1)S(1)}, u32[]{:S(2)}, u32[]{:S(2)}) collective-permute-start(bf16[144,128]{1,0:T(8,128)(2,1)S(1)} %get-tuple-element.93.x0), channel_id=1, source_target_pairs={{0,16},{8,24},{16,0},{24,8},{1,17},{9,25},{17,1},{25,9},{2,18},{10... | collective-permute-start | bytes 110600 | tf_op jit(solution)/shard_map/ppermute | solution.py:395
  96.2 4.0 %collective-permute-start.14 = (bf16[144,128]{1,0:T(8,128)(2,1)S(1)}, bf16[144,128]{1,0:T(8,128)(2,1)S(1)}, u32[]{:S(2)}, u32[]{:S(2)}) collective-permute-start(bf16[144,128]{1,0:T(8,128)(2,1)S(1)} %get-tuple-element.93.x0), channel_id=1, source_target_pairs={{0,24},{8,0},{16,8},{24,16},{1,25},{9,1},{17,9},{25,17},{2,26},{10... | collective-permute-start | bytes 110600 | tf_op jit(solution)/shard_map/ppermute | solution.py:395
  121.4 22.4 %all-to-all-start.4 = ((bf16[8,4,64,128]{3,2,1,0:T(8,128)(2,1)}), bf16[8,4,64,128]{3,2,1,0:T(8,128)(2,1)S(1)}, u32[]{:S(2)}, u32[]{:S(2)}) async-start(bf16[8,4,64,128]{3,2,1,0:T(8,128)(2,1)} %get-tuple-element.106), calls=%async_computation.4 | async-start | bytes 1048576 | tf_op jit(solution)/shard_map/all_to_all | solution.py:403
  125.0 15.4 %collective-permute-start.18 = (bf16[8,192,128]{2,1,0:T(8,128)(2,1)}, bf16[8,192,128]{2,1,0:T(8,128)(2,1)S(1)}, u32[]{:S(2)}, u32[]{:S(2)}) collective-permute-start(bf16[8,192,128]{2,1,0:T(8,128)(2,1)} %get-tuple-element.103), channel_id=1, source_target_pairs={{0,24},{8,0},{16,8},{24,16},{1,25},{9,1},{17,9},{25,17},{2,26},{10... | collective-permute-start | bytes 1179656 | tf_op jit(solution)/shard_map/ppermute | solution.py:395
  126.9 13.4 %collective-permute-start.19 = (bf16[8,192,128]{2,1,0:T(8,128)(2,1)}, bf16[8,192,128]{2,1,0:T(8,128)(2,1)S(1)}, u32[]{:S(2)}, u32[]{:S(2)}) collective-permute-start(bf16[8,192,128]{2,1,0:T(8,128)(2,1)} %get-tuple-element.104), channel_id=1, source_target_pairs={{0,16},{8,24},{16,0},{24,8},{1,17},{9,25},{17,1},{25,9},{2,18},{10... | collective-permute-start | bytes 1179656 | tf_op jit(solution)/shard_map/ppermute | solution.py:395
  127.9 16.0 %collective-permute-start.20 = (bf16[8,192,128]{2,1,0:T(8,128)(2,1)S(1)}, bf16[8,192,128]{2,1,0:T(8,128)(2,1)S(1)}, u32[]{:S(2)}, u32[]{:S(2)}) collective-permute-start(bf16[8,192,128]{2,1,0:T(8,128)(2,1)S(1)} %get-tuple-element.105), channel_id=1, source_target_pairs={{0,8},{8,16},{16,24},{24,0},{1,9},{9,17},{17,25},{25,1},{2,10},{10... | collective-permute-start | bytes 1179656 | tf_op jit(solution)/shard_map/ppermute | solution.py:395
  144.8 20.3 %all-to-all-start.5 = ((bf16[8,192,128]{2,1,0:T(8,128)(2,1)}), bf16[8,192,128]{2,1,0:T(8,128)(2,1)S(1)}, u32[]{:S(2)}, u32[]{:S(2)}) async-start(bf16[8,192,128]{2,1,0:T(8,128)(2,1)} %get-tuple-element.107), calls=%async_computation.5 | async-start | bytes 786432 | tf_op jit(solution)/shard_map/all_to_all | solution.py:403
  151.6 7.3 %collective-permute-start.17 = (bf16[128,256]{1,0:T(8,128)(2,1)S(1)}, bf16[128,256]{1,0:T(8,128)(2,1)S(1)}, u32[]{:S(2)}, u32[]{:S(2)}) collective-permute-start(bf16[128,256]{1,0:T(8,128)(2,1)S(1)} %get-tuple-element.101), channel_id=1, source_target_pairs={{8,0},{16,8},{24,16},{32,24},{40,32},{48,40},{56,48},{64,56},{72,6... | collective-permute-start | bytes 196616 | tf_op jit(solution)/shard_map/ppermute | solution.py:517
  152.9 6.0 %collective-permute-start.21 = (bf16[64,128]{1,0:T(8,128)(2,1)S(1)}, bf16[64,128]{1,0:T(8,128)(2,1)S(1)}, u32[]{:S(2)}, u32[]{:S(2)}) collective-permute-start(bf16[64,128]{1,0:T(8,128)(2,1)S(1)} %get-tuple-element.109), channel_id=1, source_target_pairs={{0,24},{8,0},{16,8},{24,16},{1,25},{9,1},{17,9},{25,17},{2,26},{10... | collective-permute-start | bytes 49160 | tf_op jit(solution)/shard_map/ppermute | solution.py:395
  155.1 5.2 %collective-permute-start.22 = (bf16[64,128]{1,0:T(8,128)(2,1)S(1)}, bf16[64,128]{1,0:T(8,128)(2,1)S(1)}, u32[]{:S(2)}, u32[]{:S(2)}) collective-permute-start(bf16[64,128]{1,0:T(8,128)(2,1)S(1)} %get-tuple-element.110), channel_id=1, source_target_pairs={{0,16},{8,24},{16,0},{24,8},{1,17},{9,25},{17,1},{25,9},{2,18},{10... | collective-permute-start | bytes 49160 | tf_op jit(solution)/shard_map/ppermute | solution.py:395
  157.7 4.9 %collective-permute-start.23 = (bf16[64,128]{1,0:T(8,128)(2,1)S(1)}, bf16[64,128]{1,0:T(8,128)(2,1)S(1)}, u32[]{:S(2)}, u32[]{:S(2)}) collective-permute-start(bf16[64,128]{1,0:T(8,128)(2,1)S(1)} %get-tuple-element.111), channel_id=1, source_target_pairs={{0,8},{8,16},{16,24},{24,0},{1,9},{9,17},{17,25},{25,1},{2,10},{10... | collective-permute-start | bytes 49160 | tf_op jit(solution)/shard_map/ppermute | solution.py:395

commit v4 on v3

--- a/solution.py
+++ b/solution.py
@@ -25,6 +25,9 @@
 PREV = FAR + 4
 HALF = 64
 TOP = 192
+REST = 48
+FIRST = 208
+MOST = FIRST - BLK
 SENT = 144
 POOL = FAR + 5
 
@@ -78,11 +81,11 @@
     pairs = []
     for i in range(NZ):
         pairs.append((keys.at[mine], top.at[i, pl.ds(0, BLK)]))
-        pairs.append((values.at[mine, pl.ds(0, HALF)], top.at[i, pl.ds(BLK, HALF)]))
+        pairs.append((values.at[mine, pl.ds(0, MOST)], top.at[i, pl.ds(BLK, MOST)]))
     copies = [pltpu.make_async_copy(a, b, sems.at[i]) for i, (a, b) in enumerate(pairs)]
     for c in copies:
         c.start()
-    low[...] = values[mine, HALF:, :]
+    low[...] = values[mine, MOST:, :]
     last[:, 0:BLK] = keys[3]
     last[:, BLK:] = values[3]
     for c in copies:
@@ -118,8 +121,8 @@
     for j, f in enumerate(far):
         spot = pl.ds(NZ * j, NZ)
         pairs.append((f.at[:, pl.ds(0, BLK)], pool.at[spot, :, left]))
-        pairs.append((f.at[:, pl.ds(BLK, HALF)], pool.at[spot, pl.ds(0, HALF), right]))
-        pairs.append((low.at[:, j], pool.at[spot, pl.ds(HALF, HALF), right]))
+        pairs.append((f.at[:, pl.ds(BLK, MOST)], pool.at[spot, pl.ds(0, MOST), right]))
+        pairs.append((low.at[:, j], pool.at[spot, pl.ds(MOST, REST), right]))
     return pairs
 
 
@@ -166,11 +169,8 @@
     state[...] = mm(lk[...], att[...], TN).astype(bf16)
 
 
-def row_kernel(x0, x1, x2, x3, out):
-    total = x0[...].astype(f32)
-    for r in (x1, x2, x3):
-        total = total + r[...].astype(f32)
-    total = total.astype(bf16)
+def row_kernel(x0, x1, out):
+    total = (x0[...].astype(f32) + x1[...].astype(f32)).astype(bf16)
     for i in range(NZ):
         out[i] = total
 
@@ -193,10 +193,9 @@
             run = run + mm(lk[r], att[r], TN)
 
 
-def linear_kernel(pos, lq, inner, local, gain, cot, x0, x1, x2, x3, zs, lin, prior, sums):
-    run = jnp.zeros((BLK, BLK), f32)
-    for j, r in enumerate((x1, x2, x3)):
-        run = run + jnp.where(pos[1] > j, r[...].astype(f32), 0.0)
+def linear_kernel(pos, lq, inner, local, gain, cot, near, pair, zs, lin, prior, sums):
+    run = jnp.where(jnp.bitwise_and(pos[1], 1) == 1, near[...].astype(f32), 0.0)
+    run = run + jnp.where(pos[1] >= 2, pair[...].astype(f32), 0.0)
     for i in range(NZ - 1):
         run = run + jnp.where(pos[0] > i, zs[i].astype(f32), 0.0)
     sums[...] = jnp.zeros((8, BLK), f32)
@@ -221,8 +220,8 @@
     return high, (row - high.astype(f32)).astype(bf16)
 
 
-def norm_kernel(features, lq, lin, gain, cot, s0, s1, s2, s3, glin, inv_out, send, local):
-    inv, pull = norm_terms(s0[...] + s1[...] + s2[...] + s3[...], features)
+def norm_kernel(features, lq, lin, gain, cot, s0, s1, glin, inv_out, send, local):
+    inv, pull = norm_terms(s0[...] + s1[...], features)
     inv_out[0:4] = inv
     inv_out[4:8] = inv
     ggain = jnp.zeros((1, BLK), f32)
@@ -244,12 +243,18 @@
     send[BLK + 8 :] = jnp.broadcast_to(rest, (8, BLK))
 
 
-def sent_kernel(x0, x1, x2, x3, out):
-    total = x0[...].astype(f32)
-    for r in (x1, x2, x3):
-        total = total + r[...].astype(f32)
+def joined(a, b):
+    total = a[...].astype(f32) + b[...].astype(f32)
     high, rest = split_row(total[BLK : BLK + 8] + total[BLK + 8 :])
-    state = total[0:BLK].astype(bf16)
+    return total[0:BLK].astype(bf16), high, rest
+
+
+def pair_kernel(x0, x1, out):
+    out[0:BLK], out[BLK : BLK + 8], out[BLK + 8 :] = joined(x0, x1)
+
+
+def sent_kernel(x0, x1, out):
+    state, high, rest = joined(x0, x1)
     for i in range(NZ):
         out[i, 0:BLK] = state
         out[i, BLK : BLK + 8] = high
@@ -274,14 +279,13 @@
 
 
 def backward_kernel(pos, names, q, lse, att, lk, dlk_in, gatt_in, local,
-                    x0, x1, x2, x3, zs, pool,
+                    near, pair, zs, pool,
                     dlk, dq, o0, o1, o2, o3, olow, own, back, ggain,
-                    acc, gatt, delta, near, lows, sems):
+                    acc, gatt, delta, dlk_buf, dq_buf, far_buf, lows, sems):
     nsel = names.shape[0]
     scale = BLK ** (-0.5)
-    later = jnp.zeros((BLK, BLK), f32)
-    for j, r in enumerate((x1, x2, x3)):
-        later = later + jnp.where(pos[1] + j + 1 < NX, r[0:BLK].astype(f32), 0.0)
+    later = jnp.where(jnp.bitwise_and(pos[1], 1) == 0, near[0:BLK].astype(f32), 0.0)
+    later = later + jnp.where(pos[1] < 2, pair[0:BLK].astype(f32), 0.0)
     gg = jnp.zeros((8, BLK), f32)
     for i in range(NZ):
         later = later + jnp.where(pos[0] < i, zs[i, 0:BLK].astype(f32), 0.0)
@@ -290,12 +294,14 @@
     for b in range(4):
         r = slice(b * BLK, (b + 1) * BLK)
         after = (later + local[b]).astype(bf16)
-        dlk[r] = (dlk_in[r] + mm(att[r], after, NT)).astype(bf16)
+        dlk_buf[r] = (dlk_in[r] + mm(att[r], after, NT)).astype(bf16)
         g = (gatt_in[r] + mm(lk[r], after)).astype(bf16)
         gatt[r] = g
         delta[b : b + 1] = as_row(
             jnp.sum(g.astype(f32) * att[r].astype(f32), axis=1, keepdims=True)
         )
+    copies = [pltpu.make_async_copy(dlk_buf, dlk, sems.at[0])]
+    copies[0].start()
     acc[...] = jnp.zeros(acc.shape, f32)
 
     def block(b, carry):
@@ -328,20 +334,24 @@
             dqb = dqb + mm(ds, keyval[:, 0:BLK], TN)
             for i, (spot, _) in enumerate(spots):
                 acc[spot] += grads[i * BLK : (i + 1) * BLK]
-        dq[rows(b), :] = (dqb * scale).astype(bf16)
+        dq_buf[rows(b), :] = (dqb * scale).astype(bf16)
         return carry
 
     lax.fori_loop(0, 4, block, 0)
+
+    def send(src, dst):
+        copies.append(pltpu.make_async_copy(src, dst, sems.at[len(copies)]))
+        copies[-1].start()
+
+    send(dq_buf, dq)
+    for j, o in ((1, o1), (2, o2), (3, o3), (0, o0)):
+        spot = slice(NZ * j, NZ * (j + 1))
+        far_buf[j, :, 0:BLK] = (acc[spot, :, 0:BLK] * scale).astype(bf16)
+        far_buf[j, :, BLK:] = acc[spot, 0:HALF, BLK:].astype(bf16)
+        send(far_buf.at[j], o)
     for j in range(NX):
         lows[:, j] = acc[NZ * j : NZ * (j + 1), HALF:, BLK:].astype(bf16)
-    near[:, 0:BLK] = (acc[0:NZ, :, 0:BLK] * scale).astype(bf16)
-    near[:, BLK:] = acc[0:NZ, 0:HALF, BLK:].astype(bf16)
-    copies = [pltpu.make_async_copy(lows, olow, sems.at[0]), pltpu.make_async_copy(near, o0, sems.at[1])]
-    for c in copies:
-        c.start()
-    for j, o in ((1, o1), (2, o2), (3, o3)):
-        o[:, 0:BLK] = (acc[NZ * j : NZ * (j + 1), :, 0:BLK] * scale).astype(bf16)
-        o[:, BLK:] = acc[NZ * j : NZ * (j + 1), 0:HALF, BLK:].astype(bf16)
+    send(lows, olow)
     own[:, :, 0:BLK] = acc[OWN : OWN + 4, :, 0:BLK] * scale
     own[:, :, BLK:] = acc[OWN : OWN + 4, :, BLK:]
     back[:, 0:BLK] = (acc[PREV, :, 0:BLK] * scale).astype(bf16)
@@ -395,6 +405,10 @@
     return lax.ppermute(value, axis, [(i, (i + by) % size) for i in range(size)])
 
 
+def flip(value, axis, size, bit):
+    return lax.ppermute(value, axis, [(i, i ^ bit) for i in range(size)])
+
+
 def in_hbm(value):
     return pltpu.with_memory_space_constraint(value, pltpu.HBM)
 
@@ -426,7 +440,7 @@
 
     tops, low, last = call(
         pick_kernel,
-        [((NZ, TOP, width), bf16), ((HALF, width), bf16), ((BLK, 2 * BLK), bf16)],
+        [((NZ, FIRST, width), bf16), ((REST, width), bf16), ((BLK, 2 * BLK), bf16)],
         (pos, in_hbm(key_block), in_hbm(k4), in_hbm(v4)),
         [SM, HB, HB, HB],
         [
@@ -441,10 +455,10 @@
     lows = [low] + [turn(low, "x", NX, j) for j in range(1, NX)]
     (lows,) = call(
         spread_kernel,
-        [((NZ, NX, HALF, width), bf16)],
+        [((NZ, NX, REST, width), bf16)],
         lows,
         [VM] * 4,
-        [pltpu.VMEM((NX, HALF, width), bf16), pltpu.SemaphoreType.DMA((NZ,))],
+        [pltpu.VMEM((NX, REST, width), bf16), pltpu.SemaphoreType.DMA((NZ,))],
         [HB],
     )
     tops = swap(tops)
@@ -461,55 +475,64 @@
         vmem=16,
     )
 
-    xs = [state] + [turn(state, "x", NX, j) for j in range(1, NX)]
+    near = flip(state, "x", NX, 1)
+    half = (state.astype(f32) + near.astype(f32)).astype(bf16)
+    pair = flip(half, "x", NX, 2)
     inner, local = call(
         within_kernel,
         [((512, width), f32), ((4, BLK, width), f32)],
         (lq, lk, att),
         [VM] * 3,
     )
-    *xs, inner, local = lax.optimization_barrier((*xs, inner, local))
-    (wide,) = call(row_kernel, [((NZ, BLK, width), bf16)], xs, [VM] * 4)
+    pair, inner, local = lax.optimization_barrier((pair, inner, local))
+    (wide,) = call(row_kernel, [((NZ, BLK, width), bf16)], (half, pair), [VM] * 2)
     lin, prior, sums = call(
         linear_kernel,
         [((512, width), f32), ((4, BLK, width), bf16), ((8, BLK), f32)],
-        (pos, lq, inner, local, gain, cot, *xs, swap(wide)),
-        [SM] + [VM] * 10,
-    )
-    sums = sums + turn(sums, "c", NC, 1)
-    ys = [sums] + [turn(sums, "y", NY, i) for i in range(1, NY)]
+        (pos, lq, inner, local, gain, cot, near, pair, swap(wide)),
+        [SM] + [VM] * 8,
+    )
+    sums = sums + flip(sums, "c", NC, 1)
+    sums = sums + flip(sums, "y", NY, 1)
+    others = flip(sums, "y", NY, 2)
     glin, inv, send, local = call(
         functools.partial(norm_kernel, features),
         [((512, width), bf16), ((8, BLK), f32), ((SENT, BLK), bf16), ((4, BLK, BLK), f32)],
-        (lq, lin, gain, cot, *ys),
-        [VM] * 8,
-    )
-    ex = [send] + [turn(send, "x", NX, -j) for j in range(1, NX)]
+        (lq, lin, gain, cot, sums, others),
+        [VM] * 6,
+    )
+    near = flip(send, "x", NX, 1)
+    (half,) = call(pair_kernel, [((SENT, width), bf16)], (send, near), [VM] * 2)
+    pair = flip(half, "x", NX, 2)
     mixed, dlq, dlk_in, gatt_in = call(
         side_kernel,
         [((512, width), bf16), ((512, width), bf16), ((512, width), f32), ((512, width), f32)],
         (inv, lin, gain, att, glin, lk, lq, prior, cot),
         [VM] * 9,
     )
-    *ex, mixed, dlq, dlk_in, gatt_in = lax.optimization_barrier((*ex, mixed, dlq, dlk_in, gatt_in))
-    (wide,) = call(sent_kernel, [((NZ, SENT, width), bf16)], ex, [VM] * 4)
+    pair, mixed, dlq, dlk_in, gatt_in = lax.optimization_barrier(
+        (pair, mixed, dlq, dlk_in, gatt_in)
+    )
+    (wide,) = call(sent_kernel, [((NZ, SENT, width), bf16)], (half, pair), [VM] * 2)
     outs = call(
         backward_kernel,
         [((512, width), bf16), ((512, width), bf16)]
         + [((NZ, TOP, width), bf16)] * 4
         + [((NZ, NX, HALF, width), bf16), ((4, BLK, 2 * BLK), f32)]
         + [((BLK, 2 * BLK), bf16), ((8, BLK), f32)],
-        (pos, names, q, lse, att, lk, dlk_in, gatt_in, local, *ex, swap(wide), pool),
-        [SM, SM] + [VM] * 13,
+        (pos, names, q, lse, att, lk, dlk_in, gatt_in, local, near, pair, swap(wide), pool),
+        [SM, SM] + [VM] * 11,
         [
             pltpu.VMEM((POOL, BLK, 2 * BLK), f32),
             pltpu.VMEM((512, width), bf16),
             pltpu.VMEM((8, BLK), f32),
-            pltpu.VMEM((NZ, TOP, width), bf16),
+            pltpu.VMEM((512, width), bf16),
+            pltpu.VMEM((512, width), bf16),
+            pltpu.VMEM((NX, NZ, TOP, width), bf16),
             pltpu.VMEM((NZ, NX, HALF, width), bf16),
-            pltpu.SemaphoreType.DMA((2,)),
+            pltpu.SemaphoreType.DMA((NX + 3,)),
         ],
-        [VM, VM, HB, VM, VM, VM, HB, VM, VM, VM],
+        [HB] * 7 + [VM, VM, VM],
         vmem=24,
     )
     dlk, dq = outs[0], outs[1]

time: 168 us -> 173 us (1.030)
  waiting for transfers between devices: 54.3 us -> 64.6 us
  starting transfers between devices: 57.1 us -> 50.2 us
    ppermute x0 -> x7, waiting for transfers between devices: none -> 20.2 us  [flip(): return lax.ppermute(value, axis, [(i, i ^ bit) for i in range(size)])]
    ppermute x22 -> x12, starting transfers between devices: 29.7 us -> 15.9 us  [turn(): lax.ppermute(value, axis, [(i, (i + by) % size) for i in range(size)])]
    ppermute x22 -> x12, waiting for transfers between devices: 33.9 us -> 23.9 us  [turn(): lax.ppermute(value, axis, [(i, (i + by) % size) for i in range(size)])]
    ppermute x0 -> x7, starting transfers between devices: none -> 6.86 us  [flip(): return lax.ppermute(value, axis, [(i, i ^ bit) for i in range(size)])]
    pallas_call x13 -> x14, Pallas kernels: 23.2 us -> 23.1 us  [call(): pl.pallas_call(body, out_shape=[jax.ShapeDtypeStruct(s, d) for s, d in ou...]
  transfers between devices with their start and end apart: 28 -> 25, of which waited for: 17 -> 18; matrix products, arithmetic and copies ran while one was open for 0% -> 1% of each run, Pallas kernels for 2% -> 2%
where the time goes in v4:
time: 173 us
  waiting for transfers between devices  64.6 us (37%)
  starting transfers between devices  50.2 us (29%)
  blocking collectives  31.7 us (18%)
  Pallas kernels  23.1 us (13%)
  local copies, waits for them, and re-layouts  2.09 us (1%)
    all_to_all x2, blocking collectives, swap(): return lax.all_to_all(value, 'z', 0, 0, tiled=True)  31.7 us
    ppermute x12, waiting for transfers between devices, turn(): lax.ppermute(value, axis, [(i, (i + by) % size) for i in range(size)])  23.9 us
    pallas_call x14, Pallas kernels, call(): pl.pallas_call(body, out_shape=[jax.ShapeDtypeStruct(s, d) for s, d in ou...  23.1 us
    all_to_all x4, starting transfers between devices, swap(): return lax.all_to_all(value, 'z', 0, 0, tiled=True)  22.5 us
    ppermute x7, waiting for transfers between devices, flip(): return lax.ppermute(value, axis, [(i, i ^ bit) for i in range(size)])  20.2 us
    ppermute x12, starting transfers between devices, turn(): lax.ppermute(value, axis, [(i, (i + by) % size) for i in range(size)])  15.9 us
    ppermute x1, waiting for transfers between devices, per_device(): prev = lax.ppermute(last, seq, [(i, i + 1) for i in range(NZ * NX - 1)])  13.4 us
    all_to_all x4, waiting for transfers between devices, swap(): return lax.all_to_all(value, 'z', 0, 0, tiled=True)  7.12 us
  transfers between devices with their start and end apart: 25, of which 18 were waited for; matrix products, arithmetic and copies ran while one was open for 1% of the time, Pallas kernels for 2%

profile of v4, /device:TPU:8, one launch (start us, length us, event | category | flops | bytes accessed | tf_op | source)
XLA Modules:
  0.0 172.7 jit_solution(7237824127764462406)
XLA Ops:
  0.6 0.0 copy-start.5
  0.6 0.0 copy-start.4
  0.7 0.1 pad_add_fusion.pos
  0.8 2.5 %shard_map.135 = (bf16[8,208,128]{2,1,0:T(8,128)(2,1)}, bf16[48,128]{1,0:T(8,128)(2,1)S(1)}, bf16[128,256]{1,0:T(8,128)(2,1)S(1)}) custom-call(s32[2]{0:T(128)S(1)} %pad_add_fusion.pos, s32[20,128]{1,0:T(8,128)} %bitcast.34, bf16[4,128,128]{2,1,0:T(8,128)(2,1)} %bitcast.30, bf16[4,128,128]{2,1,0:T(8,128)(2,1)} %bitcast.32), custom_call_target="tpu_custom_call" | custom-call | tf_op jit(solution)/shard_map/pallas_call | solution.py:42
  3.3 0.0 copy-start
  3.3 8.6 %all-to-all-start = ((bf16[8,208,128]{2,1,0:T(8,128)(2,1)}), bf16[8,208,128]{2,1,0:T(8,128)(2,1)S(1)}, u32[]{:S(2)}, u32[]{:S(2)}) async-start(bf16[8,208,128]{2,1,0:T(8,128)(2,1)} %get-tuple-element.57), calls=%async_computation | async-start | bytes 851968 | tf_op jit(solution)/shard_map/all_to_all | solution.py:417
  11.9 2.8 %collective-permute-start.2 = (bf16[48,128]{1,0:T(8,128)(2,1)S(1)}, bf16[48,128]{1,0:T(8,128)(2,1)S(1)}, u32[]{:S(2)}, u32[]{:S(2)}) collective-permute-start(bf16[48,128]{1,0:T(8,128)(2,1)S(1)} %get-tuple-element.58.l0), channel_id=1, source_target_pairs={{0,24},{8,0},{16,8},{24,16},{1,25},{9,1},{17,9},{25,17},{2,26},{10... | collective-permute-start | bytes 36872 | tf_op jit(solution)/shard_map/ppermute | solution.py:405
  14.7 0.8 collective-permute-start.1
  15.5 0.9 collective-permute-start
  16.4 3.5 %collective-permute-done.1.l2 = bf16[48,128]{1,0:T(8,128)(2,1)S(1)} collective-permute-done((bf16[48,128]{1,0:T(8,128)(2,1)S(1)}, bf16[48,128]{1,0:T(8,128)(2,1)S(1)}, u32[]{:S(2)}, u32[]{:S(2)}) %collective-permute-start.1) | collective-permute-done | bytes 12320 | tf_op jit(solution)/shard_map/ppermute | solution.py:405
  19.9 0.5 collective-permute-done.l1
  20.4 0.8 shard_map.136
  21.2 0.0 copy-start.2
  21.3 0.0 copy-start.7
  21.3 6.1 %all-to-all-done.f0 = bf16[8,208,128]{2,1,0:T(8,128)(2,1)S(1)} async-done(((bf16[8,208,128]{2,1,0:T(8,128)(2,1)}), bf16[8,208,128]{2,1,0:T(8,128)(2,1)S(1)}, u32[]{:S(2)}, u32[]{:S(2)}) %all-to-all-start) | async-done | bytes 426016 | tf_op jit(solution)/shard_map/all_to_all | solution.py:417
  27.3 3.5 %all-to-all-start.1 = ((bf16[8,4,48,128]{3,2,1,0:T(8,128)(2,1)}), bf16[8,4,48,128]{3,2,1,0:T(8,128)(2,1)S(1)}, u32[]{:S(2)}, u32[]{:S(2)}) async-start(bf16[8,4,48,128]{3,2,1,0:T(8,128)(2,1)} %shard_map.136), calls=%async_computation.1 | async-start | bytes 786432 | tf_op jit(solution)/shard_map/all_to_all | solution.py:417
  30.8 2.8 %collective-permute-start.5 = (bf16[8,208,128]{2,1,0:T(8,128)(2,1)S(1)}, bf16[8,208,128]{2,1,0:T(8,128)(2,1)S(1)}, u32[]{:S(2)}, u32[]{:S(2)}) collective-permute-start(bf16[8,208,128]{2,1,0:T(8,128)(2,1)S(1)} %all-to-all-done.f0), channel_id=1, source_target_pairs={{0,24},{8,0},{16,8},{24,16},{1,25},{9,1},{17,9},{25,17},{2,26},{10... | collective-permute-start | bytes 1277960 | tf_op jit(solution)/shard_map/ppermute | solution.py:405
  33.6 0.8 collective-permute-start.4
  34.4 0.9 collective-permute-start.3
  35.3 3.7 %collective-permute-start.6 = (bf16[128,256]{1,0:T(8,128)(2,1)S(1)}, bf16[128,256]{1,0:T(8,128)(2,1)S(1)}, u32[]{:S(2)}, u32[]{:S(2)}) collective-permute-start(bf16[128,256]{1,0:T(8,128)(2,1)S(1)} %get-tuple-element.61), channel_id=1, source_target_pairs={{0,8},{8,16},{16,24},{24,32},{32,40},{40,48},{48,56},{56,64},{64,7... | collective-permute-start | bytes 196616 | tf_op jit(solution)/shard_map/ppermute | solution.py:454
  39.0 0.8 dynamic-slice_bitcast_fusion.names
  39.8 13.4 %collective-permute-done.6.prev = bf16[128,256]{1,0:T(8,128)(2,1)S(1)} collective-permute-done((bf16[128,256]{1,0:T(8,128)(2,1)S(1)}, bf16[128,256]{1,0:T(8,128)(2,1)S(1)}, u32[]{:S(2)}, u32[]{:S(2)}) %collective-permute-start.6) | collective-permute-done | bytes 65568 | tf_op jit(solution)/shard_map/ppermute | solution.py:454
  53.2 1.7 %collective-permute-done.3.f1 = bf16[8,208,128]{2,1,0:T(8,128)(2,1)S(1)} collective-permute-done((bf16[8,208,128]{2,1,0:T(8,128)(2,1)S(1)}, bf16[8,208,128]{2,1,0:T(8,128)(2,1)S(1)}, u32[]{:S(2)}, u32[]{:S(2)}) %collective-permute-start.3) | collective-permute-done | bytes 426016 | tf_op jit(solution)/shard_map/ppermute | solution.py:405
  55.0 5.1 %shard_map.137 = (bf16[512,128]{1,0:T(8,128)(2,1)S(1)}, f32[8,128]{1,0:T(8,128)S(1)}, bf16[128,128]{1,0:T(8,128)(2,1)S(1)}, bf16[37,128,256]{2,1,0:T(8,128)(2,1)S(1)}) custom-call(s32[2]{0:T(128)S(1)} %pad_add_fusion.pos, s32[20,4]{1,0:T(8,128)S(1)} %dynamic-slice_bitcast_fusion.names, bf16[512,128]{1,0:T(8,128)(2,1)S(1)} %bitcast.28, ...), custom_call_target="tpu_custom_call" | custom-call | tf_op jit(solution)/shard_map/pallas_call | solution.py:42
  60.1 0.9 collective-permute-start.7
  61.0 3.1 %collective-permute-done.7.near = bf16[128,128]{1,0:T(8,128)(2,1)S(1)} collective-permute-done((bf16[128,128]{1,0:T(8,128)(2,1)S(1)}, bf16[128,128]{1,0:T(8,128)(2,1)S(1)}, u32[]{:S(2)}, u32[]{:S(2)}) %collective-permute-start.7) | collective-permute-done | bytes 32800 | tf_op jit(solution)/shard_map/ppermute | solution.py:409
  64.1 2.3 %collective-permute-start.8 = (bf16[128,128]{1,0:T(8,128)(2,1)S(1)}, bf16[128,128]{1,0:T(8,128)(2,1)S(1)}, u32[]{:S(2)}, u32[]{:S(2)}) collective-permute-start(bf16[128,128]{1,0:T(8,128)(2,1)S(1)} %add_convert_fusion.x0), channel_id=1, source_target_pairs={{0,16},{8,24},{16,0},{24,8},{1,17},{9,25},{17,1},{25,9},{2,18},{10... | collective-permute-start | bytes 98312 | tf_op jit(solution)/shard_map/ppermute | solution.py:409
  66.5 0.4 shard_map.138
  66.8 2.8 %collective-permute-done.8.x1.pair = bf16[128,128]{1,0:T(8,128)(2,1)S(1)} collective-permute-done((bf16[128,128]{1,0:T(8,128)(2,1)S(1)}, bf16[128,128]{1,0:T(8,128)(2,1)S(1)}, u32[]{:S(2)}, u32[]{:S(2)}) %collective-permute-start.8) | collective-permute-done | bytes 32800 | tf_op jit(solution)/shard_map/ppermute | solution.py:409
  69.7 18.5 %all_to_all.30.zs = bf16[8,128,128]{2,1,0:T(8,128)(2,1)S(1)} all-to-all(bf16[8,128,128]{2,1,0:T(8,128)(2,1)S(1)} %shard_map.139), channel_id=1, replica_groups=mesh['z'=8,'x'=4,'y'=4,'c'=2] {'z'}, dimensions={0} | all-to-all | bytes 524288 | tf_op jit(solution)/shard_map/all_to_all | solution.py:417
  88.1 1.1 shard_map.140
  89.2 0.1 collective-permute-start.9
  89.3 1.2 collective-permute-done.9
  90.4 0.4 collective-permute-start.10
  90.9 3.2 %collective-permute-done.10 = f32[8,128]{1,0:T(8,128)S(1)} collective-permute-done((f32[8,128]{1,0:T(8,128)S(1)}, f32[8,128]{1,0:T(8,128)S(1)}, u32[]{:S(2)}, u32[]{:S(2)}) %collective-permute-start.10) | collective-permute-done | bytes 4128 | tf_op jit(solution)/shard_map/ppermute | solution.py:409
  94.0 2.3 %collective-permute-start.11 = (f32[8,128]{1,0:T(8,128)S(1)}, f32[8,128]{1,0:T(8,128)S(1)}, u32[]{:S(2)}, u32[]{:S(2)}) collective-permute-start(f32[8,128]{1,0:T(8,128)S(1)} %add.19.s0), channel_id=1, source_target_pairs={{0,4},{2,6},{4,0},{6,2},{1,5},{3,7},{5,1},{7,3},{8,12},{10,14},{12... | collective-permute-start | bytes 12296 | tf_op jit(solution)/shard_map/ppermute | solution.py:409
  96.3 2.8 %collective-permute-done.11.s1 = f32[8,128]{1,0:T(8,128)S(1)} collective-permute-done((f32[8,128]{1,0:T(8,128)S(1)}, f32[8,128]{1,0:T(8,128)S(1)}, u32[]{:S(2)}, u32[]{:S(2)}) %collective-permute-start.11) | collective-permute-done | bytes 4128 | tf_op jit(solution)/shard_map/ppermute | solution.py:409
  99.1 0.4 shard_map.141
  99.6 0.1 collective-permute-start.12
  99.7 4.1 %collective-permute-done.12.x1.near = bf16[144,128]{1,0:T(8,128)(2,1)S(1)} collective-permute-done((bf16[144,128]{1,0:T(8,128)(2,1)S(1)}, bf16[144,128]{1,0:T(8,128)(2,1)S(1)}, u32[]{:S(2)}, u32[]{:S(2)}) %collective-permute-start.12) | collective-permute-done | bytes 36896 | tf_op jit(solution)/shard_map/ppermute | solution.py:409
  103.7 0.8 collective-permute-start.13
  104.5 1.7 shard_map.143
  106.2 3.1 %collective-permute-done.13.x1.pair = bf16[144,128]{1,0:T(8,128)(2,1)S(1)} collective-permute-done((bf16[144,128]{1,0:T(8,128)(2,1)S(1)}, bf16[144,128]{1,0:T(8,128)(2,1)S(1)}, u32[]{:S(2)}, u32[]{:S(2)}) %collective-permute-start.13) | collective-permute-done | bytes 36896 | tf_op jit(solution)/shard_map/ppermute | solution.py:409
  109.3 13.2 %all_to_all.31.zs = bf16[8,144,128]{2,1,0:T(8,128)(2,1)S(1)} all-to-all(bf16[8,144,128]{2,1,0:T(8,128)(2,1)S(1)} %shard_map.144), channel_id=1, replica_groups=mesh['z'=8,'x'=4,'y'=4,'c'=2] {'z'}, dimensions={0} | all-to-all | bytes 589824 | tf_op jit(solution)/shard_map/all_to_all | solution.py:417
  122.5 8.0 %shard_map.145 = (bf16[512,128]{1,0:T(8,128)(2,1)}, bf16[512,128]{1,0:T(8,128)(2,1)}, bf16[8,192,128]{2,1,0:T(8,128)(2,1)S(1)}, bf16[8,192,128]{2,1,0:T(8,128)(2...) custom-call(s32[2]{0:T(128)S(1)} %pad_add_fusion.pos, ...), custom_call_target="tpu_custom_call" | custom-call | tf_op jit(solution)/shard_map/pallas_call | solution.py:42
  130.6 0.7 copy-done.8
  131.3 3.6 %all-to-all-start.4 = ((bf16[8,4,64,128]{3,2,1,0:T(8,128)(2,1)}), bf16[8,4,64,128]{3,2,1,0:T(8,128)(2,1)S(1)}, u32[]{:S(2)}, u32[]{:S(2)}) async-start(bf16[8,4,64,128]{3,2,1,0:T(8,128)(2,1)} %get-tuple-element.94), calls=%async_computation.4 | async-start | bytes 1048576 | tf_op jit(solution)/shard_map/all_to_all | solution.py:417
  134.9 1.0 collective-permute-start.15
  136.0 1.0 collective-permute-start.16
  137.0 0.2 collective-permute-start.17
  137.1 7.7 %collective-permute-done.15.a1 = bf16[8,192,128]{2,1,0:T(8,128)(2,1)S(1)} collective-permute-done((bf16[8,192,128]{2,1,0:T(8,128)(2,1)}, bf16[8,192,128]{2,1,0:T(8,128)(2,1)S(1)}, u32[]{:S(2)}, u32[]{:S(2)}) %collective-permute-start.15) | collective-permute-done | bytes 393248 | tf_op jit(solution)/shard_map/ppermute | solution.py:405
  144.8 2.6 %collective-permute-done.16.a2 = bf16[8,192,128]{2,1,0:T(8,128)(2,1)S(1)} collective-permute-done((bf16[8,192,128]{2,1,0:T(8,128)(2,1)}, bf16[8,192,128]{2,1,0:T(8,128)(2,1)S(1)}, u32[]{:S(2)}, u32[]{:S(2)}) %collective-permute-start.16) | collective-permute-done | bytes 393248 | tf_op jit(solution)/shard_map/ppermute | solution.py:405
  147.4 4.1 %collective-permute-done.17.a3 = bf16[8,192,128]{2,1,0:T(8,128)(2,1)S(1)} collective-permute-done((bf16[8,192,128]{2,1,0:T(8,128)(2,1)S(1)}, bf16[8,192,128]{2,1,0:T(8,128)(2,1)S(1)}, u32[]{:S(2)}, u32[]{:S(2)}) %collective-permute-start.17) | collective-permute-done | bytes 393248 | tf_op jit(solution)/shard_map/ppermute | solution.py:405
  151.5 0.9 shard_map.147
  152.4 6.8 %all-to-all-start.5 = ((bf16[8,192,128]{2,1,0:T(8,128)(2,1)}), bf16[8,192,128]{2,1,0:T(8,128)(2,1)S(1)}, u32[]{:S(2)}, u32[]{:S(2)}) async-start(bf16[8,192,128]{2,1,0:T(8,128)(2,1)} %get-tuple-element.95), calls=%async_computation.5 | async-start | bytes 786432 | tf_op jit(solution)/shard_map/all_to_all | solution.py:417
  159.2 1.3 collective-permute-start.14
  160.5 2.3 %collective-permute-start.18 = (bf16[64,128]{1,0:T(8,128)(2,1)S(1)}, bf16[64,128]{1,0:T(8,128)(2,1)S(1)}, u32[]{:S(2)}, u32[]{:S(2)}) collective-permute-start(bf16[64,128]{1,0:T(8,128)(2,1)S(1)} %get-tuple-element.97), channel_id=1, source_target_pairs={{0,24},{8,0},{16,8},{24,16},{1,25},{9,1},{17,9},{25,17},{2,26},{10... | collective-permute-start | bytes 49160 | tf_op jit(solution)/shard_map/ppermute | solution.py:405
  162.8 2.5 %collective-permute-start.19 = (bf16[64,128]{1,0:T(8,128)(2,1)S(1)}, bf16[64,128]{1,0:T(8,128)(2,1)S(1)}, u32[]{:S(2)}, u32[]{:S(2)}) collective-permute-start(bf16[64,128]{1,0:T(8,128)(2,1)S(1)} %get-tuple-element.98), channel_id=1, source_target_pairs={{0,16},{8,24},{16,0},{24,8},{1,17},{9,25},{17,1},{25,9},{2,18},{10... | collective-permute-start | bytes 49160 | tf_op jit(solution)/shard_map/ppermute | solution.py:405
  165.3 0.5 slice.3
  165.8 0.7 shard_map.146
  166.5 1.5 collective-permute-done.19.l2
  168.0 2.2 %collective-permute-done.20.l3 = bf16[64,128]{1,0:T(8,128)(2,1)S(1)} collective-permute-done((bf16[64,128]{1,0:T(8,128)(2,1)S(1)}, bf16[64,128]{1,0:T(8,128)(2,1)S(1)}, u32[]{:S(2)}, u32[]{:S(2)}) %collective-permute-start.20) | collective-permute-done | bytes 16416 | tf_op jit(solution)/shard_map/ppermute | solution.py:405
  170.2 1.1 all-to-all-done.5.top
  171.3 1.4 shard_map.148
  (26 shorter events, 0.1 us)
Async XLA Ops:
  0.6 54.3 %copy-start.5 = (bf16[1,512,128]{2,1,0:T(8,128)(2,1)S(1)}, bf16[1,512,128]{2,1,0:T(8,128)(2,1)}, u32[]{:S(2)}) copy-start(bf16[1,512,128]{2,1,0:T(8,128)(2,1)} %param.10) | copy-start | bytes 393220
  0.6 54.3 %copy-start.4 = (bf16[1,512,128]{2,1,0:T(8,128)(2,1)S(1)}, bf16[1,512,128]{2,1,0:T(8,128)(2,1)}, u32[]{:S(2)}) copy-start(bf16[1,512,128]{2,1,0:T(8,128)(2,1)} %param.9) | copy-start | bytes 393220
  0.7 54.3 %copy-start.1 = (bf16[1,512,128]{2,1,0:T(8,128)(2,1)S(1)}, bf16[1,512,128]{2,1,0:T(8,128)(2,1)}, u32[]{:S(2)}) copy-start(bf16[1,512,128]{2,1,0:T(8,128)(2,1)} %param.12) | copy-start | bytes 393220
  0.7 54.3 %copy-start.3 = (bf16[1,512,128]{2,1,0:T(8,128)(2,1)S(1)}, bf16[1,512,128]{2,1,0:T(8,128)(2,1)}, u32[]{:S(2)}) copy-start(bf16[1,512,128]{2,1,0:T(8,128)(2,1)} %param.8) | copy-start | bytes 393220
  3.3 63.1 %copy-start = (bf16[1,512,128]{2,1,0:T(8,128)(2,1)S(1)}, bf16[1,512,128]{2,1,0:T(8,128)(2,1)}, u32[]{:S(2)}) copy-start(bf16[1,512,128]{2,1,0:T(8,128)(2,1)} %param.11) | copy-start | bytes 393220
  3.3 24.0 %all-to-all-start = ((bf16[8,208,128]{2,1,0:T(8,128)(2,1)}), bf16[8,208,128]{2,1,0:T(8,128)(2,1)S(1)}, u32[]{:S(2)}, u32[]{:S(2)}) async-start(bf16[8,208,128]{2,1,0:T(8,128)(2,1)} %get-tuple-element.57), calls=%async_computation | async-start | bytes 851968 | tf_op jit(solution)/shard_map/all_to_all | solution.py:417
  11.9 4.4 %collective-permute-start.2 = (bf16[48,128]{1,0:T(8,128)(2,1)S(1)}, bf16[48,128]{1,0:T(8,128)(2,1)S(1)}, u32[]{:S(2)}, u32[]{:S(2)}) collective-permute-start(bf16[48,128]{1,0:T(8,128)(2,1)S(1)} %get-tuple-element.58.l0), channel_id=1, source_target_pairs={{0,24},{8,0},{16,8},{24,16},{1,25},{9,1},{17,9},{25,17},{2,26},{10... | collective-permute-start | bytes 36872 | tf_op jit(solution)/shard_map/ppermute | solution.py:405
  14.7 5.2 %collective-permute-start.1 = (bf16[48,128]{1,0:T(8,128)(2,1)S(1)}, bf16[48,128]{1,0:T(8,128)(2,1)S(1)}, u32[]{:S(2)}, u32[]{:S(2)}) collective-permute-start(bf16[48,128]{1,0:T(8,128)(2,1)S(1)} %get-tuple-element.58.l0), channel_id=1, source_target_pairs={{0,16},{8,24},{16,0},{24,8},{1,17},{9,25},{17,1},{25,9},{2,18},{10... | collective-permute-start | bytes 36872 | tf_op jit(solution)/shard_map/ppermute | solution.py:405
  15.5 4.9 %collective-permute-start = (bf16[48,128]{1,0:T(8,128)(2,1)S(1)}, bf16[48,128]{1,0:T(8,128)(2,1)S(1)}, u32[]{:S(2)}, u32[]{:S(2)}) collective-permute-start(bf16[48,128]{1,0:T(8,128)(2,1)S(1)} %get-tuple-element.58.l0), channel_id=1, source_target_pairs={{0,8},{8,16},{16,24},{24,0},{1,9},{9,17},{17,25},{25,1},{2,10},{10... | collective-permute-start | bytes 36872 | tf_op jit(solution)/shard_map/ppermute | solution.py:405
  21.2 66.9 %copy-start.2 = (bf16[1,512,128]{2,1,0:T(8,128)(2,1)S(1)}, bf16[1,512,128]{2,1,0:T(8,128)(2,1)}, u32[]{:S(2)}) copy-start(bf16[1,512,128]{2,1,0:T(8,128)(2,1)} %param.14) | copy-start | bytes 393220
  21.3 66.9 %copy-start.7 = (f32[1,128]{1,0:T(1,128)S(1)}, f32[1,128]{1,0:T(1,128)}, u32[]{:S(2)}) copy-start(f32[1,128]{1,0:T(1,128)} %gain.5) | copy-start | bytes 1540
  27.3 27.6 %all-to-all-start.1 = ((bf16[8,4,48,128]{3,2,1,0:T(8,128)(2,1)}), bf16[8,4,48,128]{3,2,1,0:T(8,128)(2,1)S(1)}, u32[]{:S(2)}, u32[]{:S(2)}) async-start(bf16[8,4,48,128]{3,2,1,0:T(8,128)(2,1)} %shard_map.136), calls=%async_computation.1 | async-start | bytes 786432 | tf_op jit(solution)/shard_map/all_to_all | solution.py:417
  30.8 22.4 %collective-permute-start.5 = (bf16[8,208,128]{2,1,0:T(8,128)(2,1)S(1)}, bf16[8,208,128]{2,1,0:T(8,128)(2,1)S(1)}, u32[]{:S(2)}, u32[]{:S(2)}) collective-permute-start(bf16[8,208,128]{2,1,0:T(8,128)(2,1)S(1)} %all-to-all-done.f0), channel_id=1, source_target_pairs={{0,24},{8,0},{16,8},{24,16},{1,25},{9,1},{17,9},{25,17},{2,26},{10... | collective-permute-start | bytes 1277960 | tf_op jit(solution)/shard_map/ppermute | solution.py:405
  33.6 19.6 %collective-permute-start.4 = (bf16[8,208,128]{2,1,0:T(8,128)(2,1)S(1)}, bf16[8,208,128]{2,1,0:T(8,128)(2,1)S(1)}, u32[]{:S(2)}, u32[]{:S(2)}) collective-permute-start(bf16[8,208,128]{2,1,0:T(8,128)(2,1)S(1)} %all-to-all-done.f0), channel_id=1, source_target_pairs={{0,16},{8,24},{16,0},{24,8},{1,17},{9,25},{17,1},{25,9},{2,18},{10... | collective-permute-start | bytes 1277960 | tf_op jit(solution)/shard_map/ppermute | solution.py:405
  34.4 20.5 %collective-permute-start.3 = (bf16[8,208,128]{2,1,0:T(8,128)(2,1)S(1)}, bf16[8,208,128]{2,1,0:T(8,128)(2,1)S(1)}, u32[]{:S(2)}, u32[]{:S(2)}) collective-permute-start(bf16[8,208,128]{2,1,0:T(8,128)(2,1)S(1)} %all-to-all-done.f0), channel_id=1, source_target_pairs={{0,8},{8,16},{16,24},{24,0},{1,9},{9,17},{17,25},{25,1},{2,10},{10... | collective-permute-start | bytes 1277960 | tf_op jit(solution)/shard_map/ppermute | solution.py:405
  35.3 17.9 %collective-permute-start.6 = (bf16[128,256]{1,0:T(8,128)(2,1)S(1)}, bf16[128,256]{1,0:T(8,128)(2,1)S(1)}, u32[]{:S(2)}, u32[]{:S(2)}) collective-permute-start(bf16[128,256]{1,0:T(8,128)(2,1)S(1)} %get-tuple-element.61), channel_id=1, source_target_pairs={{0,8},{8,16},{16,24},{24,32},{32,40},{40,48},{48,56},{56,64},{64,7... | collective-permute-start | bytes 196616 | tf_op jit(solution)/shard_map/ppermute | solution.py:454
  60.1 4.0 %collective-permute-start.7 = (bf16[128,128]{1,0:T(8,128)(2,1)S(1)}, bf16[128,128]{1,0:T(8,128)(2,1)S(1)}, u32[]{:S(2)}, u32[]{:S(2)}) collective-permute-start(bf16[128,128]{1,0:T(8,128)(2,1)S(1)} %get-tuple-element.62), channel_id=1, source_target_pairs={{0,8},{8,0},{16,24},{24,16},{1,9},{9,1},{17,25},{25,17},{2,10},{10... | collective-permute-start | bytes 98312 | tf_op jit(solution)/shard_map/ppermute | solution.py:409
  64.1 5.5 %collective-permute-start.8 = (bf16[128,128]{1,0:T(8,128)(2,1)S(1)}, bf16[128,128]{1,0:T(8,128)(2,1)S(1)}, u32[]{:S(2)}, u32[]{:S(2)}) collective-permute-start(bf16[128,128]{1,0:T(8,128)(2,1)S(1)} %add_convert_fusion.x0), channel_id=1, source_target_pairs={{0,16},{8,24},{16,0},{24,8},{1,17},{9,25},{17,1},{25,9},{2,18},{10... | collective-permute-start | bytes 98312 | tf_op jit(solution)/shard_map/ppermute | solution.py:409
  89.2 1.2 collective-permute-start.9
  90.4 3.6 %collective-permute-start.10 = (f32[8,128]{1,0:T(8,128)S(1)}, f32[8,128]{1,0:T(8,128)S(1)}, u32[]{:S(2)}, u32[]{:S(2)}) collective-permute-start(f32[8,128]{1,0:T(8,128)S(1)} %add.18), channel_id=1, source_target_pairs={{0,2},{2,0},{4,6},{6,4},{1,3},{3,1},{5,7},{7,5},{8,10},{10,8},{12,... | collective-permute-start | bytes 12296 | tf_op jit(solution)/shard_map/ppermute | solution.py:409
  94.0 5.1 %collective-permute-start.11 = (f32[8,128]{1,0:T(8,128)S(1)}, f32[8,128]{1,0:T(8,128)S(1)}, u32[]{:S(2)}, u32[]{:S(2)}) collective-permute-start(f32[8,128]{1,0:T(8,128)S(1)} %add.19.s0), channel_id=1, source_target_pairs={{0,4},{2,6},{4,0},{6,2},{1,5},{3,7},{5,1},{7,3},{8,12},{10,14},{12... | collective-permute-start | bytes 12296 | tf_op jit(solution)/shard_map/ppermute | solution.py:409
  99.6 4.2 %collective-permute-start.12 = (bf16[144,128]{1,0:T(8,128)(2,1)S(1)}, bf16[144,128]{1,0:T(8,128)(2,1)S(1)}, u32[]{:S(2)}, u32[]{:S(2)}) collective-permute-start(bf16[144,128]{1,0:T(8,128)(2,1)S(1)} %get-tuple-element.71.x0), channel_id=1, source_target_pairs={{0,8},{8,0},{16,24},{24,16},{1,9},{9,1},{17,25},{25,17},{2,10},{10... | collective-permute-start | bytes 110600 | tf_op jit(solution)/shard_map/ppermute | solution.py:409
  103.7 5.5 %collective-permute-start.13 = (bf16[144,128]{1,0:T(8,128)(2,1)S(1)}, bf16[144,128]{1,0:T(8,128)(2,1)S(1)}, u32[]{:S(2)}, u32[]{:S(2)}) collective-permute-start(bf16[144,128]{1,0:T(8,128)(2,1)S(1)} %shard_map.142.x0), channel_id=1, source_target_pairs={{0,16},{8,24},{16,0},{24,8},{1,17},{9,25},{17,1},{25,9},{2,18},{10... | collective-permute-start | bytes 110600 | tf_op jit(solution)/shard_map/ppermute | solution.py:409
  130.5 0.8 copy-start.8
  131.3 34.5 %copy-start.6 = (s32[128,20]{0,1:T(8,128)S(1)}, s32[128,20]{0,1:T(8,128)}, u32[]{:S(2)}) copy-start(s32[128,20]{0,1:T(8,128)} %param.15) | copy-start | bytes 30724
  131.3 20.2 %all-to-all-start.4 = ((bf16[8,4,64,128]{3,2,1,0:T(8,128)(2,1)}), bf16[8,4,64,128]{3,2,1,0:T(8,128)(2,1)S(1)}, u32[]{:S(2)}, u32[]{:S(2)}) async-start(bf16[8,4,64,128]{3,2,1,0:T(8,128)(2,1)} %get-tuple-element.94), calls=%async_computation.4 | async-start | bytes 1048576 | tf_op jit(solution)/shard_map/all_to_all | solution.py:417
  134.9 9.9 %collective-permute-start.15 = (bf16[8,192,128]{2,1,0:T(8,128)(2,1)}, bf16[8,192,128]{2,1,0:T(8,128)(2,1)S(1)}, u32[]{:S(2)}, u32[]{:S(2)}) collective-permute-start(bf16[8,192,128]{2,1,0:T(8,128)(2,1)} %get-tuple-element.91), channel_id=1, source_target_pairs={{0,24},{8,0},{16,8},{24,16},{1,25},{9,1},{17,9},{25,17},{2,26},{10... | collective-permute-start | bytes 1179656 | tf_op jit(solution)/shard_map/ppermute | solution.py:405
  136.0 11.5 %collective-permute-start.16 = (bf16[8,192,128]{2,1,0:T(8,128)(2,1)}, bf16[8,192,128]{2,1,0:T(8,128)(2,1)S(1)}, u32[]{:S(2)}, u32[]{:S(2)}) collective-permute-start(bf16[8,192,128]{2,1,0:T(8,128)(2,1)} %copy-done.8), channel_id=1, source_target_pairs={{0,16},{8,24},{16,0},{24,8},{1,17},{9,25},{17,1},{25,9},{2,18},{10... | collective-permute-start | bytes 1179656 | tf_op jit(solution)/shard_map/ppermute | solution.py:405
  137.0 14.5 %collective-permute-start.17 = (bf16[8,192,128]{2,1,0:T(8,128)(2,1)S(1)}, bf16[8,192,128]{2,1,0:T(8,128)(2,1)S(1)}, u32[]{:S(2)}, u32[]{:S(2)}) collective-permute-start(bf16[8,192,128]{2,1,0:T(8,128)(2,1)S(1)} %get-tuple-element.93), channel_id=1, source_target_pairs={{0,8},{8,16},{16,24},{24,0},{1,9},{9,17},{17,25},{25,1},{2,10},{10... | collective-permute-start | bytes 1179656 | tf_op jit(solution)/shard_map/ppermute | solution.py:405
  152.4 18.9 %all-to-all-start.5 = ((bf16[8,192,128]{2,1,0:T(8,128)(2,1)}), bf16[8,192,128]{2,1,0:T(8,128)(2,1)S(1)}, u32[]{:S(2)}, u32[]{:S(2)}) async-start(bf16[8,192,128]{2,1,0:T(8,128)(2,1)} %get-tuple-element.95), calls=%async_computation.5 | async-start | bytes 786432 | tf_op jit(solution)/shard_map/all_to_all | solution.py:417
  159.2 7.3 %collective-permute-start.14 = (bf16[128,256]{1,0:T(8,128)(2,1)S(1)}, bf16[128,256]{1,0:T(8,128)(2,1)S(1)}, u32[]{:S(2)}, u32[]{:S(2)}) collective-permute-start(bf16[128,256]{1,0:T(8,128)(2,1)S(1)} %get-tuple-element.89), channel_id=1, source_target_pairs={{8,0},{16,8},{24,16},{32,24},{40,32},{48,40},{56,48},{64,56},{72,6... | collective-permute-start | bytes 196616 | tf_op jit(solution)/shard_map/ppermute | solution.py:540
  160.5 6.0 %collective-permute-start.18 = (bf16[64,128]{1,0:T(8,128)(2,1)S(1)}, bf16[64,128]{1,0:T(8,128)(2,1)S(1)}, u32[]{:S(2)}, u32[]{:S(2)}) collective-permute-start(bf16[64,128]{1,0:T(8,128)(2,1)S(1)} %get-tuple-element.97), channel_id=1, source_target_pairs={{0,24},{8,0},{16,8},{24,16},{1,25},{9,1},{17,9},{25,17},{2,26},{10... | collective-permute-start | bytes 49160 | tf_op jit(solution)/shard_map/ppermute | solution.py:405
  162.8 5.2 %collective-permute-start.19 = (bf16[64,128]{1,0:T(8,128)(2,1)S(1)}, bf16[64,128]{1,0:T(8,128)(2,1)S(1)}, u32[]{:S(2)}, u32[]{:S(2)}) collective-permute-start(bf16[64,128]{1,0:T(8,128)(2,1)S(1)} %get-tuple-element.98), channel_id=1, source_target_pairs={{0,16},{8,24},{16,0},{24,8},{1,17},{9,25},{17,1},{25,9},{2,18},{10... | collective-permute-start | bytes 49160 | tf_op jit(solution)/shard_map/ppermute | solution.py:405
  165.3 4.9 %collective-permute-start.20 = (bf16[64,128]{1,0:T(8,128)(2,1)S(1)}, bf16[64,128]{1,0:T(8,128)(2,1)S(1)}, u32[]{:S(2)}, u32[]{:S(2)}) collective-permute-start(bf16[64,128]{1,0:T(8,128)(2,1)S(1)} %get-tuple-element.99), channel_id=1, source_target_pairs={{0,8},{8,16},{16,24},{24,0},{1,9},{9,17},{17,25},{25,1},{2,10},{10... | collective-permute-start | bytes 49160 | tf_op jit(solution)/shard_map/ppermute | solution.py:405

commit v5 on v3

--- a/solution.py
+++ b/solution.py
@@ -25,6 +25,9 @@
 PREV = FAR + 4
 HALF = 64
 TOP = 192
+REST = 48
+FIRST = 208
+MOST = FIRST - BLK
 SENT = 144
 POOL = FAR + 5
 
@@ -78,11 +81,11 @@
     pairs = []
     for i in range(NZ):
         pairs.append((keys.at[mine], top.at[i, pl.ds(0, BLK)]))
-        pairs.append((values.at[mine, pl.ds(0, HALF)], top.at[i, pl.ds(BLK, HALF)]))
+        pairs.append((values.at[mine, pl.ds(0, MOST)], top.at[i, pl.ds(BLK, MOST)]))
     copies = [pltpu.make_async_copy(a, b, sems.at[i]) for i, (a, b) in enumerate(pairs)]
     for c in copies:
         c.start()
-    low[...] = values[mine, HALF:, :]
+    low[...] = values[mine, MOST:, :]
     last[:, 0:BLK] = keys[3]
     last[:, BLK:] = values[3]
     for c in copies:
@@ -118,8 +121,8 @@
     for j, f in enumerate(far):
         spot = pl.ds(NZ * j, NZ)
         pairs.append((f.at[:, pl.ds(0, BLK)], pool.at[spot, :, left]))
-        pairs.append((f.at[:, pl.ds(BLK, HALF)], pool.at[spot, pl.ds(0, HALF), right]))
-        pairs.append((low.at[:, j], pool.at[spot, pl.ds(HALF, HALF), right]))
+        pairs.append((f.at[:, pl.ds(BLK, MOST)], pool.at[spot, pl.ds(0, MOST), right]))
+        pairs.append((low.at[:, j], pool.at[spot, pl.ds(MOST, REST), right]))
     return pairs
 
 
@@ -162,7 +165,7 @@
         lse[pl.ds(b, 1), :] = as_row(row_max + jnp.log(total))
         return carry
 
-    lax.fori_loop(0, 4, block, 0)
+    lax.fori_loop(0, 4, block, 0, unroll=4)
     state[...] = mm(lk[...], att[...], TN).astype(bf16)
 
 
@@ -276,7 +279,7 @@
 def backward_kernel(pos, names, q, lse, att, lk, dlk_in, gatt_in, local,
                     x0, x1, x2, x3, zs, pool,
                     dlk, dq, o0, o1, o2, o3, olow, own, back, ggain,
-                    acc, gatt, delta, near, lows, sems):
+                    acc, gatt, delta, dlk_buf, dq_buf, far_buf, lows, sems):
     nsel = names.shape[0]
     scale = BLK ** (-0.5)
     later = jnp.zeros((BLK, BLK), f32)
@@ -290,12 +293,14 @@
     for b in range(4):
         r = slice(b * BLK, (b + 1) * BLK)
         after = (later + local[b]).astype(bf16)
-        dlk[r] = (dlk_in[r] + mm(att[r], after, NT)).astype(bf16)
+        dlk_buf[r] = (dlk_in[r] + mm(att[r], after, NT)).astype(bf16)
         g = (gatt_in[r] + mm(lk[r], after)).astype(bf16)
         gatt[r] = g
         delta[b : b + 1] = as_row(
             jnp.sum(g.astype(f32) * att[r].astype(f32), axis=1, keepdims=True)
         )
+    copies = [pltpu.make_async_copy(dlk_buf, dlk, sems.at[0])]
+    copies[0].start()
     acc[...] = jnp.zeros(acc.shape, f32)
 
     def block(b, carry):
@@ -328,20 +333,24 @@
             dqb = dqb + mm(ds, keyval[:, 0:BLK], TN)
             for i, (spot, _) in enumerate(spots):
                 acc[spot] += grads[i * BLK : (i + 1) * BLK]
-        dq[rows(b), :] = (dqb * scale).astype(bf16)
+        dq_buf[rows(b), :] = (dqb * scale).astype(bf16)
         return carry
 
-    lax.fori_loop(0, 4, block, 0)
+    lax.fori_loop(0, 4, block, 0, unroll=4)
+
+    def send(src, dst):
+        copies.append(pltpu.make_async_copy(src, dst, sems.at[len(copies)]))
+        copies[-1].start()
+
+    send(dq_buf, dq)
+    for j, o in ((1, o1), (2, o2), (3, o3), (0, o0)):
+        spot = slice(NZ * j, NZ * (j + 1))
+        far_buf[j, :, 0:BLK] = (acc[spot, :, 0:BLK] * scale).astype(bf16)
+        far_buf[j, :, BLK:] = acc[spot, 0:HALF, BLK:].astype(bf16)
+        send(far_buf.at[j], o)
     for j in range(NX):
         lows[:, j] = acc[NZ * j : NZ * (j + 1), HALF:, BLK:].astype(bf16)
-    near[:, 0:BLK] = (acc[0:NZ, :, 0:BLK] * scale).astype(bf16)
-    near[:, BLK:] = acc[0:NZ, 0:HALF, BLK:].astype(bf16)
-    copies = [pltpu.make_async_copy(lows, olow, sems.at[0]), pltpu.make_async_copy(near, o0, sems.at[1])]
-    for c in copies:
-        c.start()
-    for j, o in ((1, o1), (2, o2), (3, o3)):
-        o[:, 0:BLK] = (acc[NZ * j : NZ * (j + 1), :, 0:BLK] * scale).astype(bf16)
-        o[:, BLK:] = acc[NZ * j : NZ * (j + 1), 0:HALF, BLK:].astype(bf16)
+    send(lows, olow)
     own[:, :, 0:BLK] = acc[OWN : OWN + 4, :, 0:BLK] * scale
     own[:, :, BLK:] = acc[OWN : OWN + 4, :, BLK:]
     back[:, 0:BLK] = (acc[PREV, :, 0:BLK] * scale).astype(bf16)
@@ -426,7 +435,7 @@
 
     tops, low, last = call(
         pick_kernel,
-        [((NZ, TOP, width), bf16), ((HALF, width), bf16), ((BLK, 2 * BLK), bf16)],
+        [((NZ, FIRST, width), bf16), ((REST, width), bf16), ((BLK, 2 * BLK), bf16)],
         (pos, in_hbm(key_block), in_hbm(k4), in_hbm(v4)),
         [SM, HB, HB, HB],
         [
@@ -441,10 +450,10 @@
     lows = [low] + [turn(low, "x", NX, j) for j in range(1, NX)]
     (lows,) = call(
         spread_kernel,
-        [((NZ, NX, HALF, width), bf16)],
+        [((NZ, NX, REST, width), bf16)],
         lows,
         [VM] * 4,
-        [pltpu.VMEM((NX, HALF, width), bf16), pltpu.SemaphoreType.DMA((NZ,))],
+        [pltpu.VMEM((NX, REST, width), bf16), pltpu.SemaphoreType.DMA((NZ,))],
         [HB],
     )
     tops = swap(tops)
@@ -505,11 +514,13 @@
             pltpu.VMEM((POOL, BLK, 2 * BLK), f32),
             pltpu.VMEM((512, width), bf16),
             pltpu.VMEM((8, BLK), f32),
-            pltpu.VMEM((NZ, TOP, width), bf16),
+            pltpu.VMEM((512, width), bf16),
+            pltpu.VMEM((512, width), bf16),
+            pltpu.VMEM((NX, NZ, TOP, width), bf16),
             pltpu.VMEM((NZ, NX, HALF, width), bf16),
-            pltpu.SemaphoreType.DMA((2,)),
+            pltpu.SemaphoreType.DMA((NX + 3,)),
         ],
-        [VM, VM, HB, VM, VM, VM, HB, VM, VM, VM],
+        [HB] * 7 + [VM, VM, VM],
         vmem=24,
     )
     dlk, dq = outs[0], outs[1]

time: 168 us -> 169 us (level)
  Pallas kernels: 23.2 us -> 21.5 us
  transfers between devices with their start and end apart: 28 -> 28, of which waited for: 17 -> 17; matrix products, arithmetic and copies ran while one was open for 0% -> 1% of each run, Pallas kernels for 2% -> 2%
where the time goes in v5:
time: 169 us; the launch traced here: 168 us
  starting transfers between devices  57.4 us (34%)
  waiting for transfers between devices  55.2 us (33%)
  blocking collectives  30.6 us (18%)
  Pallas kernels  21.5 us (13%)
  local copies, waits for them, and re-layouts  2.07 us (1%)
    ppermute x22, waiting for transfers between devices, turn(): lax.ppermute(value, axis, [(i, (i + by) % size) for i in range(size)])  33.4 us
    all_to_all x2, blocking collectives, swap(): return lax.all_to_all(value, 'z', 0, 0, tiled=True)  30.6 us
    ppermute x22, starting transfers between devices, turn(): lax.ppermute(value, axis, [(i, (i + by) % size) for i in range(size)])  30 us
    all_to_all x4, starting transfers between devices, swap(): return lax.all_to_all(value, 'z', 0, 0, tiled=True)  22.5 us
    pallas_call x13, Pallas kernels, call(): pl.pallas_call(body, out_shape=[jax.ShapeDtypeStruct(s, d) for s, d in ou...  21.5 us
    ppermute x1, waiting for transfers between devices, per_device(): prev = lax.ppermute(last, seq, [(i, i + 1) for i in range(NZ * NX - 1)])  13.4 us
    all_to_all x4, waiting for transfers between devices, swap(): return lax.all_to_all(value, 'z', 0, 0, tiled=True)  8.39 us
    ppermute x1, starting transfers between devices, per_device(): prev = lax.ppermute(last, seq, [(i, i + 1) for i in range(NZ * NX - 1)])  3.7 us
  transfers between devices with their start and end apart: 28, of which 17 were waited for; matrix products, arithmetic and copies ran while one was open for 1% of the time, Pallas kernels for 2%

profile of v5, /device:TPU:8, one launch (start us, length us, event | category | flops | bytes accessed | tf_op | source)
XLA Modules:
  0.0 167.7 jit_solution(2291332987677091256)
XLA Ops:
  0.6 0.0 copy-start.5
  0.6 0.0 copy-start.4
  0.7 0.1 pad_add_fusion.pos
  0.8 2.6 %shard_map.135 = (bf16[8,208,128]{2,1,0:T(8,128)(2,1)}, bf16[48,128]{1,0:T(8,128)(2,1)S(1)}, bf16[128,256]{1,0:T(8,128)(2,1)S(1)}) custom-call(s32[2]{0:T(128)S(1)} %pad_add_fusion.pos, s32[20,128]{1,0:T(8,128)} %bitcast.34, bf16[4,128,128]{2,1,0:T(8,128)(2,1)} %bitcast.30, bf16[4,128,128]{2,1,0:T(8,128)(2,1)} %bitcast.32), custom_call_target="tpu_custom_call" | custom-call | tf_op jit(solution)/shard_map/pallas_call | solution.py:42
  3.3 8.6 %all-to-all-start = ((bf16[8,208,128]{2,1,0:T(8,128)(2,1)}), bf16[8,208,128]{2,1,0:T(8,128)(2,1)S(1)}, u32[]{:S(2)}, u32[]{:S(2)}) async-start(bf16[8,208,128]{2,1,0:T(8,128)(2,1)} %get-tuple-element.63), calls=%async_computation | async-start | bytes 851968 | tf_op jit(solution)/shard_map/all_to_all | solution.py:412
  12.0 2.8 %collective-permute-start.2 = (bf16[48,128]{1,0:T(8,128)(2,1)S(1)}, bf16[48,128]{1,0:T(8,128)(2,1)S(1)}, u32[]{:S(2)}, u32[]{:S(2)}) collective-permute-start(bf16[48,128]{1,0:T(8,128)(2,1)S(1)} %get-tuple-element.64.l0), channel_id=1, source_target_pairs={{0,24},{8,0},{16,8},{24,16},{1,25},{9,1},{17,9},{25,17},{2,26},{10... | collective-permute-start | bytes 36872 | tf_op jit(solution)/shard_map/ppermute | solution.py:404
  14.7 0.8 collective-permute-start.1
  15.5 0.9 collective-permute-start
  16.4 3.5 %collective-permute-done.1.l2 = bf16[48,128]{1,0:T(8,128)(2,1)S(1)} collective-permute-done((bf16[48,128]{1,0:T(8,128)(2,1)S(1)}, bf16[48,128]{1,0:T(8,128)(2,1)S(1)}, u32[]{:S(2)}, u32[]{:S(2)}) %collective-permute-start.1) | collective-permute-done | bytes 12320 | tf_op jit(solution)/shard_map/ppermute | solution.py:404
  19.9 0.5 collective-permute-done.l1
  20.4 0.8 shard_map.136
  21.3 0.0 copy-start.7
  21.3 6.1 %all-to-all-done.f0 = bf16[8,208,128]{2,1,0:T(8,128)(2,1)S(1)} async-done(((bf16[8,208,128]{2,1,0:T(8,128)(2,1)}), bf16[8,208,128]{2,1,0:T(8,128)(2,1)S(1)}, u32[]{:S(2)}, u32[]{:S(2)}) %all-to-all-start) | async-done | bytes 426016 | tf_op jit(solution)/shard_map/all_to_all | solution.py:412
  27.3 3.5 %all-to-all-start.1 = ((bf16[8,4,48,128]{3,2,1,0:T(8,128)(2,1)}), bf16[8,4,48,128]{3,2,1,0:T(8,128)(2,1)S(1)}, u32[]{:S(2)}, u32[]{:S(2)}) async-start(bf16[8,4,48,128]{3,2,1,0:T(8,128)(2,1)} %shard_map.136), calls=%async_computation.1 | async-start | bytes 786432 | tf_op jit(solution)/shard_map/all_to_all | solution.py:412
  30.8 2.8 %collective-permute-start.5 = (bf16[8,208,128]{2,1,0:T(8,128)(2,1)S(1)}, bf16[8,208,128]{2,1,0:T(8,128)(2,1)S(1)}, u32[]{:S(2)}, u32[]{:S(2)}) collective-permute-start(bf16[8,208,128]{2,1,0:T(8,128)(2,1)S(1)} %all-to-all-done.f0), channel_id=1, source_target_pairs={{0,24},{8,0},{16,8},{24,16},{1,25},{9,1},{17,9},{25,17},{2,26},{10... | collective-permute-start | bytes 1277960 | tf_op jit(solution)/shard_map/ppermute | solution.py:404
  33.6 0.8 collective-permute-start.4
  34.4 0.9 collective-permute-start.3
  35.3 3.7 %collective-permute-start.6 = (bf16[128,256]{1,0:T(8,128)(2,1)S(1)}, bf16[128,256]{1,0:T(8,128)(2,1)S(1)}, u32[]{:S(2)}, u32[]{:S(2)}) collective-permute-start(bf16[128,256]{1,0:T(8,128)(2,1)S(1)} %get-tuple-element.67), channel_id=1, source_target_pairs={{0,8},{8,16},{16,24},{24,32},{32,40},{40,48},{48,56},{56,64},{64,7... | collective-permute-start | bytes 196616 | tf_op jit(solution)/shard_map/ppermute | solution.py:449
  39.0 0.8 dynamic-slice_bitcast_fusion.names
  39.8 13.4 %collective-permute-done.6.prev = bf16[128,256]{1,0:T(8,128)(2,1)S(1)} collective-permute-done((bf16[128,256]{1,0:T(8,128)(2,1)S(1)}, bf16[128,256]{1,0:T(8,128)(2,1)S(1)}, u32[]{:S(2)}, u32[]{:S(2)}) %collective-permute-start.6) | collective-permute-done | bytes 65568 | tf_op jit(solution)/shard_map/ppermute | solution.py:449
  53.2 1.7 %collective-permute-done.3.f1 = bf16[8,208,128]{2,1,0:T(8,128)(2,1)S(1)} collective-permute-done((bf16[8,208,128]{2,1,0:T(8,128)(2,1)S(1)}, bf16[8,208,128]{2,1,0:T(8,128)(2,1)S(1)}, u32[]{:S(2)}, u32[]{:S(2)}) %collective-permute-start.3) | collective-permute-done | bytes 426016 | tf_op jit(solution)/shard_map/ppermute | solution.py:404
  55.0 4.2 %shard_map.137 = (bf16[512,128]{1,0:T(8,128)(2,1)S(1)}, f32[8,128]{1,0:T(8,128)S(1)}, bf16[128,128]{1,0:T(8,128)(2,1)S(1)}, bf16[37,128,256]{2,1,0:T(8,128)(2,1)S(1)}) custom-call(s32[2]{0:T(128)S(1)} %pad_add_fusion.pos, s32[20,4]{1,0:T(8,128)S(1)} %dynamic-slice_bitcast_fusion.names, bf16[512,128]{1,0:T(8,128)(2,1)S(1)} %bitcast.28, ...), custom_call_target="tpu_custom_call" | custom-call | tf_op jit(solution)/shard_map/pallas_call | solution.py:42
  59.2 2.1 %collective-permute-start.9 = (bf16[128,128]{1,0:T(8,128)(2,1)S(1)}, bf16[128,128]{1,0:T(8,128)(2,1)S(1)}, u32[]{:S(2)}, u32[]{:S(2)}) collective-permute-start(bf16[128,128]{1,0:T(8,128)(2,1)S(1)} %get-tuple-element.74.x0), channel_id=1, source_target_pairs={{0,24},{8,0},{16,8},{24,16},{1,25},{9,1},{17,9},{25,17},{2,26},{10... | collective-permute-start | bytes 98312 | tf_op jit(solution)/shard_map/ppermute | solution.py:404
  61.4 0.8 collective-permute-start.8
  62.2 0.8 collective-permute-start.7
  63.0 0.4 shard_map.138
  63.4 3.4 %collective-permute-done.8.x2 = bf16[128,128]{1,0:T(8,128)(2,1)S(1)} collective-permute-done((bf16[128,128]{1,0:T(8,128)(2,1)S(1)}, bf16[128,128]{1,0:T(8,128)(2,1)S(1)}, u32[]{:S(2)}, u32[]{:S(2)}) %collective-permute-start.8) | collective-permute-done | bytes 32800 | tf_op jit(solution)/shard_map/ppermute | solution.py:404
  66.8 0.5 collective-permute-done.7.x1
  67.3 17.4 %all_to_all.30.zs = bf16[8,128,128]{2,1,0:T(8,128)(2,1)S(1)} all-to-all(bf16[8,128,128]{2,1,0:T(8,128)(2,1)S(1)} %shard_map.139), channel_id=1, replica_groups=mesh['z'=8,'x'=4,'y'=4,'c'=2] {'z'}, dimensions={0} | all-to-all | bytes 524288 | tf_op jit(solution)/shard_map/all_to_all | solution.py:412
  84.7 1.1 shard_map.140
  85.8 0.1 collective-permute-start.10
  85.8 1.2 collective-permute-done.10
  87.0 0.5 collective-permute-start.13
  87.4 2.6 %collective-permute-start.12 = (f32[8,128]{1,0:T(8,128)S(1)}, f32[8,128]{1,0:T(8,128)S(1)}, u32[]{:S(2)}, u32[]{:S(2)}) collective-permute-start(f32[8,128]{1,0:T(8,128)S(1)} %add.11.s0), channel_id=1, source_target_pairs={{0,4},{2,6},{4,0},{6,2},{1,5},{3,7},{5,1},{7,3},{8,12},{10,14},{12... | collective-permute-start | bytes 12296 | tf_op jit(solution)/shard_map/ppermute | solution.py:404
  90.0 1.9 %collective-permute-start.11 = (f32[8,128]{1,0:T(8,128)S(1)}, f32[8,128]{1,0:T(8,128)S(1)}, u32[]{:S(2)}, u32[]{:S(2)}) collective-permute-start(f32[8,128]{1,0:T(8,128)S(1)} %add.11.s0), channel_id=1, source_target_pairs={{0,2},{2,4},{4,6},{6,0},{1,3},{3,5},{5,7},{7,1},{8,10},{10,12},{12... | collective-permute-start | bytes 12296 | tf_op jit(solution)/shard_map/ppermute | solution.py:404
  91.9 0.6 collective-permute-done.12.s2
  92.6 1.1 collective-permute-done.11.s1
  93.6 0.4 shard_map.141
  94.1 0.8 collective-permute-start.16
  94.8 2.7 %collective-permute-start.15 = (bf16[144,128]{1,0:T(8,128)(2,1)S(1)}, bf16[144,128]{1,0:T(8,128)(2,1)S(1)}, u32[]{:S(2)}, u32[]{:S(2)}) collective-permute-start(bf16[144,128]{1,0:T(8,128)(2,1)S(1)} %get-tuple-element.93.x0), channel_id=1, source_target_pairs={{0,16},{8,24},{16,0},{24,8},{1,17},{9,25},{17,1},{25,9},{2,18},{10... | collective-permute-start | bytes 110600 | tf_op jit(solution)/shard_map/ppermute | solution.py:404
  97.5 0.9 collective-permute-start.14
  98.4 1.7 shard_map.142
  100.1 0.2 collective-permute-done.15.x2
  100.3 1.2 collective-permute-done.14.x1
  101.5 13.2 %all_to_all.31.zs = bf16[8,144,128]{2,1,0:T(8,128)(2,1)S(1)} all-to-all(bf16[8,144,128]{2,1,0:T(8,128)(2,1)S(1)} %shard_map.143), channel_id=1, replica_groups=mesh['z'=8,'x'=4,'y'=4,'c'=2] {'z'}, dimensions={0} | all-to-all | bytes 589824 | tf_op jit(solution)/shard_map/all_to_all | solution.py:412
  114.7 7.3 %shard_map.144 = (bf16[512,128]{1,0:T(8,128)(2,1)}, bf16[512,128]{1,0:T(8,128)(2,1)}, bf16[8,192,128]{2,1,0:T(8,128)(2,1)S(1)}, bf16[8,192,128]{2,1,0:T(8,128)(2...) custom-call(s32[2]{0:T(128)S(1)} %pad_add_fusion.pos, ...), custom_call_target="tpu_custom_call" | custom-call | tf_op jit(solution)/shard_map/pallas_call | solution.py:42
  122.0 0.7 copy-done.8
  122.8 3.6 %all-to-all-start.4 = ((bf16[8,4,64,128]{3,2,1,0:T(8,128)(2,1)}), bf16[8,4,64,128]{3,2,1,0:T(8,128)(2,1)S(1)}, u32[]{:S(2)}, u32[]{:S(2)}) async-start(bf16[8,4,64,128]{3,2,1,0:T(8,128)(2,1)} %get-tuple-element.106), calls=%async_computation.4 | async-start | bytes 1048576 | tf_op jit(solution)/shard_map/all_to_all | solution.py:412
  126.4 2.2 %collective-permute-start.18 = (bf16[8,192,128]{2,1,0:T(8,128)(2,1)}, bf16[8,192,128]{2,1,0:T(8,128)(2,1)S(1)}, u32[]{:S(2)}, u32[]{:S(2)}) collective-permute-start(bf16[8,192,128]{2,1,0:T(8,128)(2,1)} %get-tuple-element.103), channel_id=1, source_target_pairs={{0,24},{8,0},{16,8},{24,16},{1,25},{9,1},{17,9},{25,17},{2,26},{10... | collective-permute-start | bytes 1179656 | tf_op jit(solution)/shard_map/ppermute | solution.py:404
  128.6 0.7 collective-permute-start.19
  129.3 0.3 collective-permute-start.20
  129.6 12.3 %collective-permute-done.18.a1 = bf16[8,192,128]{2,1,0:T(8,128)(2,1)S(1)} collective-permute-done((bf16[8,192,128]{2,1,0:T(8,128)(2,1)}, bf16[8,192,128]{2,1,0:T(8,128)(2,1)S(1)}, u32[]{:S(2)}, u32[]{:S(2)}) %collective-permute-start.18) | collective-permute-done | bytes 393248 | tf_op jit(solution)/shard_map/ppermute | solution.py:404
  141.8 3.4 %collective-permute-done.20.a3 = bf16[8,192,128]{2,1,0:T(8,128)(2,1)S(1)} collective-permute-done((bf16[8,192,128]{2,1,0:T(8,128)(2,1)S(1)}, bf16[8,192,128]{2,1,0:T(8,128)(2,1)S(1)}, u32[]{:S(2)}, u32[]{:S(2)}) %collective-permute-start.20) | collective-permute-done | bytes 393248 | tf_op jit(solution)/shard_map/ppermute | solution.py:404
  145.3 0.9 shard_map.146
  146.2 6.8 %all-to-all-start.5 = ((bf16[8,192,128]{2,1,0:T(8,128)(2,1)}), bf16[8,192,128]{2,1,0:T(8,128)(2,1)S(1)}, u32[]{:S(2)}, u32[]{:S(2)}) async-start(bf16[8,192,128]{2,1,0:T(8,128)(2,1)} %get-tuple-element.107), calls=%async_computation.5 | async-start | bytes 786432 | tf_op jit(solution)/shard_map/all_to_all | solution.py:412
  153.0 1.3 collective-permute-start.17
  154.3 2.0 %collective-permute-start.21 = (bf16[64,128]{1,0:T(8,128)(2,1)S(1)}, bf16[64,128]{1,0:T(8,128)(2,1)S(1)}, u32[]{:S(2)}, u32[]{:S(2)}) collective-permute-start(bf16[64,128]{1,0:T(8,128)(2,1)S(1)} %get-tuple-element.109), channel_id=1, source_target_pairs={{0,24},{8,0},{16,8},{24,16},{1,25},{9,1},{17,9},{25,17},{2,26},{10... | collective-permute-start | bytes 49160 | tf_op jit(solution)/shard_map/ppermute | solution.py:404
  156.3 2.7 %collective-permute-start.22 = (bf16[64,128]{1,0:T(8,128)(2,1)S(1)}, bf16[64,128]{1,0:T(8,128)(2,1)S(1)}, u32[]{:S(2)}, u32[]{:S(2)}) collective-permute-start(bf16[64,128]{1,0:T(8,128)(2,1)S(1)} %get-tuple-element.110), channel_id=1, source_target_pairs={{0,16},{8,24},{16,0},{24,8},{1,17},{9,25},{17,1},{25,9},{2,18},{10... | collective-permute-start | bytes 49160 | tf_op jit(solution)/shard_map/ppermute | solution.py:404
  159.1 0.5 slice.3
  159.6 0.7 shard_map.145
  160.3 1.3 collective-permute-done.22.l2
  161.5 2.5 %collective-permute-done.23.l3 = bf16[64,128]{1,0:T(8,128)(2,1)S(1)} collective-permute-done((bf16[64,128]{1,0:T(8,128)(2,1)S(1)}, bf16[64,128]{1,0:T(8,128)(2,1)S(1)}, u32[]{:S(2)}, u32[]{:S(2)}) %collective-permute-start.23) | collective-permute-done | bytes 16416 | tf_op jit(solution)/shard_map/ppermute | solution.py:404
  164.0 2.3 %all-to-all-done.5.top = bf16[8,192,128]{2,1,0:T(8,128)(2,1)S(1)} async-done(((bf16[8,192,128]{2,1,0:T(8,128)(2,1)}), bf16[8,192,128]{2,1,0:T(8,128)(2,1)S(1)}, u32[]{:S(2)}, u32[]{:S(2)}) %all-to-all-start.5) | async-done | bytes 393248 | tf_op jit(solution)/shard_map/all_to_all | solution.py:412
  166.3 1.4 shard_map.147
  (29 shorter events, 0.1 us)
Async XLA Ops:
  0.6 54.4 %copy-start.5 = (bf16[1,512,128]{2,1,0:T(8,128)(2,1)S(1)}, bf16[1,512,128]{2,1,0:T(8,128)(2,1)}, u32[]{:S(2)}) copy-start(bf16[1,512,128]{2,1,0:T(8,128)(2,1)} %param.10) | copy-start | bytes 393220
  0.6 54.3 %copy-start.4 = (bf16[1,512,128]{2,1,0:T(8,128)(2,1)S(1)}, bf16[1,512,128]{2,1,0:T(8,128)(2,1)}, u32[]{:S(2)}) copy-start(bf16[1,512,128]{2,1,0:T(8,128)(2,1)} %param.9) | copy-start | bytes 393220
  0.7 54.3 %copy-start = (bf16[1,512,128]{2,1,0:T(8,128)(2,1)S(1)}, bf16[1,512,128]{2,1,0:T(8,128)(2,1)}, u32[]{:S(2)}) copy-start(bf16[1,512,128]{2,1,0:T(8,128)(2,1)} %param.12) | copy-start | bytes 393220
  0.7 54.3 %copy-start.3 = (bf16[1,512,128]{2,1,0:T(8,128)(2,1)S(1)}, bf16[1,512,128]{2,1,0:T(8,128)(2,1)}, u32[]{:S(2)}) copy-start(bf16[1,512,128]{2,1,0:T(8,128)(2,1)} %param.8) | copy-start | bytes 393220
  3.3 59.6 %copy-start.1 = (bf16[1,512,128]{2,1,0:T(8,128)(2,1)S(1)}, bf16[1,512,128]{2,1,0:T(8,128)(2,1)}, u32[]{:S(2)}) copy-start(bf16[1,512,128]{2,1,0:T(8,128)(2,1)} %param.11) | copy-start | bytes 393220
  3.3 24.0 %all-to-all-start = ((bf16[8,208,128]{2,1,0:T(8,128)(2,1)}), bf16[8,208,128]{2,1,0:T(8,128)(2,1)S(1)}, u32[]{:S(2)}, u32[]{:S(2)}) async-start(bf16[8,208,128]{2,1,0:T(8,128)(2,1)} %get-tuple-element.63), calls=%async_computation | async-start | bytes 851968 | tf_op jit(solution)/shard_map/all_to_all | solution.py:412
  12.0 4.4 %collective-permute-start.2 = (bf16[48,128]{1,0:T(8,128)(2,1)S(1)}, bf16[48,128]{1,0:T(8,128)(2,1)S(1)}, u32[]{:S(2)}, u32[]{:S(2)}) collective-permute-start(bf16[48,128]{1,0:T(8,128)(2,1)S(1)} %get-tuple-element.64.l0), channel_id=1, source_target_pairs={{0,24},{8,0},{16,8},{24,16},{1,25},{9,1},{17,9},{25,17},{2,26},{10... | collective-permute-start | bytes 36872 | tf_op jit(solution)/shard_map/ppermute | solution.py:404
  14.7 5.2 %collective-permute-start.1 = (bf16[48,128]{1,0:T(8,128)(2,1)S(1)}, bf16[48,128]{1,0:T(8,128)(2,1)S(1)}, u32[]{:S(2)}, u32[]{:S(2)}) collective-permute-start(bf16[48,128]{1,0:T(8,128)(2,1)S(1)} %get-tuple-element.64.l0), channel_id=1, source_target_pairs={{0,16},{8,24},{16,0},{24,8},{1,17},{9,25},{17,1},{25,9},{2,18},{10... | collective-permute-start | bytes 36872 | tf_op jit(solution)/shard_map/ppermute | solution.py:404
  15.5 4.9 %collective-permute-start = (bf16[48,128]{1,0:T(8,128)(2,1)S(1)}, bf16[48,128]{1,0:T(8,128)(2,1)S(1)}, u32[]{:S(2)}, u32[]{:S(2)}) collective-permute-start(bf16[48,128]{1,0:T(8,128)(2,1)S(1)} %get-tuple-element.64.l0), channel_id=1, source_target_pairs={{0,8},{8,16},{16,24},{24,0},{1,9},{9,17},{17,25},{25,1},{2,10},{10... | collective-permute-start | bytes 36872 | tf_op jit(solution)/shard_map/ppermute | solution.py:404
  21.3 63.4 %copy-start.2 = (bf16[1,512,128]{2,1,0:T(8,128)(2,1)S(1)}, bf16[1,512,128]{2,1,0:T(8,128)(2,1)}, u32[]{:S(2)}) copy-start(bf16[1,512,128]{2,1,0:T(8,128)(2,1)} %param.14) | copy-start | bytes 393220
  21.3 63.4 %copy-start.7 = (f32[1,128]{1,0:T(1,128)S(1)}, f32[1,128]{1,0:T(1,128)}, u32[]{:S(2)}) copy-start(f32[1,128]{1,0:T(1,128)} %gain.5) | copy-start | bytes 1540
  27.3 27.6 %all-to-all-start.1 = ((bf16[8,4,48,128]{3,2,1,0:T(8,128)(2,1)}), bf16[8,4,48,128]{3,2,1,0:T(8,128)(2,1)S(1)}, u32[]{:S(2)}, u32[]{:S(2)}) async-start(bf16[8,4,48,128]{3,2,1,0:T(8,128)(2,1)} %shard_map.136), calls=%async_computation.1 | async-start | bytes 786432 | tf_op jit(solution)/shard_map/all_to_all | solution.py:412
  30.8 22.4 %collective-permute-start.5 = (bf16[8,208,128]{2,1,0:T(8,128)(2,1)S(1)}, bf16[8,208,128]{2,1,0:T(8,128)(2,1)S(1)}, u32[]{:S(2)}, u32[]{:S(2)}) collective-permute-start(bf16[8,208,128]{2,1,0:T(8,128)(2,1)S(1)} %all-to-all-done.f0), channel_id=1, source_target_pairs={{0,24},{8,0},{16,8},{24,16},{1,25},{9,1},{17,9},{25,17},{2,26},{10... | collective-permute-start | bytes 1277960 | tf_op jit(solution)/shard_map/ppermute | solution.py:404
  33.6 19.6 %collective-permute-start.4 = (bf16[8,208,128]{2,1,0:T(8,128)(2,1)S(1)}, bf16[8,208,128]{2,1,0:T(8,128)(2,1)S(1)}, u32[]{:S(2)}, u32[]{:S(2)}) collective-permute-start(bf16[8,208,128]{2,1,0:T(8,128)(2,1)S(1)} %all-to-all-done.f0), channel_id=1, source_target_pairs={{0,16},{8,24},{16,0},{24,8},{1,17},{9,25},{17,1},{25,9},{2,18},{10... | collective-permute-start | bytes 1277960 | tf_op jit(solution)/shard_map/ppermute | solution.py:404
  34.4 20.5 %collective-permute-start.3 = (bf16[8,208,128]{2,1,0:T(8,128)(2,1)S(1)}, bf16[8,208,128]{2,1,0:T(8,128)(2,1)S(1)}, u32[]{:S(2)}, u32[]{:S(2)}) collective-permute-start(bf16[8,208,128]{2,1,0:T(8,128)(2,1)S(1)} %all-to-all-done.f0), channel_id=1, source_target_pairs={{0,8},{8,16},{16,24},{24,0},{1,9},{9,17},{17,25},{25,1},{2,10},{10... | collective-permute-start | bytes 1277960 | tf_op jit(solution)/shard_map/ppermute | solution.py:404
  35.3 17.9 %collective-permute-start.6 = (bf16[128,256]{1,0:T(8,128)(2,1)S(1)}, bf16[128,256]{1,0:T(8,128)(2,1)S(1)}, u32[]{:S(2)}, u32[]{:S(2)}) collective-permute-start(bf16[128,256]{1,0:T(8,128)(2,1)S(1)} %get-tuple-element.67), channel_id=1, source_target_pairs={{0,8},{8,16},{16,24},{24,32},{32,40},{40,48},{48,56},{56,64},{64,7... | collective-permute-start | bytes 196616 | tf_op jit(solution)/shard_map/ppermute | solution.py:449
  59.2 4.1 %collective-permute-start.9 = (bf16[128,128]{1,0:T(8,128)(2,1)S(1)}, bf16[128,128]{1,0:T(8,128)(2,1)S(1)}, u32[]{:S(2)}, u32[]{:S(2)}) collective-permute-start(bf16[128,128]{1,0:T(8,128)(2,1)S(1)} %get-tuple-element.74.x0), channel_id=1, source_target_pairs={{0,24},{8,0},{16,8},{24,16},{1,25},{9,1},{17,9},{25,17},{2,26},{10... | collective-permute-start | bytes 98312 | tf_op jit(solution)/shard_map/ppermute | solution.py:404
  61.4 5.4 %collective-permute-start.8 = (bf16[128,128]{1,0:T(8,128)(2,1)S(1)}, bf16[128,128]{1,0:T(8,128)(2,1)S(1)}, u32[]{:S(2)}, u32[]{:S(2)}) collective-permute-start(bf16[128,128]{1,0:T(8,128)(2,1)S(1)} %get-tuple-element.74.x0), channel_id=1, source_target_pairs={{0,16},{8,24},{16,0},{24,8},{1,17},{9,25},{17,1},{25,9},{2,18},{10... | collective-permute-start | bytes 98312 | tf_op jit(solution)/shard_map/ppermute | solution.py:404
  62.2 5.1 %collective-permute-start.7 = (bf16[128,128]{1,0:T(8,128)(2,1)S(1)}, bf16[128,128]{1,0:T(8,128)(2,1)S(1)}, u32[]{:S(2)}, u32[]{:S(2)}) collective-permute-start(bf16[128,128]{1,0:T(8,128)(2,1)S(1)} %get-tuple-element.74.x0), channel_id=1, source_target_pairs={{0,8},{8,16},{16,24},{24,0},{1,9},{9,17},{17,25},{25,1},{2,10},{10... | collective-permute-start | bytes 98312 | tf_op jit(solution)/shard_map/ppermute | solution.py:404
  85.8 1.2 collective-permute-start.10
  87.0 4.9 %collective-permute-start.13 = (f32[8,128]{1,0:T(8,128)S(1)}, f32[8,128]{1,0:T(8,128)S(1)}, u32[]{:S(2)}, u32[]{:S(2)}) collective-permute-start(f32[8,128]{1,0:T(8,128)S(1)} %add.11.s0), channel_id=1, source_target_pairs={{0,6},{2,0},{4,2},{6,4},{1,7},{3,1},{5,3},{7,5},{8,14},{10,8},{12,... | collective-permute-start | bytes 12296 | tf_op jit(solution)/shard_map/ppermute | solution.py:404
  87.4 5.1 %collective-permute-start.12 = (f32[8,128]{1,0:T(8,128)S(1)}, f32[8,128]{1,0:T(8,128)S(1)}, u32[]{:S(2)}, u32[]{:S(2)}) collective-permute-start(f32[8,128]{1,0:T(8,128)S(1)} %add.11.s0), channel_id=1, source_target_pairs={{0,4},{2,6},{4,0},{6,2},{1,5},{3,7},{5,1},{7,3},{8,12},{10,14},{12... | collective-permute-start | bytes 12296 | tf_op jit(solution)/shard_map/ppermute | solution.py:404
  90.0 3.6 %collective-permute-start.11 = (f32[8,128]{1,0:T(8,128)S(1)}, f32[8,128]{1,0:T(8,128)S(1)}, u32[]{:S(2)}, u32[]{:S(2)}) collective-permute-start(f32[8,128]{1,0:T(8,128)S(1)} %add.11.s0), channel_id=1, source_target_pairs={{0,2},{2,4},{4,6},{6,0},{1,3},{3,5},{5,7},{7,1},{8,10},{10,12},{12... | collective-permute-start | bytes 12296 | tf_op jit(solution)/shard_map/ppermute | solution.py:404
  94.1 6.0 %collective-permute-start.16 = (bf16[144,128]{1,0:T(8,128)(2,1)S(1)}, bf16[144,128]{1,0:T(8,128)(2,1)S(1)}, u32[]{:S(2)}, u32[]{:S(2)}) collective-permute-start(bf16[144,128]{1,0:T(8,128)(2,1)S(1)} %get-tuple-element.93.x0), channel_id=1, source_target_pairs={{0,8},{8,16},{16,24},{24,0},{1,9},{9,17},{17,25},{25,1},{2,10},{10... | collective-permute-start | bytes 110600 | tf_op jit(solution)/shard_map/ppermute | solution.py:404
  94.8 5.5 %collective-permute-start.15 = (bf16[144,128]{1,0:T(8,128)(2,1)S(1)}, bf16[144,128]{1,0:T(8,128)(2,1)S(1)}, u32[]{:S(2)}, u32[]{:S(2)}) collective-permute-start(bf16[144,128]{1,0:T(8,128)(2,1)S(1)} %get-tuple-element.93.x0), channel_id=1, source_target_pairs={{0,16},{8,24},{16,0},{24,8},{1,17},{9,25},{17,1},{25,9},{2,18},{10... | collective-permute-start | bytes 110600 | tf_op jit(solution)/shard_map/ppermute | solution.py:404
  97.5 4.0 %collective-permute-start.14 = (bf16[144,128]{1,0:T(8,128)(2,1)S(1)}, bf16[144,128]{1,0:T(8,128)(2,1)S(1)}, u32[]{:S(2)}, u32[]{:S(2)}) collective-permute-start(bf16[144,128]{1,0:T(8,128)(2,1)S(1)} %get-tuple-element.93.x0), channel_id=1, source_target_pairs={{0,24},{8,0},{16,8},{24,16},{1,25},{9,1},{17,9},{25,17},{2,26},{10... | collective-permute-start | bytes 110600 | tf_op jit(solution)/shard_map/ppermute | solution.py:404
  122.0 0.7 copy-start.8
  122.8 36.8 %copy-start.6 = (s32[128,20]{0,1:T(8,128)S(1)}, s32[128,20]{0,1:T(8,128)}, u32[]{:S(2)}) copy-start(s32[128,20]{0,1:T(8,128)} %param.15) | copy-start | bytes 30724
  122.8 22.5 %all-to-all-start.4 = ((bf16[8,4,64,128]{3,2,1,0:T(8,128)(2,1)}), bf16[8,4,64,128]{3,2,1,0:T(8,128)(2,1)S(1)}, u32[]{:S(2)}, u32[]{:S(2)}) async-start(bf16[8,4,64,128]{3,2,1,0:T(8,128)(2,1)} %get-tuple-element.106), calls=%async_computation.4 | async-start | bytes 1048576 | tf_op jit(solution)/shard_map/all_to_all | solution.py:412
  126.4 15.4 %collective-permute-start.18 = (bf16[8,192,128]{2,1,0:T(8,128)(2,1)}, bf16[8,192,128]{2,1,0:T(8,128)(2,1)S(1)}, u32[]{:S(2)}, u32[]{:S(2)}) collective-permute-start(bf16[8,192,128]{2,1,0:T(8,128)(2,1)} %get-tuple-element.103), channel_id=1, source_target_pairs={{0,24},{8,0},{16,8},{24,16},{1,25},{9,1},{17,9},{25,17},{2,26},{10... | collective-permute-start | bytes 1179656 | tf_op jit(solution)/shard_map/ppermute | solution.py:404
  128.6 13.2 %collective-permute-start.19 = (bf16[8,192,128]{2,1,0:T(8,128)(2,1)}, bf16[8,192,128]{2,1,0:T(8,128)(2,1)S(1)}, u32[]{:S(2)}, u32[]{:S(2)}) collective-permute-start(bf16[8,192,128]{2,1,0:T(8,128)(2,1)} %copy-done.8), channel_id=1, source_target_pairs={{0,16},{8,24},{16,0},{24,8},{1,17},{9,25},{17,1},{25,9},{2,18},{10... | collective-permute-start | bytes 1179656 | tf_op jit(solution)/shard_map/ppermute | solution.py:404
  129.3 16.0 %collective-permute-start.20 = (bf16[8,192,128]{2,1,0:T(8,128)(2,1)S(1)}, bf16[8,192,128]{2,1,0:T(8,128)(2,1)S(1)}, u32[]{:S(2)}, u32[]{:S(2)}) collective-permute-start(bf16[8,192,128]{2,1,0:T(8,128)(2,1)S(1)} %get-tuple-element.105), channel_id=1, source_target_pairs={{0,8},{8,16},{16,24},{24,0},{1,9},{9,17},{17,25},{25,1},{2,10},{10... | collective-permute-start | bytes 1179656 | tf_op jit(solution)/shard_map/ppermute | solution.py:404
  146.2 20.1 %all-to-all-start.5 = ((bf16[8,192,128]{2,1,0:T(8,128)(2,1)}), bf16[8,192,128]{2,1,0:T(8,128)(2,1)S(1)}, u32[]{:S(2)}, u32[]{:S(2)}) async-start(bf16[8,192,128]{2,1,0:T(8,128)(2,1)} %get-tuple-element.107), calls=%async_computation.5 | async-start | bytes 786432 | tf_op jit(solution)/shard_map/all_to_all | solution.py:412
  153.0 7.3 %collective-permute-start.17 = (bf16[128,256]{1,0:T(8,128)(2,1)S(1)}, bf16[128,256]{1,0:T(8,128)(2,1)S(1)}, u32[]{:S(2)}, u32[]{:S(2)}) collective-permute-start(bf16[128,256]{1,0:T(8,128)(2,1)S(1)} %get-tuple-element.101), channel_id=1, source_target_pairs={{8,0},{16,8},{24,16},{32,24},{40,32},{48,40},{56,48},{64,56},{72,6... | collective-permute-start | bytes 196616 | tf_op jit(solution)/shard_map/ppermute | solution.py:528
  154.3 6.0 %collective-permute-start.21 = (bf16[64,128]{1,0:T(8,128)(2,1)S(1)}, bf16[64,128]{1,0:T(8,128)(2,1)S(1)}, u32[]{:S(2)}, u32[]{:S(2)}) collective-permute-start(bf16[64,128]{1,0:T(8,128)(2,1)S(1)} %get-tuple-element.109), channel_id=1, source_target_pairs={{0,24},{8,0},{16,8},{24,16},{1,25},{9,1},{17,9},{25,17},{2,26},{10... | collective-permute-start | bytes 49160 | tf_op jit(solution)/shard_map/ppermute | solution.py:404
  156.3 5.2 %collective-permute-start.22 = (bf16[64,128]{1,0:T(8,128)(2,1)S(1)}, bf16[64,128]{1,0:T(8,128)(2,1)S(1)}, u32[]{:S(2)}, u32[]{:S(2)}) collective-permute-start(bf16[64,128]{1,0:T(8,128)(2,1)S(1)} %get-tuple-element.110), channel_id=1, source_target_pairs={{0,16},{8,24},{16,0},{24,8},{1,17},{9,25},{17,1},{25,9},{2,18},{10... | collective-permute-start | bytes 49160 | tf_op jit(solution)/shard_map/ppermute | solution.py:404
  159.0 4.9 %collective-permute-start.23 = (bf16[64,128]{1,0:T(8,128)(2,1)S(1)}, bf16[64,128]{1,0:T(8,128)(2,1)S(1)}, u32[]{:S(2)}, u32[]{:S(2)}) collective-permute-start(bf16[64,128]{1,0:T(8,128)(2,1)S(1)} %get-tuple-element.111), channel_id=1, source_target_pairs={{0,8},{8,16},{16,24},{24,0},{1,9},{9,17},{17,25},{25,1},{2,10},{10... | collective-permute-start | bytes 49160 | tf_op jit(solution)/shard_map/ppermute | solution.py:404
